TPU v7x, 32 devices: a whole 2x2x4 slice. The times are simulated.
32 devices in a mesh: blk: 16 (over z, y, x), grp: 2 (over core).
Axes of the slice: x: 2, y: 2, z: 4, core: 2. Of those that a mesh axis runs over, the one named last changes fastest.
Arguments:
- atom_value: float32 [512, 128], P('blk'), may hold values from 0 to 1
- target_value: float32 [512, 128], P('blk'), may hold values from 0 to 1
- observed: int32 [512, 128], P('blk'), may hold values 0 or 1
- block_owner: int32 [1024, 4], replicated, may hold values from 0 to 15, all different within a row; in each aligned block of 64 rows (0 to 63, 64 to 127, ...) at most 32 rows name the same one
- block_local: int32 [1024, 4], replicated, may hold values from 0 to 31
- slot_index: int32 [3, 2, 131072], P(None, 'grp', 'blk'), may hold values from 0 to 512, as said below
- coefficient: float32 [3, 2, 131072], P(None, 'grp', 'blk'), may hold values from -1.5 to 1.5, as said below
- offset: float32 [2, 131072], P('grp', 'blk'), may hold values from -1 to 0.5
- dual_value: float32 [3, 2, 131072], P(None, 'grp', 'blk'), may hold values from -1.5 to 1.5
- template: int32 [2, 1024], P('grp', 'blk'), may hold values from 0 to 19
- weight: float32 [40], replicated, may hold values from 0.5 to 4
Outputs:
- consensus: float32 [512, 128], P('blk')
- dual_next: float32 [3, 2, 131072], P(None, 'grp', 'blk')
- weight_next: float32 [40], replicated
Inputs may be any that keep to these rules, and one draw needn't show every extreme that they name: `block_owner`: each tile lists 4 different owners; in each aligned block of 64 tiles no owner is listed more than 32 times. `slot_index`: the value 4 * 128 marks an unused slot; slots 0 and 1 of every rule are in use. `coefficient`: every magnitude is 0.5 or more.
All inputs are finite; a program needn't handle non-finite values. No bound on the sum of `observed` on one device may be relied on, other than what follows from the above.
Results may differ from a plain program's by a relative error of at most 0.00026.
Values sent between devices are 32-bit elements; how exact they have to be, the bound alone decides.
No kernel may reach another device: no remote copies, remote signals or barrier semaphores. Data moves between devices by JAX's collectives and lax.ppermute only.
A program may use at most 64 MiB of HBM per device.

v0:
```python
import jax
import jax.numpy as jnp
from jax import lax
from jax.sharding import PartitionSpec as P

TEMPL = 40
ITERS = 2


PENALTY = 1.0
LEARN_RATE = 2.0


def local(
    atom_value,
    target_value,
    observed,
    block_owner,
    block_local,
    slot_index,
    coefficient,
    offset,
    dual_value,
    template,
    weight,
):
    device_index = lax.axis_index("blk")
    blk_count = lax.axis_size("blk")
    group_count = lax.axis_size("grp")
    group_index = lax.axis_index("grp")
    atom_blk, width = atom_value.shape
    tile_dev = template.shape[1]
    list_len = block_owner.shape[1]
    spots = max(2, 2 * tile_dev * list_len // blk_count)
    window_len = list_len * width
    tile_step = min(8, tile_dev)
    block_num = tile_dev // tile_step
    own_owner = lax.dynamic_slice_in_dim(block_owner, device_index * tile_dev, tile_dev, 0).reshape(
        -1
    )
    owner_hot = (own_owner[:, None] == jnp.arange(blk_count, dtype=jnp.int32)[None, :]).astype(
        jnp.int32
    )
    slot_rank = jnp.sum(jnp.cumsum(owner_hot, axis=0) * owner_hot, axis=1) - 1
    destination = own_owner * spots + slot_rank
    placement = (
        jnp.arange(blk_count * spots, dtype=jnp.int32)[:, None] == destination[None, :]
    ).astype(jnp.float32)
    all_owner = block_owner.reshape(blk_count, tile_dev * list_len)
    all_local = block_local.reshape(blk_count, tile_dev * list_len)
    mine = (all_owner == device_index).astype(jnp.int32)
    column = jnp.where(mine == 1, jnp.cumsum(mine, axis=1) - 1, spots)
    spot_hit = column[:, :, None] == jnp.arange(spots, dtype=jnp.int32)[None, None, :]
    requested = jnp.sum(jnp.where(spot_hit, all_local[:, :, None], 0), axis=1)
    receive_table = (
        jnp.arange(atom_blk, dtype=jnp.int32)[:, None] == requested.reshape(-1)[None, :]
    ).astype(jnp.float32)
    slots = slot_index[:, 0, :]
    coeffs = coefficient[:, 0, :]
    offsets = offset[0]
    duals = dual_value[:, 0, :]
    arity = slots.shape[0]
    row_count = slots.shape[1]
    in_use = slots < window_len
    slot_blocks = slots.reshape(arity, block_num, tile_step, width).transpose(1, 0, 2, 3)
    lanes = jnp.arange(window_len, dtype=jnp.int32)
    active = jnp.where(in_use, coeffs, 0.0)
    norm_sq = jnp.sum(active * active, axis=0)
    per_group = TEMPL // group_count
    templates = group_index * per_group + template[0]
    table = (templates[:, None] == jnp.arange(TEMPL, dtype=jnp.int32)[None, :]).astype(jnp.float32)
    tile_weight = jnp.dot(table, weight, precision=lax.Precision.HIGHEST)
    row_weight = jnp.repeat(tile_weight, width)
    squared = jnp.repeat(templates % 2 == 1, width)

    def spread_rows(windows):
        fields = windows.shape[0]
        window_blocks = windows.reshape(fields, block_num, tile_step, window_len).transpose(
            1, 0, 2, 3
        )

        def spread_one_block(pair):
            slot_part, window_part = pair
            onehot = (slot_part[..., None] == lanes).astype(jnp.float32)
            return jnp.einsum(
                "strj,ftj->fstr", onehot, window_part, precision=lax.Precision.HIGHEST
            )

        spread = lax.map(spread_one_block, (slot_blocks, window_blocks))
        return spread.transpose(1, 2, 0, 3, 4).reshape(fields, arity, row_count)

    def collect(contrib):
        contrib_blocks = contrib.reshape(arity, block_num, tile_step, width).transpose(1, 0, 2, 3)

        def collect_one_block(pair):
            slot_part, contrib_part = pair
            onehot = (slot_part[..., None] == lanes).astype(jnp.float32)
            return jnp.einsum("strj,str->tj", onehot, contrib_part, precision=lax.Precision.HIGHEST)

        summed = lax.map(collect_one_block, (slot_blocks, contrib_blocks))
        return summed.reshape(tile_dev * list_len, width)

    def to_owners(window):
        placed = jnp.dot(placement, window, precision=lax.Precision.HIGHEST)
        return placed.reshape(blk_count, spots, width)

    def from_sources(arrived):
        return jnp.dot(
            receive_table,
            arrived.reshape(blk_count * spots, width),
            precision=lax.Precision.HIGHEST,
        )

    def energy(copies):
        linear_part = offsets + jnp.sum(active * copies, axis=0)
        positive = jnp.maximum(linear_part, 0.0)
        row_energy = jnp.where(squared, positive * positive, positive)
        tile_energy = jnp.sum(row_energy.reshape(tile_dev, width), axis=1)
        return jnp.dot(tile_energy, table, precision=lax.Precision.HIGHEST)

    count_send = to_owners(collect(in_use.astype(jnp.float32)))
    owner_counts = lax.all_to_all(count_send, "blk", split_axis=0, concat_axis=0, tiled=True)
    part_count = from_sources(owner_counts)
    counted = lax.psum(part_count, "grp")
    values = atom_value
    moved = duals
    for sweep in range(ITERS):
        fetch_arrived = lax.all_to_all(
            values[requested], "blk", split_axis=0, concat_axis=0, tiled=True
        )
        copies = spread_rows(fetch_arrived[own_owner, slot_rank][None])[0]
        if sweep > 0:
            duals = duals + jnp.where(in_use, moved - copies, 0.0)
        shifted = copies - duals
        hinge_linear_part = offsets + jnp.sum(active * shifted, axis=0)
        plain_step = jnp.clip(hinge_linear_part / norm_sq, 0.0, row_weight / PENALTY)
        square_step = (
            2.0
            * row_weight
            * jnp.maximum(hinge_linear_part, 0.0)
            / (PENALTY + 2.0 * row_weight * norm_sq)
        )
        chosen = jnp.where(squared, square_step, plain_step)
        moved = shifted - chosen[None, :] * active
        sum_send = to_owners(collect(jnp.where(in_use, moved + duals, 0.0)))
        owner_sums = lax.all_to_all(sum_send, "blk", split_axis=0, concat_axis=0, tiled=True)
        part_sum = from_sources(owner_sums)
        total = lax.psum(part_sum, "grp")
        values = jnp.where(
            observed == 1, atom_value, jnp.clip((total + values) / (counted + 1.0), 0.0, 1.0)
        )
    arrived_value, arrived_target = (
        lax.all_to_all(values[requested], "blk", split_axis=0, concat_axis=0, tiled=True),
        lax.all_to_all(target_value[requested], "blk", split_axis=0, concat_axis=0, tiled=True),
    )
    final_window = arrived_value[own_owner, slot_rank]
    target_window = arrived_target[own_owner, slot_rank]
    both_rows = spread_rows(jnp.stack([final_window, target_window]))
    copies = both_rows[0]
    target_rows = both_rows[1]
    dual_next = duals + jnp.where(in_use, moved - copies, 0.0)
    e_value, e_target = lax.psum((energy(copies), energy(target_rows)), ("blk", "grp"))
    weight_next = weight * jnp.exp(-LEARN_RATE * (e_value - e_target) / (e_value + e_target + 1.0))
    return (values, dual_next[:, None, :], weight_next)


def solution(mesh):
    in_specs = (
        P("blk", None),
        P("blk", None),
        P("blk", None),
        P(),
        P(),
        P(None, "grp", "blk"),
        P(None, "grp", "blk"),
        P("grp", "blk"),
        P(None, "grp", "blk"),
        P("grp", "blk"),
        P(),
    )
    out_specs = (P("blk", None), P(None, "grp", "blk"), P())
    return jax.shard_map(local, mesh=mesh, in_specs=in_specs, out_specs=out_specs, check_vma=False)
```

profile of v0, /device:TPU:0, one launch (start us, length us, event | category | flops | bytes accessed | tf_op | source)
XLA Modules:
  0.0 280.9 jit_solution(15638405372162156725)
XLA Ops:
  6.1 8.5 %all-to-all-start = ((f32[16,32,128]{2,1,0:T(8,128)}), f32[16,32,128]{2,1,0:T(8,128)S(1)}, u32[]{:S(2)}, u32[]{:S(2)}) async-start(f32[16,32,128]{2,1,0:T(8,128)} %bitcast.5), calls=%async_computation | async-start | bytes 524288 | tf_op jit(solution)/shard_map/all_to_all | solution.py:128
  16.9 18.4 %while.68 = (s32[]{:T(128)}, f32[8,8,512]{2,1,0:T(8,128)S(1)}, s32[8,3,8,128]{3,2,1,0:T(8,128)S(1)}, f32[8,3,8,128]{3,2,0,1:T(8,128)S(1)}, s32[]{:T(128)}) while((s32[]{:T(128)}, f32[8,8,512]{2,1,0:T(8,128)S(1)}, s32[8,3,8,128]{3,2,1,0:T(8,128)S(1)}, f32[8,3,8,128]{3,2,0,1:T(8,128)S(1)}, s32[]{:T(128)}) %tuple.151), condition=%wide.region_14.15_spmd.clone, body=%wide.region_13.14_spmd.clone.sunk | while | flops 20447232 | bytes 122953 | solution.py:100
  36.8 6.9 %all-to-all-start.2 = ((f32[16,32,128]{2,1,0:T(8,128)}), f32[16,32,128]{2,1,0:T(8,128)S(1)}, u32[]{:S(2)}, u32[]{:S(2)}) async-start(f32[16,32,128]{2,1,0:T(8,128)} %fusion.33), calls=%async_computation.2 | async-start | bytes 524288 | tf_op jit(solution)/shard_map/all_to_all | solution.py:122
  45.7 25.0 %while.66 = (s32[]{:T(128)}, f32[8,1,3,8,128]{4,3,0,2,1:T(8,128)S(1)}, f32[8,1,8,512]{3,2,1,0:T(8,128)S(1)}, s32[8,3,8,128]{3,2,1,0:T(8,128)S(1)}, s32[]{:T(128)}) while((s32[]{:T(128)}, f32[8,1,3,8,128]{4,3,0,2,1:T(8,128)S(1)}, f32[8,1,8,512]{3,2,1,0:T(8,128)S(1)}, s32[8,3,8,128]{3,2,1,0:T(8,128)S(1)}, s32[]{:T(128)}) %tuple.168), condition=%wide.region_7.8_spmd.clone, body=%wide.region_6.7_spmd.clone.sunk | while | flops 20447232 | bytes 122953 | solution.py:89
  45.8 3.1 %fusion.104 = f32[8,1,3,128]{3,1,2,0:T(1,128)S(1)} fusion(f32[8,512,1,1]{1,0,2,3:T(8,128)S(1)} %dynamic-slice_bitcast_fusion.14, s32[3,8,128]{2,1,0:T(8,128)S(1)} %dynamic-slice_bitcast_fusion.15), kind=kOutput, calls=%fused_computation.15.clone.1 | convolution fusion | flops 20447232 | bytes 40960 | tf_op jit(solution)/shard_map/while/body/eval_jaxpr/strj,ftj->fstr/dot_general | solution.py:85
  48.9 3.1 %fusion.104 = f32[8,1,3,128]{3,1,2,0:T(1,128)S(1)} fusion(f32[8,512,1,1]{1,0,2,3:T(8,128)S(1)} %dynamic-slice_bitcast_fusion.14, s32[3,8,128]{2,1,0:T(8,128)S(1)} %dynamic-slice_bitcast_fusion.15), kind=kOutput, calls=%fused_computation.15.clone.1 | convolution fusion | flops 20447232 | bytes 40960 | tf_op jit(solution)/shard_map/while/body/eval_jaxpr/strj,ftj->fstr/dot_general | solution.py:85
  52.0 3.1 %fusion.104 = f32[8,1,3,128]{3,1,2,0:T(1,128)S(1)} fusion(f32[8,512,1,1]{1,0,2,3:T(8,128)S(1)} %dynamic-slice_bitcast_fusion.14, s32[3,8,128]{2,1,0:T(8,128)S(1)} %dynamic-slice_bitcast_fusion.15), kind=kOutput, calls=%fused_computation.15.clone.1 | convolution fusion | flops 20447232 | bytes 40960 | tf_op jit(solution)/shard_map/while/body/eval_jaxpr/strj,ftj->fstr/dot_general | solution.py:85
  71.7 18.4 %while.67 = (s32[]{:T(128)}, f32[8,8,512]{2,1,0:T(8,128)S(1)}, s32[8,3,8,128]{3,2,1,0:T(8,128)S(1)}, f32[8,3,8,128]{3,2,0,1:T(8,128)S(1)}, s32[]{:T(128)}) while((s32[]{:T(128)}, f32[8,8,512]{2,1,0:T(8,128)S(1)}, s32[8,3,8,128]{3,2,1,0:T(8,128)S(1)}, f32[8,3,8,128]{3,2,0,1:T(8,128)S(1)}, s32[]{:T(128)}) %tuple.165), condition=%wide.region_11.12_spmd.clone, body=%wide.region_10.11_spmd.clone.sunk | while | flops 20447232 | bytes 122953 | solution.py:100
  91.2 7.0 %all-to-all-start.1 = ((f32[16,32,128]{2,1,0:T(8,128)}), f32[16,32,128]{2,1,0:T(8,128)S(1)}, u32[]{:S(2)}, u32[]{:S(2)}) async-start(f32[16,32,128]{2,1,0:T(8,128)} %fusion.35), calls=%async_computation.1 | async-start | bytes 524288 | tf_op jit(solution)/shard_map/all_to_all | solution.py:146
  98.6 8.2 %all-to-all-done.1 = f32[16,32,128]{2,1,0:T(8,128)S(1)} async-done(((f32[16,32,128]{2,1,0:T(8,128)}), f32[16,32,128]{2,1,0:T(8,128)S(1)}, u32[]{:S(2)}, u32[]{:S(2)}) %all-to-all-start.1) | async-done | bytes 262176 | tf_op jit(solution)/shard_map/all_to_all | solution.py:146
  107.0 3.4 %all-reduce.1 = (f32[32,128]{1,0:T(8,128)S(1)}, f32[32,128]{1,0:T(8,128)S(1)}) all-reduce(f32[32,128]{1,0:T(8,128)S(1)} %fusion.56, f32[32,128]{1,0:T(8,128)S(1)} %fusion.55), channel_id=1, replica_groups=mesh['blk'=16,'grp'=2] {'grp'}, use_global_device_ids=true, to_apply=%region_12.13 | all-reduce | flops 8192 | bytes 65536 | tf_op jit(solution)/shard_map/psum | solution.py:148
  112.1 3.8 %all-to-all-start.3 = ((f32[16,32,128]{2,1,0:T(8,128)}), f32[16,32,128]{2,1,0:T(8,128)S(1)}, u32[]{:S(2)}, u32[]{:S(2)}) async-start(f32[16,32,128]{2,1,0:T(8,128)} %bitcast.25), calls=%async_computation.3 | async-start | bytes 524288 | tf_op jit(solution)/shard_map/all_to_all | solution.py:128
  115.9 10.4 %all-to-all-done.3 = f32[16,32,128]{2,1,0:T(8,128)S(1)} async-done(((f32[16,32,128]{2,1,0:T(8,128)}), f32[16,32,128]{2,1,0:T(8,128)S(1)}, u32[]{:S(2)}, u32[]{:S(2)}) %all-to-all-start.3) | async-done | bytes 262176 | tf_op jit(solution)/shard_map/all_to_all | solution.py:128
  128.2 25.0 %while.69 = (s32[]{:T(128)}, f32[8,1,3,8,128]{4,3,0,2,1:T(8,128)S(1)}, f32[8,1,8,512]{3,2,1,0:T(8,128)S(1)}, s32[8,3,8,128]{3,2,1,0:T(8,128)S(1)}, s32[]{:T(128)}) while((s32[]{:T(128)}, f32[8,1,3,8,128]{4,3,0,2,1:T(8,128)S(1)}, f32[8,1,8,512]{3,2,1,0:T(8,128)S(1)}, s32[8,3,8,128]{3,2,1,0:T(8,128)S(1)}, s32[]{:T(128)}) %tuple.169), condition=%wide.region_17.18_spmd.clone, body=%wide.region_16.17_spmd.clone.sunk | while | flops 20447232 | bytes 122953 | solution.py:89
  153.7 18.4 %while.70 = (s32[]{:T(128)}, f32[8,8,512]{2,1,0:T(8,128)S(1)}, s32[8,3,8,128]{3,2,1,0:T(8,128)S(1)}, f32[8,3,8,128]{3,2,0,1:T(8,128)S(1)}, s32[]{:T(128)}) while((s32[]{:T(128)}, f32[8,8,512]{2,1,0:T(8,128)S(1)}, s32[8,3,8,128]{3,2,1,0:T(8,128)S(1)}, f32[8,3,8,128]{3,2,0,1:T(8,128)S(1)}, s32[]{:T(128)}) %tuple.167), condition=%wide.region_20.21_spmd.clone, body=%wide.region_19.20_spmd.clone.sunk | while | flops 20447232 | bytes 122953 | solution.py:100
  173.3 3.5 %all-to-all-start.4 = ((f32[16,32,128]{2,1,0:T(8,128)}), f32[16,32,128]{2,1,0:T(8,128)S(1)}, u32[]{:S(2)}, u32[]{:S(2)}) async-start(f32[16,32,128]{2,1,0:T(8,128)} %fusion.31), calls=%async_computation.4 | async-start | bytes 524288 | tf_op jit(solution)/shard_map/all_to_all | solution.py:146
  178.5 7.7 %all-to-all-done.4 = f32[16,32,128]{2,1,0:T(8,128)S(1)} async-done(((f32[16,32,128]{2,1,0:T(8,128)}), f32[16,32,128]{2,1,0:T(8,128)S(1)}, u32[]{:S(2)}, u32[]{:S(2)}) %all-to-all-start.4) | async-done | bytes 262176 | tf_op jit(solution)/shard_map/all_to_all | solution.py:146
  186.2 3.5 %all-to-all-start.6 = ((f32[16,32,128]{2,1,0:T(8,128)}), f32[16,32,128]{2,1,0:T(8,128)S(1)}, u32[]{:S(2)}, u32[]{:S(2)}) async-start(f32[16,32,128]{2,1,0:T(8,128)} %bitcast.41), calls=%async_computation.6 | async-start | bytes 524288 | tf_op jit(solution)/shard_map/all_to_all | solution.py:154
  190.0 3.4 %psum.37 = f32[32,128]{1,0:T(8,128)S(1)} all-reduce(f32[32,128]{1,0:T(8,128)S(1)} %fusion.54), channel_id=1, replica_groups=mesh['blk'=16,'grp'=2] {'grp'}, use_global_device_ids=true, to_apply=%region_21.22 | all-reduce | flops 4096 | bytes 32768 | tf_op jit(solution)/shard_map/psum | solution.py:148
  195.0 4.0 %all-to-all-done.6 = f32[16,32,128]{2,1,0:T(8,128)S(1)} async-done(((f32[16,32,128]{2,1,0:T(8,128)}), f32[16,32,128]{2,1,0:T(8,128)S(1)}, u32[]{:S(2)}, u32[]{:S(2)}) %all-to-all-start.6) | async-done | bytes 262176 | tf_op jit(solution)/shard_map/all_to_all | solution.py:154
  199.0 3.5 %all-to-all-start.5 = ((f32[16,32,128]{2,1,0:T(8,128)}), f32[16,32,128]{2,1,0:T(8,128)S(1)}, u32[]{:S(2)}, u32[]{:S(2)}) async-start(f32[16,32,128]{2,1,0:T(8,128)} %bitcast.39), calls=%async_computation.5 | async-start | bytes 524288 | tf_op jit(solution)/shard_map/all_to_all | solution.py:153
  204.7 7.7 %all-to-all-done.5 = f32[16,32,128]{2,1,0:T(8,128)S(1)} async-done(((f32[16,32,128]{2,1,0:T(8,128)}), f32[16,32,128]{2,1,0:T(8,128)S(1)}, u32[]{:S(2)}, u32[]{:S(2)}) %all-to-all-start.5) | async-done | bytes 262176 | tf_op jit(solution)/shard_map/all_to_all | solution.py:153
  214.5 25.1 %while.71 = (s32[]{:T(128)}, f32[8,2,3,8,128]{4,1,2,3,0:T(2,128)S(1)}, f32[8,2,8,512]{3,1,2,0:T(2,128)S(1)}, s32[8,3,8,128]{3,2,0,1:T(8,128)S(1)}, s32[]{:T(128)}) while((s32[]{:T(128)}, f32[8,2,3,8,128]{4,1,2,3,0:T(2,128)S(1)}, f32[8,2,8,512]{3,1,2,0:T(2,128)S(1)}, s32[8,3,8,128]{3,2,0,1:T(8,128)S(1)}, s32[]{:T(128)}) %tuple.163), condition=%wide.region_23.24_spmd.clone, body=%wide.region_22.23_spmd.clone.sunk | while | flops 39321600 | bytes 123969 | solution.py:89
  214.5 3.1 %fusion.115 = f32[8,2,3,8,128]{4,1,2,3,0:T(2,128)S(1)} fusion(f32[8,2,3,8,128]{4,1,2,3,0:T(2,128)S(1)} %get-tuple-element.649, s32[]{:T(128)} %get-tuple-element.648, s32[3,8,128]{2,0,1:T(4,128)S(1)} %bitcast.319, f32[8,2,8,512]{3,1,2,0:T(2,128)S(1)} %get-tuple-element.655), kind=kOutput, calls=%fused_computation.50.clone.1 | convolution fusion | flops 39321600 | bytes 74752 | tf_op jit(solution)/shard_map/while/body/eval_jaxpr/strj,ftj->fstr/dot_general | solution.py:85
  217.7 3.1 %fusion.115 = f32[8,2,3,8,128]{4,1,2,3,0:T(2,128)S(1)} fusion(f32[8,2,3,8,128]{4,1,2,3,0:T(2,128)S(1)} %get-tuple-element.649, s32[]{:T(128)} %get-tuple-element.648, s32[3,8,128]{2,0,1:T(4,128)S(1)} %bitcast.319, f32[8,2,8,512]{3,1,2,0:T(2,128)S(1)} %get-tuple-element.655), kind=kOutput, calls=%fused_computation.50.clone.1 | convolution fusion | flops 39321600 | bytes 74752 | tf_op jit(solution)/shard_map/while/body/eval_jaxpr/strj,ftj->fstr/dot_general | solution.py:85
  220.8 3.1 %fusion.115 = f32[8,2,3,8,128]{4,1,2,3,0:T(2,128)S(1)} fusion(f32[8,2,3,8,128]{4,1,2,3,0:T(2,128)S(1)} %get-tuple-element.649, s32[]{:T(128)} %get-tuple-element.648, s32[3,8,128]{2,0,1:T(4,128)S(1)} %bitcast.319, f32[8,2,8,512]{3,1,2,0:T(2,128)S(1)} %get-tuple-element.655), kind=kOutput, calls=%fused_computation.50.clone.1 | convolution fusion | flops 39321600 | bytes 74752 | tf_op jit(solution)/shard_map/while/body/eval_jaxpr/strj,ftj->fstr/dot_general | solution.py:85
  223.9 3.1 %fusion.115 = f32[8,2,3,8,128]{4,1,2,3,0:T(2,128)S(1)} fusion(f32[8,2,3,8,128]{4,1,2,3,0:T(2,128)S(1)} %get-tuple-element.649, s32[]{:T(128)} %get-tuple-element.648, s32[3,8,128]{2,0,1:T(4,128)S(1)} %bitcast.319, f32[8,2,8,512]{3,1,2,0:T(2,128)S(1)} %get-tuple-element.655), kind=kOutput, calls=%fused_computation.50.clone.1 | convolution fusion | flops 39321600 | bytes 74752 | tf_op jit(solution)/shard_map/while/body/eval_jaxpr/strj,ftj->fstr/dot_general | solution.py:85
  227.1 3.1 %fusion.115 = f32[8,2,3,8,128]{4,1,2,3,0:T(2,128)S(1)} fusion(f32[8,2,3,8,128]{4,1,2,3,0:T(2,128)S(1)} %get-tuple-element.649, s32[]{:T(128)} %get-tuple-element.648, s32[3,8,128]{2,0,1:T(4,128)S(1)} %bitcast.319, f32[8,2,8,512]{3,1,2,0:T(2,128)S(1)} %get-tuple-element.655), kind=kOutput, calls=%fused_computation.50.clone.1 | convolution fusion | flops 39321600 | bytes 74752 | tf_op jit(solution)/shard_map/while/body/eval_jaxpr/strj,ftj->fstr/dot_general | solution.py:85
  230.2 3.1 %fusion.115 = f32[8,2,3,8,128]{4,1,2,3,0:T(2,128)S(1)} fusion(f32[8,2,3,8,128]{4,1,2,3,0:T(2,128)S(1)} %get-tuple-element.649, s32[]{:T(128)} %get-tuple-element.648, s32[3,8,128]{2,0,1:T(4,128)S(1)} %bitcast.319, f32[8,2,8,512]{3,1,2,0:T(2,128)S(1)} %get-tuple-element.655), kind=kOutput, calls=%fused_computation.50.clone.1 | convolution fusion | flops 39321600 | bytes 74752 | tf_op jit(solution)/shard_map/while/body/eval_jaxpr/strj,ftj->fstr/dot_general | solution.py:85
  233.4 3.1 %fusion.115 = f32[8,2,3,8,128]{4,1,2,3,0:T(2,128)S(1)} fusion(f32[8,2,3,8,128]{4,1,2,3,0:T(2,128)S(1)} %get-tuple-element.649, s32[]{:T(128)} %get-tuple-element.648, s32[3,8,128]{2,0,1:T(4,128)S(1)} %bitcast.319, f32[8,2,8,512]{3,1,2,0:T(2,128)S(1)} %get-tuple-element.655), kind=kOutput, calls=%fused_computation.50.clone.1 | convolution fusion | flops 39321600 | bytes 74752 | tf_op jit(solution)/shard_map/while/body/eval_jaxpr/strj,ftj->fstr/dot_general | solution.py:85
  236.5 3.1 %fusion.115 = f32[8,2,3,8,128]{4,1,2,3,0:T(2,128)S(1)} fusion(f32[8,2,3,8,128]{4,1,2,3,0:T(2,128)S(1)} %get-tuple-element.649, s32[]{:T(128)} %get-tuple-element.648, s32[3,8,128]{2,0,1:T(4,128)S(1)} %bitcast.319, f32[8,2,8,512]{3,1,2,0:T(2,128)S(1)} %get-tuple-element.655), kind=kOutput, calls=%fused_computation.50.clone.1 | convolution fusion | flops 39321600 | bytes 74752 | tf_op jit(solution)/shard_map/while/body/eval_jaxpr/strj,ftj->fstr/dot_general | solution.py:85
  240.6 38.8 %all-reduce = (f32[40]{0:T(128)S(1)}, f32[40]{0:T(128)S(1)}) all-reduce(f32[40]{0:T(128)S(1)} %convolution_bitcast_fusion.1, f32[40]{0:T(128)S(1)} %convolution_bitcast_fusion), channel_id=1, replica_groups=mesh['blk'=16,'grp'=2] {'blk','grp'}, use_global_device_ids=true, to_apply=%region_26.27 | all-reduce | flops 80 | bytes 640 | tf_op jit(solution)/shard_map/psum | solution.py:162
  (280 shorter events, 124.6 us)
Async XLA Ops:
  0.6 176.2 %copy-start = (f32[32,128]{1,0:T(8,128)S(1)}, f32[32,128]{1,0:T(8,128)}, u32[]{:S(2)}) copy-start(f32[32,128]{1,0:T(8,128)} %param.24) | copy-start | bytes 49156
  1.6 1.8 copy-start.7
  3.4 1.1 copy-start.1
  6.1 10.6 %copy-start.4 = (s32[3,1,8192]{2,1,0:T(1,128)S(1)}, s32[3,1,8192]{2,1,0:T(1,128)}, u32[]{:S(2)}) copy-start(s32[3,1,8192]{2,1,0:T(1,128)} %param.28) | copy-start | bytes 294916
  6.1 30.7 %all-to-all-start = ((f32[16,32,128]{2,1,0:T(8,128)}), f32[16,32,128]{2,1,0:T(8,128)S(1)}, u32[]{:S(2)}, u32[]{:S(2)}) async-start(f32[16,32,128]{2,1,0:T(8,128)} %bitcast.5), calls=%async_computation | async-start | bytes 524288 | tf_op jit(solution)/shard_map/all_to_all | solution.py:128
  16.9 18.4 %copy-start.9 = (s32[1,64]{1,0:T(1,128)S(1)}, s32[1,64]{1,0:T(1,128)}, u32[]{:S(2)}) copy-start(s32[1,64]{1,0:T(1,128)} %param.32) | copy-start | bytes 772
  16.9 18.5 %copy-start.10 = (f32[40]{0:T(128)S(1)}, f32[40]{0:T(128)}, u32[]{:S(2)}) copy-start(f32[40]{0:T(128)} %param.33) | copy-start | bytes 484
  36.8 54.4 %all-to-all-start.2 = ((f32[16,32,128]{2,1,0:T(8,128)}), f32[16,32,128]{2,1,0:T(8,128)S(1)}, u32[]{:S(2)}, u32[]{:S(2)}) async-start(f32[16,32,128]{2,1,0:T(8,128)} %fusion.33), calls=%async_computation.2 | async-start | bytes 524288 | tf_op jit(solution)/shard_map/all_to_all | solution.py:122
  45.7 25.1 %copy-start.3 = (f32[3,1,8192]{2,1,0:T(1,128)S(1)}, f32[3,1,8192]{2,1,0:T(1,128)}, u32[]{:S(2)}) copy-start(f32[3,1,8192]{2,1,0:T(1,128)} %param.29) | copy-start | bytes 294916
  45.7 25.1 %copy-start.5 = (f32[3,1,8192]{2,1,0:T(1,128)S(1)}, f32[3,1,8192]{2,1,0:T(1,128)}, u32[]{:S(2)}) copy-start(f32[3,1,8192]{2,1,0:T(1,128)} %param.31) | copy-start | bytes 294916
  70.7 0.8 copy-start.6
  91.2 19.2 %copy-start.8 = (s32[32,128]{1,0:T(8,128)S(1)}, s32[32,128]{1,0:T(8,128)}, u32[]{:S(2)}) copy-start(s32[32,128]{1,0:T(8,128)} %param.25) | copy-start | bytes 49156
  91.2 15.6 %all-to-all-start.1 = ((f32[16,32,128]{2,1,0:T(8,128)}), f32[16,32,128]{2,1,0:T(8,128)S(1)}, u32[]{:S(2)}, u32[]{:S(2)}) async-start(f32[16,32,128]{2,1,0:T(8,128)} %fusion.35), calls=%async_computation.1 | async-start | bytes 524288 | tf_op jit(solution)/shard_map/all_to_all | solution.py:146
  112.1 14.2 %all-to-all-start.3 = ((f32[16,32,128]{2,1,0:T(8,128)}), f32[16,32,128]{2,1,0:T(8,128)S(1)}, u32[]{:S(2)}, u32[]{:S(2)}) async-start(f32[16,32,128]{2,1,0:T(8,128)} %bitcast.25), calls=%async_computation.3 | async-start | bytes 524288 | tf_op jit(solution)/shard_map/all_to_all | solution.py:128
  173.3 13.0 %all-to-all-start.4 = ((f32[16,32,128]{2,1,0:T(8,128)}), f32[16,32,128]{2,1,0:T(8,128)S(1)}, u32[]{:S(2)}, u32[]{:S(2)}) async-start(f32[16,32,128]{2,1,0:T(8,128)} %fusion.31), calls=%async_computation.4 | async-start | bytes 524288 | tf_op jit(solution)/shard_map/all_to_all | solution.py:146
  186.2 12.8 %all-to-all-start.6 = ((f32[16,32,128]{2,1,0:T(8,128)}), f32[16,32,128]{2,1,0:T(8,128)S(1)}, u32[]{:S(2)}, u32[]{:S(2)}) async-start(f32[16,32,128]{2,1,0:T(8,128)} %bitcast.41), calls=%async_computation.6 | async-start | bytes 524288 | tf_op jit(solution)/shard_map/all_to_all | solution.py:154
  193.4 1.7 copy-start.2
  199.0 13.3 %all-to-all-start.5 = ((f32[16,32,128]{2,1,0:T(8,128)}), f32[16,32,128]{2,1,0:T(8,128)S(1)}, u32[]{:S(2)}, u32[]{:S(2)}) async-start(f32[16,32,128]{2,1,0:T(8,128)} %bitcast.39), calls=%async_computation.5 | async-start | bytes 524288 | tf_op jit(solution)/shard_map/all_to_all | solution.py:153
where the time goes:
time: 282 us; the launch traced here: 281 us
  matrix products  133 us (47%)
  blocking collectives  45.5 us (16%)
  waiting for transfers between devices  38 us (13%)
  starting transfers between devices  36.8 us (13%)
  local copies, waits for them, and re-layouts  19.2 us (7%)
  other arithmetic  6.26 us (2%)
    dot_general x24, matrix products, spread_one_block(): jnp.einsum('strj,ftj->fstr', onehot, window_part, precision=lax.Precision...  74.3 us
    dot_general x24, matrix products, collect_one_block(): jnp.einsum('strj,str->tj', onehot, contrib_part, precision=lax.Precision....  54.4 us
    psum x1, blocking collectives, local(): lax.psum((energy(copies), energy(target_rows)), ('blk', 'grp'))  38.8 us
    all_to_all x3, waiting for transfers between devices, local(): lax.all_to_all(values[requested], 'blk', split_axis=0, concat_axis=0, til...  18 us
    all_to_all x2, waiting for transfers between devices, local(): lax.all_to_all(sum_send, 'blk', split_axis=0, concat_axis=0, tiled=True)  15.9 us
    all_to_all x3, starting transfers between devices, local(): lax.all_to_all(values[requested], 'blk', split_axis=0, concat_axis=0, til...  15.8 us
    all_to_all x2, starting transfers between devices, local(): lax.all_to_all(sum_send, 'blk', split_axis=0, concat_axis=0, tiled=True)  10.6 us
    all_to_all x1, starting transfers between devices, local(): lax.all_to_all(count_send, 'blk', split_axis=0, concat_axis=0, tiled=True)  6.9 us
  transfers between devices with their start and end apart: 7, of which 5 were waited for; matrix products, arithmetic and copies ran while one was open for 27% of the time, Pallas kernels for 0%

commit v1 on v0

v1 whole, which is shorter than its diff:
```python
import jax
import jax.numpy as jnp
from jax import lax
from jax.experimental import pallas as pl
from jax.experimental.pallas import tpu as pltpu
from jax.sharding import PartitionSpec as P

TEMPL = 40
PENALTY = 1.0
LEARN_RATE = 2.0
GROUP = 8
VMEM = pltpu.VMEM
SMEM = pltpu.SMEM


def bits_of(count):
    bits, bit = [], 1
    while bit < count:
        bits.append(bit)
        bit *= 2
    return bits


def swap_cores(value):
    return lax.ppermute(value, "grp", [(0, 1), (1, 0)])


def exchange(value, steps, count):
    perm = [
        (2 * b + core, 2 * (b ^ steps[core]) + core) for b in range(count) for core in range(2)
    ]
    return lax.ppermute(value, ("blk", "grp"), perm)


def all_sum(value, count):
    bits = bits_of(count)
    half = len(bits) // 2
    turned = bits[half:] + bits[:half]
    for steps in zip(bits, turned):
        value = value + exchange(value, steps, count)
    return value


def row_of(row, height, width):
    return jnp.broadcast_to(row, (height, width))


def refresh(total, before, counted, observed):
    moved = jnp.clip((total + before) / (counted + 1.0), 0.0, 1.0)
    return jnp.where(observed > 0.5, before, moved)


def load_windows(place_ref, field_ref, window_ref, tiles, list_len):
    @pl.loop(0, tiles // GROUP)
    def _(group):
        base = pl.multiple_of(group * GROUP, GROUP)
        for i in range(GROUP):
            for k in range(list_len):
                spot = place_ref[(base + i) * list_len + k]
                window_ref[k, pl.ds(base + i, 1), :] = field_ref[pl.ds(spot, 1), :]


def fetch_rows(window_ref, rows, slot, list_len, width):
    lane = slot & (width - 1)
    which = slot // width
    result = jnp.zeros(slot.shape, jnp.float32)
    for k in range(list_len):
        taken = jnp.take_along_axis(window_ref[k, rows, :], lane, axis=1, mode="promise_in_bounds")
        result = jnp.where(which == k, taken, result)
    return result


def split_three(value):
    first = value.astype(jnp.bfloat16).astype(jnp.float32)
    rest = value - first
    second = rest.astype(jnp.bfloat16).astype(jnp.float32)
    return first, second, rest - second


def scatter_tile(place_ref, sum_ref, tile, lanes, whichs, values, list_len, width):
    hot, left = [], []
    pieces = len(values[0])
    height = 16
    row = lax.broadcasted_iota(jnp.int32, (height, width), 0)
    spot = lax.broadcasted_iota(jnp.int32, (width, width), 0)
    for lane, which, parts in zip(lanes, whichs, values):
        hot.append((row_of(lane, width, width) == spot).astype(jnp.float32).astype(jnp.bfloat16))
        value = row_of(parts[-1], height, width)
        for j in range(pieces - 2, -1, -1):
            value = jnp.where(row // list_len == j, row_of(parts[j], height, width), value)
        keep = row_of(which, height, width) == row % list_len
        keep = keep & (row < pieces * list_len)
        left.append(jnp.where(keep, value, 0.0).astype(jnp.bfloat16))
    summed = lax.dot_general(
        jnp.concatenate(left, axis=1),
        jnp.concatenate(hot, axis=1),
        (((1,), (1,)), ((), ())),
        preferred_element_type=jnp.float32,
    )
    total = summed[0:list_len]
    for j in range(1, pieces):
        total = total + summed[j * list_len : (j + 1) * list_len]
    spots = [place_ref[tile * list_len + k] for k in range(list_len)]
    olds = [sum_ref[pl.ds(at, 1), :] for at in spots]
    for k, at in enumerate(spots):
        sum_ref[pl.ds(at, 1), :] = olds[k] + total[k : k + 1]


def count_kernel(place_ref, slot_ref, keep_ref, send_ref, sum_ref, *, list_len):
    arity, tiles, width = slot_ref.shape
    half = keep_ref.shape[0]
    sum_ref[...] = jnp.zeros_like(sum_ref)

    @pl.loop(0, tiles // GROUP)
    def _(group):
        base = pl.multiple_of(group * GROUP, GROUP)
        rows = pl.ds(base, GROUP)
        slots = [slot_ref[s, rows, :] for s in range(arity)]
        one = jnp.ones((1, width), jnp.float32)
        for i in range(GROUP):
            scatter_tile(
                place_ref,
                sum_ref,
                base + i,
                [q[i : i + 1] & (width - 1) for q in slots],
                [q[i : i + 1] // width for q in slots],
                [(one,)] * arity,
                list_len,
                width,
            )

    keep_ref[...] = sum_ref[:half]
    send_ref[...] = sum_ref[half:]


def sweep_kernel(*refs, list_len, first):
    if first:
        (place_ref, field_ref, slot_ref, coef_ref, off_ref, dual_ref, temp_ref, weight_ref,
         moved_ref, keep_ref, send_ref, window_ref, sum_ref) = refs
    else:
        (place_ref, mine_ref, other_ref, before_ref, counted_ref, observed_ref,
         slot_ref, coef_ref, off_ref, dual_ref, old_ref, temp_ref, weight_ref,
         moved_ref, next_ref, field_ref, keep_ref, send_ref, window_ref, sum_ref) = refs
    arity, tiles, width = slot_ref.shape
    half = keep_ref.shape[0]
    if not first:
        for part, source in ((slice(0, half), mine_ref), (slice(half, None), other_ref)):
            field_ref[part] = refresh(
                source[...], before_ref[part], counted_ref[part], observed_ref[part]
            )
    load_windows(place_ref, field_ref, window_ref, tiles, list_len)
    sum_ref[...] = jnp.zeros_like(sum_ref)

    @pl.loop(0, tiles // GROUP)
    def _(group):
        base = pl.multiple_of(group * GROUP, GROUP)
        rows = pl.ds(base, GROUP)
        templ = temp_ref[rows, :]
        templates = weight_ref.shape[1]
        hot = row_of(templ, GROUP, templates) == lax.broadcasted_iota(
            jnp.int32, (GROUP, templates), 1
        )
        weight = jnp.sum(
            jnp.where(hot, row_of(weight_ref[...], GROUP, templates), 0.0), axis=1, keepdims=True
        )
        weight = jnp.broadcast_to(weight, (GROUP, width))
        squared = jnp.broadcast_to(templ % 2 == 1, (GROUP, width))
        slots = [slot_ref[s, rows, :] for s in range(arity)]
        used = [q < list_len * width for q in slots]
        acts = [jnp.where(used[s], coef_ref[s, rows, :], 0.0) for s in range(arity)]
        copies = [fetch_rows(window_ref, rows, q, list_len, width) for q in slots]
        duals = [dual_ref[s, rows, :] for s in range(arity)]
        if not first:
            duals = [
                d + jnp.where(m, old_ref[s, rows, :] - c, 0.0)
                for s, (d, m, c) in enumerate(zip(duals, used, copies))
            ]
            for s in range(arity):
                next_ref[s, rows, :] = duals[s]
        shifted = [c - d for c, d in zip(copies, duals)]
        linear = sum(a * v for a, v in zip(acts, shifted)) + off_ref[rows, :]
        norm = sum(a * a for a in acts)
        plain = jnp.clip(linear / norm, 0.0, weight / PENALTY)
        square = 2.0 * weight * jnp.maximum(linear, 0.0) / (PENALTY + 2.0 * weight * norm)
        chosen = jnp.where(squared, square, plain)
        parts = []
        for s in range(arity):
            moved = shifted[s] - chosen * acts[s]
            moved_ref[s, rows, :] = moved
            parts.append(split_three(jnp.where(used[s], moved + duals[s], 0.0)))
        for i in range(GROUP):
            scatter_tile(
                place_ref,
                sum_ref,
                base + i,
                [q[i : i + 1] & (width - 1) for q in slots],
                [q[i : i + 1] // width for q in slots],
                [tuple(p[i : i + 1] for p in part) for part in parts],
                list_len,
                width,
            )

    keep_ref[...] = sum_ref[:half]
    send_ref[...] = sum_ref[half:]


def energy_kernel(*refs, list_len, last):
    if last:
        (place_ref, own_ref, mine_ref, other_ref, before_ref, counted_ref, observed_ref,
         slot_ref, coef_ref, off_ref, dual_ref, old_ref, temp_ref, weight_ref,
         energy_ref, next_ref, owned_ref, window_ref, field_ref) = refs
    else:
        (place_ref, field_ref, slot_ref, coef_ref, off_ref, temp_ref, weight_ref,
         energy_ref, window_ref) = refs
    arity, tiles, width = slot_ref.shape
    templates = weight_ref.shape[1]
    if last:
        half = mine_ref.shape[0]
        for part, source in ((slice(0, half), mine_ref), (slice(half, None), other_ref)):
            field_ref[part] = refresh(
                source[...], before_ref[part], counted_ref[part], observed_ref[part]
            )
        piece = owned_ref.shape[0] // 2
        for h in range(2):
            start = pl.multiple_of(own_ref[h], GROUP)
            owned_ref[h * piece : (h + 1) * piece] = field_ref[pl.ds(start, piece), :]
    load_windows(place_ref, field_ref, window_ref, tiles, list_len)

    def step(group, total):
        base = pl.multiple_of(group * GROUP, GROUP)
        rows = pl.ds(base, GROUP)
        templ = temp_ref[rows, :]
        hot = row_of(templ, GROUP, templates) == lax.broadcasted_iota(
            jnp.int32, (GROUP, templates), 1
        )
        squared = jnp.broadcast_to(templ % 2 == 1, (GROUP, width))
        linear = off_ref[rows, :]
        for s in range(arity):
            slot = slot_ref[s, rows, :]
            used = slot < list_len * width
            copy = fetch_rows(window_ref, rows, slot, list_len, width)
            linear = linear + jnp.where(used, coef_ref[s, rows, :], 0.0) * copy
            if last:
                next_ref[s, rows, :] = dual_ref[s, rows, :] + jnp.where(
                    used, old_ref[s, rows, :] - copy, 0.0
                )
        positive = jnp.maximum(linear, 0.0)
        rule = jnp.where(squared, positive * positive, positive)
        tile = jnp.sum(rule, axis=1, keepdims=True)
        return total + jnp.where(hot, jnp.broadcast_to(tile, (GROUP, templates)), 0.0)

    total = lax.fori_loop(
        0, tiles // GROUP, step, jnp.zeros((GROUP, templates), jnp.float32)
    )
    energy_ref[...] = jnp.sum(total, axis=0, keepdims=True)


def specs(count, scalars):
    return [pl.BlockSpec(memory_space=SMEM)] * scalars + [
        pl.BlockSpec(memory_space=VMEM)
    ] * (count - scalars)


def call(body, args, scalars, outs, scratch):
    shapes = tuple(jax.ShapeDtypeStruct(s, jnp.float32) for s in outs)
    return pl.pallas_call(
        body,
        out_shape=shapes,
        in_specs=specs(len(args), scalars),
        out_specs=tuple(specs(len(outs), 0)),
        scratch_shapes=[VMEM(s, jnp.float32) for s in scratch],
    )(*args)


def local(
    atom_value,
    target_value,
    observed,
    block_owner,
    block_local,
    slot_index,
    coefficient,
    offset,
    dual_value,
    template,
    weight,
):
    device = lax.axis_index("blk")
    count = lax.axis_size("blk")
    core = lax.axis_index("grp")
    groups = lax.axis_size("grp")
    atom_blk, width = atom_value.shape
    tiles = template.shape[1]
    list_len = block_owner.shape[1]
    arity = slot_index.shape[0]
    piece = atom_blk // 2
    half = count * piece
    bits = bits_of(count)
    middle = len(bits) // 2
    order = bits[middle:] + bits[:middle]

    def position(owner):
        return sum(((owner // bit) % 2) << j for j, bit in enumerate(order))

    def place_of(owner, spot):
        return ((spot // piece) ^ core) * half + position(owner) * piece + spot % piece

    start = device * tiles
    place = place_of(
        lax.dynamic_slice_in_dim(block_owner, start, tiles, 0),
        lax.dynamic_slice_in_dim(block_local, start, tiles, 0),
    ).reshape(-1)
    own = place_of(device, jnp.arange(2, dtype=jnp.int32) * piece)
    slots = slot_index.reshape(arity, tiles, width)
    coeffs = coefficient.reshape(arity, tiles, width)
    offsets = offset.reshape(tiles, width)
    duals = dual_value.reshape(arity, tiles, width)
    templates = (core * (TEMPL // groups) + template[0])[:, None]
    weights = weight[None, :]
    big = (2 * half, width)
    small = (half, width)
    rule = (arity, tiles, width)
    window = (list_len, tiles, width)

    gathered = jnp.stack(
        [
            lax.dynamic_slice_in_dim(f.astype(jnp.float32), core * piece, piece, 0)
            for f in (atom_value, observed, target_value)
        ]
    )
    for bit in order:
        arrived = exchange(gathered, (bit, bit), count)
        high = (device // bit) % 2 == 1
        gathered = jnp.where(
            high,
            jnp.concatenate([arrived, gathered], axis=1),
            jnp.concatenate([gathered, arrived], axis=1),
        )
    gathered = jnp.concatenate([gathered, swap_cores(gathered)], axis=1)
    values, fixed, targets = gathered[0], gathered[1], gathered[2]

    def reduce_all(keep, send):
        mine = all_sum(keep + swap_cores(send), count)
        return mine, swap_cores(mine)

    count_keep, count_send = call(
        lambda *r: count_kernel(*r, list_len=list_len), (place, slots), 1, (small, small), (big,)
    )
    counted = jnp.concatenate(reduce_all(count_keep, count_send), axis=0)

    moved, keep, send = call(
        lambda *r: sweep_kernel(*r, list_len=list_len, first=True),
        (place, values, slots, coeffs, offsets, duals, templates, weights),
        1,
        (rule, small, small),
        (window, big),
    )
    mine, other = reduce_all(keep, send)
    moved, duals, values, keep, send = call(
        lambda *r: sweep_kernel(*r, list_len=list_len, first=False),
        (place, mine, other, values, counted, fixed,
         slots, coeffs, offsets, duals, moved, templates, weights),
        1,
        (rule, rule, big, small, small),
        (window, big),
    )
    mine, other = reduce_all(keep, send)
    (energy_target,) = call(
        lambda *r: energy_kernel(*r, list_len=list_len, last=False),
        (place, targets, slots, coeffs, offsets, templates, weights),
        1,
        ((1, TEMPL),),
        (window,),
    )
    energy_value, dual_next, consensus = call(
        lambda *r: energy_kernel(*r, list_len=list_len, last=True),
        (place, own, mine, other, values, counted, fixed,
         slots, coeffs, offsets, duals, moved, templates, weights),
        2,
        ((1, TEMPL), rule, (atom_blk, width)),
        (window, big),
    )
    energies = jnp.concatenate([energy_value, energy_target], axis=0)
    energies = all_sum(energies + swap_cores(energies), count)
    e_value, e_target = energies[0], energies[1]
    weight_next = weight * jnp.exp(-LEARN_RATE * (e_value - e_target) / (e_value + e_target + 1.0))
    return consensus, dual_next.reshape(dual_value.shape), weight_next


def solution(mesh):
    in_specs = (
        P("blk", None),
        P("blk", None),
        P("blk", None),
        P(),
        P(),
        P(None, "grp", "blk"),
        P(None, "grp", "blk"),
        P("grp", "blk"),
        P(None, "grp", "blk"),
        P("grp", "blk"),
        P(),
    )
    out_specs = (P("blk", None), P(None, "grp", "blk"), P())
    return jax.shard_map(local, mesh=mesh, in_specs=in_specs, out_specs=out_specs, check_vma=False)
```

time: 282 us -> 124 us (0.44)
  matrix products: 133 us -> 0 us
  blocking collectives: 45.5 us -> 0 us
  Pallas kernels: 0 us -> 24.9 us
  local copies, waits for them, and re-layouts: 19.2 us -> 4.27 us
  waiting for transfers between devices: 38 us -> 45.1 us
  starting transfers between devices: 36.8 us -> 42.6 us
    dot_general x57 -> x0, matrix products: 133 us -> none  [the longest x24 74.3 us: spread_one_block(): jnp.einsum('strj,ftj->fstr', onehot, window_part, precision=lax.Precision...]
    psum x3 -> x0, blocking collectives: 45.5 us -> none  [the longest x1 38.8 us: local(): lax.psum((energy(copies), energy(target_rows)), ('blk', 'grp'))]
    ppermute x0 -> x28, waiting for transfers between devices: none -> 45.1 us  [the longest x20 42.3 us: exchange(): return lax.ppermute(value, ('blk', 'grp'), perm)]
    ppermute x0 -> x28, starting transfers between devices: none -> 42.6 us  [the longest x20 40.7 us: exchange(): return lax.ppermute(value, ('blk', 'grp'), perm)]
    all_to_all x7 -> x0, waiting for transfers between devices: 38 us -> none  [the longest x3 18 us: local(): lax.all_to_all(values[requested], 'blk', split_axis=0, concat_axis=0, til...]
    all_to_all x7 -> x0, starting transfers between devices: 36.8 us -> none  [the longest x3 15.8 us: local(): lax.all_to_all(values[requested], 'blk', split_axis=0, concat_axis=0, til...]
    pallas_call x0 -> x5, Pallas kernels: none -> 24.9 us  [call(): pl.pallas_call(body, out_shape=shapes, in_specs=specs(len(args), scalars)...]
    gather x8 -> x0, local copies, waits for them, and re-layouts: 14.2 us -> none  [the longest x3 4.94 us: local(): values[requested]]
  transfers between devices with their start and end apart: 7 -> 28, of which waited for: 5 -> 20; matrix products, arithmetic and copies ran while one was open for 27% -> 4% of each run, Pallas kernels for 0% -> 12%
where the time goes in v1:
time: 124 us; the launch traced here: 123 us
  waiting for transfers between devices  45.1 us (36%)
  starting transfers between devices  42.6 us (34%)
  Pallas kernels  24.9 us (20%)
  other arithmetic  5.44 us (4%)
  local copies, waits for them, and re-layouts  4.27 us (3%)
    ppermute x20, waiting for transfers between devices, exchange(): return lax.ppermute(value, ('blk', 'grp'), perm)  42.3 us
    ppermute x20, starting transfers between devices, exchange(): return lax.ppermute(value, ('blk', 'grp'), perm)  40.7 us
    pallas_call x5, Pallas kernels, call(): pl.pallas_call(body, out_shape=shapes, in_specs=specs(len(args), scalars)...  24.9 us
    ppermute x8, waiting for transfers between devices, swap_cores(): return lax.ppermute(value, 'grp', [(0, 1), (1, 0)])  2.83 us
  transfers between devices with their start and end apart: 28, of which 20 were waited for; matrix products, arithmetic and copies ran while one was open for 4% of the time, Pallas kernels for 12%

profile of v1, /device:TPU:0, one launch (start us, length us, event | category | flops | bytes accessed | tf_op | source)
XLA Modules:
  0.0 123.2 jit_solution(3513453287241576602)
XLA Ops:
  2.1 3.1 %collective-permute-start = (f32[3,16,128]{2,1,0:T(8,128)S(1)}, f32[3,16,128]{2,1,0:T(8,128)S(1)}, u32[]{:S(2)}, u32[]{:S(2)}) collective-permute-start(f32[3,16,128]{2,1,0:T(8,128)S(1)} %pad_maximum_fusion.2), channel_id=1, source_target_pairs={{0,8},{1,9},{2,10},{3,11},{4,12},{5,13},{6,14},{7,15},{8,0},{9,1},... | collective-permute-start | bytes 73736 | tf_op jit(solution)/shard_map/ppermute | solution.py:32
  5.1 1.8 %collective-permute-done = f32[3,16,128]{2,1,0:T(8,128)S(1)} collective-permute-done((f32[3,16,128]{2,1,0:T(8,128)S(1)}, f32[3,16,128]{2,1,0:T(8,128)S(1)}, u32[]{:S(2)}, u32[]{:S(2)}) %collective-permute-start) | collective-permute-done | bytes 24608 | tf_op jit(solution)/shard_map/ppermute | solution.py:32
  6.9 3.0 %collective-permute-start.1 = (f32[3,32,128]{2,1,0:T(8,128)S(1)}, f32[3,32,128]{2,1,0:T(8,128)S(1)}, u32[]{:S(2)}, u32[]{:S(2)}) collective-permute-start(f32[3,32,128]{2,1,0:T(8,128)S(1)} %maximum_select_fusion.3), channel_id=1, source_target_pairs={{0,16},{1,17},{2,18},{3,19},{4,20},{5,21},{6,22},{7,23},{8,24},{9,... | collective-permute-start | bytes 147464 | tf_op jit(solution)/shard_map/ppermute | solution.py:32
  10.0 2.1 %collective-permute-done.1 = f32[3,32,128]{2,1,0:T(8,128)S(1)} collective-permute-done((f32[3,32,128]{2,1,0:T(8,128)S(1)}, f32[3,32,128]{2,1,0:T(8,128)S(1)}, u32[]{:S(2)}, u32[]{:S(2)}) %collective-permute-start.1) | collective-permute-done | bytes 49184 | tf_op jit(solution)/shard_map/ppermute | solution.py:32
  12.0 1.9 %collective-permute-start.2 = (f32[3,64,128]{2,1,0:T(8,128)S(1)}, f32[3,64,128]{2,1,0:T(8,128)S(1)}, u32[]{:S(2)}, u32[]{:S(2)}) collective-permute-start(f32[3,64,128]{2,1,0:T(8,128)S(1)} %maximum_select_fusion.2), channel_id=1, source_target_pairs={{0,2},{1,3},{2,0},{3,1},{4,6},{5,7},{6,4},{7,5},{8,10},{9,11},{10,... | collective-permute-start | bytes 294920 | tf_op jit(solution)/shard_map/ppermute | solution.py:32
  13.9 2.8 %collective-permute-done.2 = f32[3,64,128]{2,1,0:T(8,128)S(1)} collective-permute-done((f32[3,64,128]{2,1,0:T(8,128)S(1)}, f32[3,64,128]{2,1,0:T(8,128)S(1)}, u32[]{:S(2)}, u32[]{:S(2)}) %collective-permute-start.2) | collective-permute-done | bytes 98336 | tf_op jit(solution)/shard_map/ppermute | solution.py:32
  16.7 1.9 %collective-permute-start.3 = (f32[3,128,128]{2,1,0:T(8,128)S(1)}, f32[3,128,128]{2,1,0:T(8,128)S(1)}, u32[]{:S(2)}, u32[]{:S(2)}) collective-permute-start(f32[3,128,128]{2,1,0:T(8,128)S(1)} %maximum_select_fusion.1), channel_id=1, source_target_pairs={{0,4},{1,5},{2,6},{3,7},{4,0},{5,1},{6,2},{7,3},{8,12},{9,13},{10,... | collective-permute-start | bytes 589832 | tf_op jit(solution)/shard_map/ppermute | solution.py:32
  18.7 3.8 %collective-permute-done.3 = f32[3,128,128]{2,1,0:T(8,128)S(1)} collective-permute-done((f32[3,128,128]{2,1,0:T(8,128)S(1)}, f32[3,128,128]{2,1,0:T(8,128)S(1)}, u32[]{:S(2)}, u32[]{:S(2)}) %collective-permute-start.3) | collective-permute-done | bytes 196640 | tf_op jit(solution)/shard_map/ppermute | solution.py:32
  24.2 4.8 %shard_map.131 = (f32[256,128]{1,0:T(8,128)}, f32[256,128]{1,0:T(8,128)}) custom-call(s32[256]{0:T(256)} %reshape.44.r_0_, s32[3,64,128]{2,1,0:T(8,128)} %bitcast.22), custom_call_target="tpu_custom_call" | custom-call | tf_op jit(solution)/shard_map/pallas_call | solution.py:266
  31.3 6.4 %shard_map.130 = (f32[3,64,128]{2,1,0:T(8,128)}, f32[256,128]{1,0:T(8,128)}, f32[256,128]{1,0:T(8,128)}) custom-call(s32[256]{0:T(256)} %reshape.44.r_0_, f32[512,128]{1,0:T(8,128)} %get-tuple-element.36.r_1_.r_3_, s32[3,64,128]{2,1,0:T(8,128)} %bitcast.23, f32[3,64,128]{2,1,0:T(8,128)} %bitcast.27, f32[64,128]{1,0:T(8,128)} %bitcast.31, ...), custom_call_target="tpu_custom_call" | custom-call | tf_op jit(solution)/shard_map/pallas_call | solution.py:266
  38.2 1.9 %collective-permute-start.12 = (f32[256,128]{1,0:T(8,128)S(1)}, f32[256,128]{1,0:T(8,128)S(1)}, u32[]{:S(2)}, u32[]{:S(2)}) collective-permute-start(f32[256,128]{1,0:T(8,128)S(1)} %add.215), channel_id=1, source_target_pairs={{0,2},{1,9},{2,0},{3,11},{4,6},{5,13},{6,4},{7,15},{8,10},{9,1},{1... | collective-permute-start | bytes 393224 | tf_op jit(solution)/shard_map/ppermute | solution.py:32
  41.3 2.0 %collective-permute-done.12 = f32[256,128]{1,0:T(8,128)S(1)} collective-permute-done((f32[256,128]{1,0:T(8,128)S(1)}, f32[256,128]{1,0:T(8,128)S(1)}, u32[]{:S(2)}, u32[]{:S(2)}) %collective-permute-start.12) | collective-permute-done | bytes 131104 | tf_op jit(solution)/shard_map/ppermute | solution.py:32
  43.3 1.9 %collective-permute-start.13 = (f32[256,128]{1,0:T(8,128)S(1)}, f32[256,128]{1,0:T(8,128)S(1)}, u32[]{:S(2)}, u32[]{:S(2)}) collective-permute-start(f32[256,128]{1,0:T(8,128)S(1)} %add.216), channel_id=1, source_target_pairs={{0,4},{1,17},{2,6},{3,19},{4,0},{5,21},{6,2},{7,23},{8,12},{9,25},... | collective-permute-start | bytes 393224 | tf_op jit(solution)/shard_map/ppermute | solution.py:32
  48.3 2.0 %collective-permute-start.14 = (f32[256,128]{1,0:T(8,128)S(1)}, f32[256,128]{1,0:T(8,128)S(1)}, u32[]{:S(2)}, u32[]{:S(2)}) collective-permute-start(f32[256,128]{1,0:T(8,128)S(1)} %add.217), channel_id=1, source_target_pairs={{0,8},{1,3},{2,10},{3,1},{4,12},{5,7},{6,14},{7,5},{8,0},{9,11},{1... | collective-permute-start | bytes 393224 | tf_op jit(solution)/shard_map/ppermute | solution.py:32
  53.6 2.8 %collective-permute-start.15 = (f32[256,128]{1,0:T(8,128)S(1)}, f32[256,128]{1,0:T(8,128)S(1)}, u32[]{:S(2)}, u32[]{:S(2)}) collective-permute-start(f32[256,128]{1,0:T(8,128)S(1)} %add.218), channel_id=1, source_target_pairs={{0,16},{1,5},{2,18},{3,7},{4,20},{5,1},{6,22},{7,3},{8,24},{9,13},... | collective-permute-start | bytes 393224 | tf_op jit(solution)/shard_map/ppermute | solution.py:32
  56.4 2.0 %collective-permute-start.9 = (f32[256,128]{1,0:T(8,128)S(1)}, f32[256,128]{1,0:T(8,128)S(1)}, u32[]{:S(2)}, u32[]{:S(2)}) collective-permute-start(f32[256,128]{1,0:T(8,128)S(1)} %add.213), channel_id=1, source_target_pairs={{0,16},{1,5},{2,18},{3,7},{4,20},{5,1},{6,22},{7,3},{8,24},{9,13},... | collective-permute-start | bytes 393224 | tf_op jit(solution)/shard_map/ppermute | solution.py:32
  58.4 2.5 %collective-permute-done.15 = f32[256,128]{1,0:T(8,128)S(1)} collective-permute-done((f32[256,128]{1,0:T(8,128)S(1)}, f32[256,128]{1,0:T(8,128)S(1)}, u32[]{:S(2)}, u32[]{:S(2)}) %collective-permute-start.15) | collective-permute-done | bytes 131104 | tf_op jit(solution)/shard_map/ppermute | solution.py:32
  64.5 6.8 %shard_map.132 = (f32[3,64,128]{2,1,0:T(8,128)}, f32[3,64,128]{2,1,0:T(8,128)}, f32[512,128]{1,0:T(8,128)}, f32[256,128]{1,0:T(8,128)}, f32[256,128]{1,0:T(8,128)}) custom-call(s32[256]{0:T(256)} %reshape.44.r_0_, f32[256,128]{1,0:T(8,128)} %copy-done.1, f32[256,128]{1,0:T(8,128)} %copy-done.5, f32[512,128]{1,0:T(8,128)} %get-tuple-element.36.r_1_.r_3_, ...), custom_call_target="tpu_custom_call" | custom-call | tf_op jit(solution)/shard_map/pallas_call | solution.py:266
  73.7 3.0 %collective-permute-start.18 = (f32[256,128]{1,0:T(8,128)S(1)}, f32[256,128]{1,0:T(8,128)S(1)}, u32[]{:S(2)}, u32[]{:S(2)}) collective-permute-start(f32[256,128]{1,0:T(8,128)S(1)} %add.220), channel_id=1, source_target_pairs={{0,2},{1,9},{2,0},{3,11},{4,6},{5,13},{6,4},{7,15},{8,10},{9,1},{1... | collective-permute-start | bytes 393224 | tf_op jit(solution)/shard_map/ppermute | solution.py:32
  76.8 2.9 %collective-permute-done.18 = f32[256,128]{1,0:T(8,128)S(1)} collective-permute-done((f32[256,128]{1,0:T(8,128)S(1)}, f32[256,128]{1,0:T(8,128)S(1)}, u32[]{:S(2)}, u32[]{:S(2)}) %collective-permute-start.18) | collective-permute-done | bytes 131104 | tf_op jit(solution)/shard_map/ppermute | solution.py:32
  79.7 2.1 %collective-permute-start.19 = (f32[256,128]{1,0:T(8,128)S(1)}, f32[256,128]{1,0:T(8,128)S(1)}, u32[]{:S(2)}, u32[]{:S(2)}) collective-permute-start(f32[256,128]{1,0:T(8,128)S(1)} %add.221), channel_id=1, source_target_pairs={{0,4},{1,17},{2,6},{3,19},{4,0},{5,21},{6,2},{7,23},{8,12},{9,25},... | collective-permute-start | bytes 393224 | tf_op jit(solution)/shard_map/ppermute | solution.py:32
  81.9 2.9 %collective-permute-done.19 = f32[256,128]{1,0:T(8,128)S(1)} collective-permute-done((f32[256,128]{1,0:T(8,128)S(1)}, f32[256,128]{1,0:T(8,128)S(1)}, u32[]{:S(2)}, u32[]{:S(2)}) %collective-permute-start.19) | collective-permute-done | bytes 131104 | tf_op jit(solution)/shard_map/ppermute | solution.py:32
  86.1 3.7 %collective-permute-done.20 = f32[256,128]{1,0:T(8,128)S(1)} collective-permute-done((f32[256,128]{1,0:T(8,128)S(1)}, f32[256,128]{1,0:T(8,128)S(1)}, u32[]{:S(2)}, u32[]{:S(2)}) %collective-permute-start.20) | collective-permute-done | bytes 131104 | tf_op jit(solution)/shard_map/ppermute | solution.py:32
  89.9 2.6 %collective-permute-start.21 = (f32[256,128]{1,0:T(8,128)S(1)}, f32[256,128]{1,0:T(8,128)S(1)}, u32[]{:S(2)}, u32[]{:S(2)}) collective-permute-start(f32[256,128]{1,0:T(8,128)S(1)} %add.223), channel_id=1, source_target_pairs={{0,16},{1,5},{2,18},{3,7},{4,20},{5,1},{6,22},{7,3},{8,24},{9,13},... | collective-permute-start | bytes 393224 | tf_op jit(solution)/shard_map/ppermute | solution.py:32
  92.5 4.7 %collective-permute-done.21 = f32[256,128]{1,0:T(8,128)S(1)} collective-permute-done((f32[256,128]{1,0:T(8,128)S(1)}, f32[256,128]{1,0:T(8,128)S(1)}, u32[]{:S(2)}, u32[]{:S(2)}) %collective-permute-start.21) | collective-permute-done | bytes 131104 | tf_op jit(solution)/shard_map/ppermute | solution.py:32
  97.9 3.2 %shard_map.134 = f32[1,40]{1,0:T(1,128)} custom-call(s32[256]{0:T(256)} %reshape.44.r_0_, f32[512,128]{1,0:T(8,128)} %get-tuple-element.35.r_1_, s32[3,64,128]{2,1,0:T(8,128)} %bitcast.25, f32[3,64,128]{2,1,0:T(8,128)} %bitcast.29, f32[64,128]{1,0:T(8,128)} %bitcast.33, s32[64,1]{1,0:T(8,128)} %copy.20.r_6_.r_11_.r_12_.r_5_, f32[1,40]{1,0:T(1,128)} %bitcast.39), custom_call_target="tpu_custom_call" | custom-call | tf_op jit(solution)/shard_map/pallas_call | solution.py:266
  101.7 3.7 %shard_map.133 = (f32[1,40]{1,0:T(1,128)}, f32[3,64,128]{2,1,0:T(8,128)}, f32[32,128]{1,0:T(8,128)}) custom-call(s32[256]{0:T(256)} %reshape.44.r_0_, s32[2]{0:T(128)} %fusion.26.r_1_, f32[256,128]{1,0:T(8,128)} %copy-done, f32[256,128]{1,0:T(8,128)} %copy-done.2, f32[512,128]{1,0:T(8,128)} %get-tuple-element.23.r_4_, ...), custom_call_target="tpu_custom_call" | custom-call | tf_op jit(solution)/shard_map/pallas_call | solution.py:266
  107.3 2.0 %collective-permute-start.24 = (f32[2,40]{1,0:T(2,128)S(1)}, f32[2,40]{1,0:T(2,128)S(1)}, u32[]{:S(2)}, u32[]{:S(2)}) collective-permute-start(f32[2,40]{1,0:T(2,128)S(1)} %fusion.27), channel_id=1, source_target_pairs={{0,2},{1,9},{2,0},{3,11},{4,6},{5,13},{6,4},{7,15},{8,10},{9,1},{1... | collective-permute-start | bytes 968 | tf_op jit(solution)/shard_map/ppermute | solution.py:32
  111.0 2.1 %collective-permute-start.25 = (f32[2,40]{1,0:T(2,128)S(1)}, f32[2,40]{1,0:T(2,128)S(1)}, u32[]{:S(2)}, u32[]{:S(2)}) collective-permute-start(f32[2,40]{1,0:T(2,128)S(1)} %fusion.28), channel_id=1, source_target_pairs={{0,4},{1,17},{2,6},{3,19},{4,0},{5,21},{6,2},{7,23},{8,12},{9,25},... | collective-permute-start | bytes 968 | tf_op jit(solution)/shard_map/ppermute | solution.py:32
  115.3 2.9 %collective-permute-done.26 = f32[2,40]{1,0:T(2,128)S(1)} collective-permute-done((f32[2,40]{1,0:T(2,128)S(1)}, f32[2,40]{1,0:T(2,128)S(1)}, u32[]{:S(2)}, u32[]{:S(2)}) %collective-permute-start.26) | collective-permute-done | bytes 352 | tf_op jit(solution)/shard_map/ppermute | solution.py:32
  118.2 2.0 %collective-permute-start.27 = (f32[2,40]{1,0:T(2,128)S(1)}, f32[2,40]{1,0:T(2,128)S(1)}, u32[]{:S(2)}, u32[]{:S(2)}) collective-permute-start(f32[2,40]{1,0:T(2,128)S(1)} %add.228), channel_id=1, source_target_pairs={{0,16},{1,5},{2,18},{3,7},{4,20},{5,1},{6,22},{7,3},{8,24},{9,13},... | collective-permute-start | bytes 968 | tf_op jit(solution)/shard_map/ppermute | solution.py:32
  120.2 2.5 %collective-permute-done.27 = f32[2,40]{1,0:T(2,128)S(1)} collective-permute-done((f32[2,40]{1,0:T(2,128)S(1)}, f32[2,40]{1,0:T(2,128)S(1)}, u32[]{:S(2)}, u32[]{:S(2)}) %collective-permute-start.27) | collective-permute-done | bytes 352 | tf_op jit(solution)/shard_map/ppermute | solution.py:32
  (88 shorter events, 28.4 us)
Async XLA Ops:
  2.1 4.9 %collective-permute-start = (f32[3,16,128]{2,1,0:T(8,128)S(1)}, f32[3,16,128]{2,1,0:T(8,128)S(1)}, u32[]{:S(2)}, u32[]{:S(2)}) collective-permute-start(f32[3,16,128]{2,1,0:T(8,128)S(1)} %pad_maximum_fusion.2), channel_id=1, source_target_pairs={{0,8},{1,9},{2,10},{3,11},{4,12},{5,13},{6,14},{7,15},{8,0},{9,1},... | collective-permute-start | bytes 73736 | tf_op jit(solution)/shard_map/ppermute | solution.py:32
  6.9 5.1 %collective-permute-start.1 = (f32[3,32,128]{2,1,0:T(8,128)S(1)}, f32[3,32,128]{2,1,0:T(8,128)S(1)}, u32[]{:S(2)}, u32[]{:S(2)}) collective-permute-start(f32[3,32,128]{2,1,0:T(8,128)S(1)} %maximum_select_fusion.3), channel_id=1, source_target_pairs={{0,16},{1,17},{2,18},{3,19},{4,20},{5,21},{6,22},{7,23},{8,24},{9,... | collective-permute-start | bytes 147464 | tf_op jit(solution)/shard_map/ppermute | solution.py:32
  12.0 4.7 %collective-permute-start.2 = (f32[3,64,128]{2,1,0:T(8,128)S(1)}, f32[3,64,128]{2,1,0:T(8,128)S(1)}, u32[]{:S(2)}, u32[]{:S(2)}) collective-permute-start(f32[3,64,128]{2,1,0:T(8,128)S(1)} %maximum_select_fusion.2), channel_id=1, source_target_pairs={{0,2},{1,3},{2,0},{3,1},{4,6},{5,7},{6,4},{7,5},{8,10},{9,11},{10,... | collective-permute-start | bytes 294920 | tf_op jit(solution)/shard_map/ppermute | solution.py:32
  16.7 5.7 %collective-permute-start.3 = (f32[3,128,128]{2,1,0:T(8,128)S(1)}, f32[3,128,128]{2,1,0:T(8,128)S(1)}, u32[]{:S(2)}, u32[]{:S(2)}) collective-permute-start(f32[3,128,128]{2,1,0:T(8,128)S(1)} %maximum_select_fusion.1), channel_id=1, source_target_pairs={{0,4},{1,5},{2,6},{3,7},{4,0},{5,1},{6,2},{7,3},{8,12},{9,13},{10,... | collective-permute-start | bytes 589832 | tf_op jit(solution)/shard_map/ppermute | solution.py:32
  22.5 7.9 %collective-permute-start.4 = (f32[3,256,128]{2,1,0:T(8,128)S(1)}, f32[3,256,128]{2,1,0:T(8,128)S(1)}, u32[]{:S(2)}, u32[]{:S(2)}) collective-permute-start(f32[3,256,128]{2,1,0:T(8,128)S(1)} %maximum_select_fusion), channel_id=1, source_target_pairs={{0,1},{1,0},{2,3},{3,2},{4,5},{5,4},{6,7},{7,6},{8,9},{9,8},{10,11... | collective-permute-start | bytes 1179656 | tf_op jit(solution)/shard_map/ppermute | solution.py:25
  29.0 9.2 %collective-permute-start.11 = (f32[256,128]{1,0:T(8,128)}, f32[256,128]{1,0:T(8,128)S(1)}, u32[]{:S(2)}, u32[]{:S(2)}) collective-permute-start(f32[256,128]{1,0:T(8,128)} %get-tuple-element.19), channel_id=1, source_target_pairs={{0,1},{1,0},{2,3},{3,2},{4,5},{5,4},{6,7},{7,6},{8,9},{9,8},{10,11... | collective-permute-start | bytes 393224 | tf_op jit(solution)/shard_map/ppermute | solution.py:25
  31.3 6.9 %copy-start.3 = (f32[256,128]{1,0:T(8,128)S(1)}, f32[256,128]{1,0:T(8,128)}, u32[]{:S(2)}) copy-start(f32[256,128]{1,0:T(8,128)} %get-tuple-element.18) | copy-start | bytes 393220
  37.7 2.4 %collective-permute-start.5 = (f32[256,128]{1,0:T(8,128)}, f32[256,128]{1,0:T(8,128)S(1)}, u32[]{:S(2)}, u32[]{:S(2)}) collective-permute-start(f32[256,128]{1,0:T(8,128)} %get-tuple-element.17), channel_id=1, source_target_pairs={{0,1},{1,0},{2,3},{3,2},{4,5},{5,4},{6,7},{7,6},{8,9},{9,8},{10,11... | collective-permute-start | bytes 393224 | tf_op jit(solution)/shard_map/ppermute | solution.py:25
  38.2 1.9 %copy-start.4 = (f32[256,128]{1,0:T(8,128)S(1)}, f32[256,128]{1,0:T(8,128)}, u32[]{:S(2)}) copy-start(f32[256,128]{1,0:T(8,128)} %get-tuple-element.16) | copy-start | bytes 393220
  38.2 5.0 %collective-permute-start.12 = (f32[256,128]{1,0:T(8,128)S(1)}, f32[256,128]{1,0:T(8,128)S(1)}, u32[]{:S(2)}, u32[]{:S(2)}) collective-permute-start(f32[256,128]{1,0:T(8,128)S(1)} %add.215), channel_id=1, source_target_pairs={{0,2},{1,9},{2,0},{3,11},{4,6},{5,13},{6,4},{7,15},{8,10},{9,1},{1... | collective-permute-start | bytes 393224 | tf_op jit(solution)/shard_map/ppermute | solution.py:32
  40.1 5.1 %collective-permute-start.6 = (f32[256,128]{1,0:T(8,128)S(1)}, f32[256,128]{1,0:T(8,128)S(1)}, u32[]{:S(2)}, u32[]{:S(2)}) collective-permute-start(f32[256,128]{1,0:T(8,128)S(1)} %add.210), channel_id=1, source_target_pairs={{0,2},{1,9},{2,0},{3,11},{4,6},{5,13},{6,4},{7,15},{8,10},{9,1},{1... | collective-permute-start | bytes 393224 | tf_op jit(solution)/shard_map/ppermute | solution.py:32
  43.3 5.0 %collective-permute-start.13 = (f32[256,128]{1,0:T(8,128)S(1)}, f32[256,128]{1,0:T(8,128)S(1)}, u32[]{:S(2)}, u32[]{:S(2)}) collective-permute-start(f32[256,128]{1,0:T(8,128)S(1)} %add.216), channel_id=1, source_target_pairs={{0,4},{1,17},{2,6},{3,19},{4,0},{5,21},{6,2},{7,23},{8,12},{9,25},... | collective-permute-start | bytes 393224 | tf_op jit(solution)/shard_map/ppermute | solution.py:32
  45.2 5.1 %collective-permute-start.7 = (f32[256,128]{1,0:T(8,128)S(1)}, f32[256,128]{1,0:T(8,128)S(1)}, u32[]{:S(2)}, u32[]{:S(2)}) collective-permute-start(f32[256,128]{1,0:T(8,128)S(1)} %add.211), channel_id=1, source_target_pairs={{0,4},{1,17},{2,6},{3,19},{4,0},{5,21},{6,2},{7,23},{8,12},{9,25},... | collective-permute-start | bytes 393224 | tf_op jit(solution)/shard_map/ppermute | solution.py:32
  48.3 5.2 %collective-permute-start.14 = (f32[256,128]{1,0:T(8,128)S(1)}, f32[256,128]{1,0:T(8,128)S(1)}, u32[]{:S(2)}, u32[]{:S(2)}) collective-permute-start(f32[256,128]{1,0:T(8,128)S(1)} %add.217), channel_id=1, source_target_pairs={{0,8},{1,3},{2,10},{3,1},{4,12},{5,7},{6,14},{7,5},{8,0},{9,11},{1... | collective-permute-start | bytes 393224 | tf_op jit(solution)/shard_map/ppermute | solution.py:32
  50.3 6.1 %collective-permute-start.8 = (f32[256,128]{1,0:T(8,128)S(1)}, f32[256,128]{1,0:T(8,128)S(1)}, u32[]{:S(2)}, u32[]{:S(2)}) collective-permute-start(f32[256,128]{1,0:T(8,128)S(1)} %add.212), channel_id=1, source_target_pairs={{0,8},{1,3},{2,10},{3,1},{4,12},{5,7},{6,14},{7,5},{8,0},{9,11},{1... | collective-permute-start | bytes 393224 | tf_op jit(solution)/shard_map/ppermute | solution.py:32
  53.6 7.3 %collective-permute-start.15 = (f32[256,128]{1,0:T(8,128)S(1)}, f32[256,128]{1,0:T(8,128)S(1)}, u32[]{:S(2)}, u32[]{:S(2)}) collective-permute-start(f32[256,128]{1,0:T(8,128)S(1)} %add.218), channel_id=1, source_target_pairs={{0,16},{1,5},{2,18},{3,7},{4,20},{5,1},{6,22},{7,3},{8,24},{9,13},... | collective-permute-start | bytes 393224 | tf_op jit(solution)/shard_map/ppermute | solution.py:32
  56.4 5.9 %collective-permute-start.9 = (f32[256,128]{1,0:T(8,128)S(1)}, f32[256,128]{1,0:T(8,128)S(1)}, u32[]{:S(2)}, u32[]{:S(2)}) collective-permute-start(f32[256,128]{1,0:T(8,128)S(1)} %add.213), channel_id=1, source_target_pairs={{0,16},{1,5},{2,18},{3,7},{4,20},{5,1},{6,22},{7,3},{8,24},{9,13},... | collective-permute-start | bytes 393224 | tf_op jit(solution)/shard_map/ppermute | solution.py:32
  60.9 1.6 %collective-permute-start.16 = (f32[256,128]{1,0:T(8,128)S(1)}, f32[256,128]{1,0:T(8,128)S(1)}, u32[]{:S(2)}, u32[]{:S(2)}) collective-permute-start(f32[256,128]{1,0:T(8,128)S(1)} %add.219), channel_id=1, source_target_pairs={{0,1},{1,0},{2,3},{3,2},{4,5},{5,4},{6,7},{7,6},{8,9},{9,8},{10,11... | collective-permute-start | bytes 393224 | tf_op jit(solution)/shard_map/ppermute | solution.py:25
  62.4 1.4 %collective-permute-start.10 = (f32[256,128]{1,0:T(8,128)S(1)}, f32[256,128]{1,0:T(8,128)S(1)}, u32[]{:S(2)}, u32[]{:S(2)}) collective-permute-start(f32[256,128]{1,0:T(8,128)S(1)} %add.214.r_1_), channel_id=1, source_target_pairs={{0,1},{1,0},{2,3},{3,2},{4,5},{5,4},{6,7},{7,6},{8,9},{9,8},{10,11... | collective-permute-start | bytes 393224 | tf_op jit(solution)/shard_map/ppermute | solution.py:25
  71.3 1.6 %collective-permute-start.17 = (f32[256,128]{1,0:T(8,128)}, f32[256,128]{1,0:T(8,128)S(1)}, u32[]{:S(2)}, u32[]{:S(2)}) collective-permute-start(f32[256,128]{1,0:T(8,128)} %get-tuple-element.22), channel_id=1, source_target_pairs={{0,1},{1,0},{2,3},{3,2},{4,5},{5,4},{6,7},{7,6},{8,9},{9,8},{10,11... | collective-permute-start | bytes 393224 | tf_op jit(solution)/shard_map/ppermute | solution.py:25
  73.7 6.0 %collective-permute-start.18 = (f32[256,128]{1,0:T(8,128)S(1)}, f32[256,128]{1,0:T(8,128)S(1)}, u32[]{:S(2)}, u32[]{:S(2)}) collective-permute-start(f32[256,128]{1,0:T(8,128)S(1)} %add.220), channel_id=1, source_target_pairs={{0,2},{1,9},{2,0},{3,11},{4,6},{5,13},{6,4},{7,15},{8,10},{9,1},{1... | collective-permute-start | bytes 393224 | tf_op jit(solution)/shard_map/ppermute | solution.py:32
  79.7 5.1 %collective-permute-start.19 = (f32[256,128]{1,0:T(8,128)S(1)}, f32[256,128]{1,0:T(8,128)S(1)}, u32[]{:S(2)}, u32[]{:S(2)}) collective-permute-start(f32[256,128]{1,0:T(8,128)S(1)} %add.221), channel_id=1, source_target_pairs={{0,4},{1,17},{2,6},{3,19},{4,0},{5,21},{6,2},{7,23},{8,12},{9,25},... | collective-permute-start | bytes 393224 | tf_op jit(solution)/shard_map/ppermute | solution.py:32
  84.8 5.0 %collective-permute-start.20 = (f32[256,128]{1,0:T(8,128)S(1)}, f32[256,128]{1,0:T(8,128)S(1)}, u32[]{:S(2)}, u32[]{:S(2)}) collective-permute-start(f32[256,128]{1,0:T(8,128)S(1)} %add.222), channel_id=1, source_target_pairs={{0,8},{1,3},{2,10},{3,1},{4,12},{5,7},{6,14},{7,5},{8,0},{9,11},{1... | collective-permute-start | bytes 393224 | tf_op jit(solution)/shard_map/ppermute | solution.py:32
  89.9 7.3 %collective-permute-start.21 = (f32[256,128]{1,0:T(8,128)S(1)}, f32[256,128]{1,0:T(8,128)S(1)}, u32[]{:S(2)}, u32[]{:S(2)}) collective-permute-start(f32[256,128]{1,0:T(8,128)S(1)} %add.223), channel_id=1, source_target_pairs={{0,16},{1,5},{2,18},{3,7},{4,20},{5,1},{6,22},{7,3},{8,24},{9,13},... | collective-permute-start | bytes 393224 | tf_op jit(solution)/shard_map/ppermute | solution.py:32
  97.2 3.8 %copy-start = (f32[256,128]{1,0:T(8,128)}, f32[256,128]{1,0:T(8,128)S(1)}, u32[]{:S(2)}) copy-start(f32[256,128]{1,0:T(8,128)S(1)} %add.224.r_2_) | copy-start | bytes 393220
  97.2 3.8 %collective-permute-start.22 = (f32[256,128]{1,0:T(8,128)S(1)}, f32[256,128]{1,0:T(8,128)S(1)}, u32[]{:S(2)}, u32[]{:S(2)}) collective-permute-start(f32[256,128]{1,0:T(8,128)S(1)} %add.224.r_2_), channel_id=1, source_target_pairs={{0,1},{1,0},{2,3},{3,2},{4,5},{5,4},{6,7},{7,6},{8,9},{9,8},{10,11... | collective-permute-start | bytes 393224 | tf_op jit(solution)/shard_map/ppermute | solution.py:25
  106.0 1.4 %collective-permute-start.23 = (f32[2,40]{1,0:T(2,128)S(1)}, f32[2,40]{1,0:T(2,128)S(1)}, u32[]{:S(2)}, u32[]{:S(2)}) collective-permute-start(f32[2,40]{1,0:T(2,128)S(1)} %pad_maximum_fusion.3), channel_id=1, source_target_pairs={{0,1},{1,0},{2,3},{3,2},{4,5},{5,4},{6,7},{7,6},{8,9},{9,8},{10,11... | collective-permute-start | bytes 968 | tf_op jit(solution)/shard_map/ppermute | solution.py:25
  107.3 3.6 %collective-permute-start.24 = (f32[2,40]{1,0:T(2,128)S(1)}, f32[2,40]{1,0:T(2,128)S(1)}, u32[]{:S(2)}, u32[]{:S(2)}) collective-permute-start(f32[2,40]{1,0:T(2,128)S(1)} %fusion.27), channel_id=1, source_target_pairs={{0,2},{1,9},{2,0},{3,11},{4,6},{5,13},{6,4},{7,15},{8,10},{9,1},{1... | collective-permute-start | bytes 968 | tf_op jit(solution)/shard_map/ppermute | solution.py:32
  111.0 3.6 %collective-permute-start.25 = (f32[2,40]{1,0:T(2,128)S(1)}, f32[2,40]{1,0:T(2,128)S(1)}, u32[]{:S(2)}, u32[]{:S(2)}) collective-permute-start(f32[2,40]{1,0:T(2,128)S(1)} %fusion.28), channel_id=1, source_target_pairs={{0,4},{1,17},{2,6},{3,19},{4,0},{5,21},{6,2},{7,23},{8,12},{9,25},... | collective-permute-start | bytes 968 | tf_op jit(solution)/shard_map/ppermute | solution.py:32
  114.6 3.6 %collective-permute-start.26 = (f32[2,40]{1,0:T(2,128)S(1)}, f32[2,40]{1,0:T(2,128)S(1)}, u32[]{:S(2)}, u32[]{:S(2)}) collective-permute-start(f32[2,40]{1,0:T(2,128)S(1)} %add.227), channel_id=1, source_target_pairs={{0,8},{1,3},{2,10},{3,1},{4,12},{5,7},{6,14},{7,5},{8,0},{9,11},{1... | collective-permute-start | bytes 968 | tf_op jit(solution)/shard_map/ppermute | solution.py:32
  118.2 4.5 %copy-start.6 = (f32[40]{0:T(128)S(1)}, f32[40]{0:T(128)}, u32[]{:S(2)}) copy-start(f32[40]{0:T(128)} %param.21) | copy-start | bytes 484
  118.2 4.5 %collective-permute-start.27 = (f32[2,40]{1,0:T(2,128)S(1)}, f32[2,40]{1,0:T(2,128)S(1)}, u32[]{:S(2)}, u32[]{:S(2)}) collective-permute-start(f32[2,40]{1,0:T(2,128)S(1)} %add.228), channel_id=1, source_target_pairs={{0,16},{1,5},{2,18},{3,7},{4,20},{5,1},{6,22},{7,3},{8,24},{9,13},... | collective-permute-start | bytes 968 | tf_op jit(solution)/shard_map/ppermute | solution.py:32
  (7 other events, 4.7 us)

commit v2 on v1

v2 whole, which is shorter than its diff:
```python
import jax
import jax.numpy as jnp
from jax import lax
from jax.experimental import pallas as pl
from jax.experimental.pallas import tpu as pltpu
from jax.sharding import PartitionSpec as P

TEMPL = 40
PENALTY = 1.0
LEARN_RATE = 2.0
GROUP = 8
LIMIT = 8 * 1024 * 1024
UNROLL = 8
VMEM = pltpu.VMEM
SMEM = pltpu.SMEM


def bits_of(count):
    bits, bit = [], 1
    while bit < count:
        bits.append(bit)
        bit *= 2
    return bits


def swap_cores(value):
    return lax.ppermute(value, "grp", [(0, 1), (1, 0)])


def exchange(value, steps, count):
    perm = [
        (2 * b + core, 2 * (b ^ steps[core]) + core) for b in range(count) for core in range(2)
    ]
    return lax.ppermute(value, ("blk", "grp"), perm)


def sum_steps(count, turned):
    bits = bits_of(count)
    middle = len(bits) // 2
    low, high = bits[:middle], bits[middle:]
    if turned:
        low, high = high, low
    return list(zip(low + high, low[::-1] + high[::-1]))


def all_sum(values, count):
    orders = [sum_steps(count, i % 2 == 1) for i in range(len(values))]
    for turn in range(len(orders[0])):
        sent = [exchange(v, order[turn], count) for v, order in zip(values, orders)]
        values = [v + r for v, r in zip(values, sent)]
    return values


def row_of(row, height, width):
    return jnp.broadcast_to(row, (height, width))


def refresh(total, before, counted, observed):
    moved = jnp.clip((total + before) / (counted + 1.0), 0.0, 1.0)
    return jnp.where(observed > 0.5, before, moved)


def load_windows(place_ref, field_ref, window_ref, tiles, list_len):
    @pl.loop(0, tiles // GROUP, unroll=UNROLL)
    def _(group):
        base = pl.multiple_of(group * GROUP, GROUP)
        for i in range(GROUP):
            for k in range(list_len):
                spot = place_ref[(base + i) * list_len + k]
                window_ref[k, pl.ds(base + i, 1), :] = field_ref[pl.ds(spot, 1), :]


def fetch_rows(window_ref, rows, slot, list_len, width):
    lane = slot & (width - 1)
    which = slot // width
    result = jnp.zeros(slot.shape, jnp.float32)
    for k in range(list_len):
        taken = jnp.take_along_axis(window_ref[k, rows, :], lane, axis=1, mode="promise_in_bounds")
        result = jnp.where(which == k, taken, result)
    return result


def split_three(value):
    first = value.astype(jnp.bfloat16).astype(jnp.float32)
    rest = value - first
    second = rest.astype(jnp.bfloat16).astype(jnp.float32)
    return first, second, rest - second


def scatter_tile(place_ref, sum_ref, tile, lows, tops, values, list_len, width):
    narrow = width // 2
    height = 2 * list_len
    row = lax.broadcasted_iota(jnp.int32, (height, width), 0)
    spot = lax.broadcasted_iota(jnp.int32, (narrow, width), 0)
    hot, left = [], []
    for low, top, parts in zip(lows, tops, values):
        hot.append((row_of(low, narrow, width) == spot).astype(jnp.float32).astype(jnp.bfloat16))
        here = row_of(top, height, width) == row
        left.append(
            jnp.concatenate(
                [jnp.where(here, row_of(part, height, width), 0.0) for part in parts], axis=0
            ).astype(jnp.bfloat16)
        )
    summed = lax.dot_general(
        jnp.concatenate(left, axis=1),
        jnp.concatenate(hot, axis=1),
        (((1,), (1,)), ((), ())),
        preferred_element_type=jnp.float32,
    )
    total = summed[:height]
    for j in range(1, len(values[0])):
        total = total + summed[j * height : (j + 1) * height]
    total = jnp.concatenate([total[:list_len], total[list_len:]], axis=1)
    spots = [place_ref[tile * list_len + k] for k in range(list_len)]
    olds = [sum_ref[pl.ds(at, 1), :] for at in spots]
    for k, at in enumerate(spots):
        sum_ref[pl.ds(at, 1), :] = olds[k] + total[k : k + 1]


def slot_parts(slot, list_len, width):
    narrow = width // 2
    low = slot & (narrow - 1)
    top = ((slot & (width - 1)) // narrow) * list_len + slot // width
    return low, jnp.where(slot < list_len * width, top, 2 * list_len)


def hand_out(sum_ref, refs):
    height = refs[0].shape[0]
    for i, ref in enumerate(refs):
        ref[...] = sum_ref[i * height : (i + 1) * height]


def renew(field_ref, source_refs, before_ref, counted_refs, observed_ref):
    height = source_refs[0].shape[0]
    share = counted_refs[0].shape[0] // height
    for i, source in enumerate(source_refs):
        part = slice(i * height, (i + 1) * height)
        counted = counted_refs[i // share][(i % share) * height : (i % share + 1) * height]
        field_ref[part] = refresh(source[...], before_ref[part], counted, observed_ref[part])


def count_kernel(*refs, list_len):
    place_ref, slot_ref = refs[:2]
    out_refs, sum_ref = refs[2:-1], refs[-1]
    arity, tiles, width = slot_ref.shape
    sum_ref[...] = jnp.zeros_like(sum_ref)

    @pl.loop(0, tiles // GROUP, unroll=UNROLL)
    def _(group):
        base = pl.multiple_of(group * GROUP, GROUP)
        rows = pl.ds(base, GROUP)
        halves = [slot_parts(slot_ref[s, rows, :], list_len, width) for s in range(arity)]
        one = jnp.ones((1, width), jnp.float32)
        for i in range(GROUP):
            scatter_tile(
                place_ref,
                sum_ref,
                base + i,
                [h[0][i : i + 1] for h in halves],
                [h[1][i : i + 1] for h in halves],
                [(one,)] * arity,
                list_len,
                width,
            )

    hand_out(sum_ref, out_refs)


def sweep_kernel(*refs, list_len, first, streams):
    refs = list(refs)

    def take(number):
        taken = refs[:number]
        del refs[:number]
        return taken

    (place_ref,) = take(1)
    if first:
        (field_ref,) = take(1)
    else:
        sources, counts = take(streams), take(2)
        before_ref, observed_ref, old_ref = take(3)
    slot_ref, coef_ref, off_ref, dual_ref, temp_ref, weight_ref, moved_ref = take(7)
    if not first:
        next_ref, field_ref = take(2)
    out_refs = take(streams)
    window_ref, sum_ref = refs
    arity, tiles, width = slot_ref.shape
    templates = weight_ref.shape[1]
    if not first:
        renew(field_ref, sources, before_ref, counts, observed_ref)
    load_windows(place_ref, field_ref, window_ref, tiles, list_len)
    sum_ref[...] = jnp.zeros_like(sum_ref)

    @pl.loop(0, tiles // GROUP, unroll=UNROLL)
    def _(group):
        base = pl.multiple_of(group * GROUP, GROUP)
        rows = pl.ds(base, GROUP)
        templ = temp_ref[rows, :]
        hot = row_of(templ, GROUP, templates) == lax.broadcasted_iota(
            jnp.int32, (GROUP, templates), 1
        )
        weight = jnp.sum(
            jnp.where(hot, row_of(weight_ref[...], GROUP, templates), 0.0), axis=1, keepdims=True
        )
        weight = jnp.broadcast_to(weight, (GROUP, width))
        squared = jnp.broadcast_to(templ % 2 == 1, (GROUP, width))
        slots = [slot_ref[s, rows, :] for s in range(arity)]
        used = [q < list_len * width for q in slots]
        acts = [jnp.where(used[s], coef_ref[s, rows, :], 0.0) for s in range(arity)]
        copies = [fetch_rows(window_ref, rows, q, list_len, width) for q in slots]
        duals = [dual_ref[s, rows, :] for s in range(arity)]
        if not first:
            duals = [
                d + jnp.where(m, old_ref[s, rows, :] - c, 0.0)
                for s, (d, m, c) in enumerate(zip(duals, used, copies))
            ]
            for s in range(arity):
                next_ref[s, rows, :] = duals[s]
        shifted = [c - d for c, d in zip(copies, duals)]
        linear = sum(a * v for a, v in zip(acts, shifted)) + off_ref[rows, :]
        norm = sum(a * a for a in acts)
        plain = jnp.clip(linear / norm, 0.0, weight / PENALTY)
        square = 2.0 * weight * jnp.maximum(linear, 0.0) / (PENALTY + 2.0 * weight * norm)
        chosen = jnp.where(squared, square, plain)
        parts = []
        for s in range(arity):
            moved = shifted[s] - chosen * acts[s]
            moved_ref[s, rows, :] = moved
            parts.append(split_three(jnp.where(used[s], moved + duals[s], 0.0)))
        halves = [slot_parts(q, list_len, width) for q in slots]
        for i in range(GROUP):
            scatter_tile(
                place_ref,
                sum_ref,
                base + i,
                [h[0][i : i + 1] for h in halves],
                [h[1][i : i + 1] for h in halves],
                [tuple(p[i : i + 1] for p in part) for part in parts],
                list_len,
                width,
            )

    hand_out(sum_ref, out_refs)


def energy_kernel(*refs, list_len, streams):
    refs = list(refs)

    def take(number):
        taken = refs[:number]
        del refs[:number]
        return taken

    place_ref, own_ref = take(2)
    sources, counts = take(streams), take(2)
    before_ref, observed_ref, target_ref, old_ref = take(4)
    slot_ref, coef_ref, off_ref, dual_ref, temp_ref, weight_ref = take(6)
    energy_ref, next_ref, owned_ref = take(3)
    window_ref, other_ref, field_ref = refs
    arity, tiles, width = slot_ref.shape
    templates = weight_ref.shape[1]
    renew(field_ref, sources, before_ref, counts, observed_ref)
    piece = owned_ref.shape[0] // 2
    for h in range(2):
        start = pl.multiple_of(own_ref[h], GROUP)
        owned_ref[h * piece : (h + 1) * piece] = field_ref[pl.ds(start, piece), :]
    load_windows(place_ref, field_ref, window_ref, tiles, list_len)
    load_windows(place_ref, target_ref, other_ref, tiles, list_len)

    def step(group, totals):
        base = pl.multiple_of(group * GROUP, GROUP)
        rows = pl.ds(base, GROUP)
        templ = temp_ref[rows, :]
        hot = row_of(templ, GROUP, templates) == lax.broadcasted_iota(
            jnp.int32, (GROUP, templates), 1
        )
        squared = jnp.broadcast_to(templ % 2 == 1, (GROUP, width))
        linears = [off_ref[rows, :]] * 2
        for s in range(arity):
            slot = slot_ref[s, rows, :]
            used = slot < list_len * width
            act = jnp.where(used, coef_ref[s, rows, :], 0.0)
            copies = [
                fetch_rows(ref, rows, slot, list_len, width) for ref in (window_ref, other_ref)
            ]
            linears = [line + act * copy for line, copy in zip(linears, copies)]
            next_ref[s, rows, :] = dual_ref[s, rows, :] + jnp.where(
                used, old_ref[s, rows, :] - copies[0], 0.0
            )
        results = []
        for total, line in zip(totals, linears):
            positive = jnp.maximum(line, 0.0)
            rule = jnp.where(squared, positive * positive, positive)
            tile = jnp.sum(rule, axis=1, keepdims=True)
            results.append(
                total + jnp.where(hot, jnp.broadcast_to(tile, (GROUP, templates)), 0.0)
            )
        return tuple(results)

    zero = jnp.zeros((GROUP, templates), jnp.float32)
    totals = lax.fori_loop(0, tiles // GROUP, step, (zero, zero), unroll=UNROLL)
    for i, total in enumerate(totals):
        energy_ref[i : i + 1, :] = jnp.sum(total, axis=0, keepdims=True)


def specs(count, scalars):
    return [pl.BlockSpec(memory_space=SMEM)] * scalars + [
        pl.BlockSpec(memory_space=VMEM)
    ] * (count - scalars)


def call(body, args, scalars, outs, scratch, work):
    shapes = tuple(jax.ShapeDtypeStruct(s, jnp.float32) for s in outs)
    return pl.pallas_call(
        body,
        out_shape=shapes,
        in_specs=specs(len(args), scalars),
        out_specs=tuple(specs(len(outs), 0)),
        scratch_shapes=[VMEM(s, jnp.float32) for s in scratch],
        compiler_params=pltpu.CompilerParams(vmem_limit_bytes=LIMIT),
        cost_estimate=pl.CostEstimate(flops=0, bytes_accessed=work, transcendentals=0),
    )(*args)


def local(
    atom_value,
    target_value,
    observed,
    block_owner,
    block_local,
    slot_index,
    coefficient,
    offset,
    dual_value,
    template,
    weight,
):
    device = lax.axis_index("blk")
    count = lax.axis_size("blk")
    core = lax.axis_index("grp")
    groups = lax.axis_size("grp")
    atom_blk, width = atom_value.shape
    tiles = template.shape[1]
    list_len = block_owner.shape[1]
    arity = slot_index.shape[0]
    piece = atom_blk // 2
    half = count * piece
    bits = bits_of(count)
    middle = len(bits) // 2
    low, high = bits[:middle], bits[middle:]
    orders = (high + low, high[::-1] + low[::-1])

    def position(owner, part):
        spots = [
            sum(((owner // bit) % 2) << j for j, bit in enumerate(order)) for order in orders
        ]
        return jnp.where(part == 0, spots[0], spots[1])

    def place_of(owner, spot):
        part = spot // piece
        return (part ^ core) * half + position(owner, part) * piece + spot % piece

    start = device * tiles
    place = place_of(
        lax.dynamic_slice_in_dim(block_owner, start, tiles, 0),
        lax.dynamic_slice_in_dim(block_local, start, tiles, 0),
    ).reshape(-1)
    own = place_of(device, jnp.arange(2, dtype=jnp.int32) * piece)
    slots = slot_index.reshape(arity, tiles, width)
    coeffs = coefficient.reshape(arity, tiles, width)
    offsets = offset.reshape(tiles, width)
    duals = dual_value.reshape(arity, tiles, width)
    templates = (core * (TEMPL // groups) + template[0])[:, None]
    weights = weight[None, :]
    big = (2 * half, width)
    stream = (half // 2, width)
    small = (half, width)
    streams = 4
    rule = (arity, tiles, width)
    window = (list_len, tiles, width)

    gathered = jnp.stack(
        [
            lax.dynamic_slice_in_dim(f.astype(jnp.float32), core * piece, piece, 0)
            for f in (atom_value, observed, target_value)
        ]
    )
    counts = None
    pending = sum_steps(count, False)
    for turn, steps in enumerate(zip(*orders)):
        arrived = exchange(gathered, steps, count)
        step = jnp.where(core == 0, steps[0], steps[1])
        upper = (device // step) % 2 == 1
        if turn == 0:
            counts = call(
                lambda *r: count_kernel(*r, list_len=list_len),
                (place, slots), 1, (small, small), (big,), 10_000_000,
            )
        elif turn == 1:
            counts = counts[0] + swap_cores(counts[1])
        else:
            counts = counts + exchange(counts, pending.pop(0), count)
        gathered = jnp.where(
            upper,
            jnp.concatenate([arrived, gathered], axis=1),
            jnp.concatenate([gathered, arrived], axis=1),
        )
        gathered, counts = lax.optimization_barrier((gathered, counts))
    gathered = jnp.concatenate([gathered, swap_cores(gathered)], axis=1)
    values, fixed, targets = gathered[0], gathered[1], gathered[2]
    for steps in pending:
        counts = counts + exchange(counts, steps, count)
    counts = [counts, swap_cores(counts)]

    def reduce_all(parts):
        mine = [keep + swap_cores(send) for keep, send in zip(parts[:2], parts[2:])]
        mine = all_sum(mine, count)
        return mine + [swap_cores(m) for m in mine]

    moved, *sums = call(
        lambda *r: sweep_kernel(*r, list_len=list_len, first=True, streams=streams),
        (place, values, slots, coeffs, offsets, duals, templates, weights),
        1,
        (rule,) + (stream,) * streams,
        (window, big),
        15_000_000,
    )
    sums = reduce_all(sums)
    moved, duals, values, *sums = call(
        lambda *r: sweep_kernel(*r, list_len=list_len, first=False, streams=streams),
        (place, *sums, *counts, values, fixed, moved,
         slots, coeffs, offsets, duals, templates, weights),
        1,
        (rule, rule, big) + (stream,) * streams,
        (window, big),
        15_000_000,
    )
    sums = reduce_all(sums)
    energies, dual_next, consensus = call(
        lambda *r: energy_kernel(*r, list_len=list_len, streams=streams),
        (place, own, *sums, *counts, values, fixed, targets, moved,
         slots, coeffs, offsets, duals, templates, weights),
        2,
        ((2, TEMPL), rule, (atom_blk, width)),
        (window, window, big),
        10_000_000,
    )
    (energies,) = all_sum([energies + swap_cores(energies)], count)
    e_value, e_target = energies[0], energies[1]
    weight_next = weight * jnp.exp(-LEARN_RATE * (e_value - e_target) / (e_value + e_target + 1.0))
    return consensus, dual_next.reshape(dual_value.shape), weight_next


def solution(mesh):
    in_specs = (
        P("blk", None),
        P("blk", None),
        P("blk", None),
        P(),
        P(),
        P(None, "grp", "blk"),
        P(None, "grp", "blk"),
        P("grp", "blk"),
        P(None, "grp", "blk"),
        P("grp", "blk"),
        P(),
    )
    out_specs = (P("blk", None), P(None, "grp", "blk"), P())
    return jax.shard_map(local, mesh=mesh, in_specs=in_specs, out_specs=out_specs, check_vma=False)
```

time: 124 us -> 105 us (0.85)
  Pallas kernels: 24.9 us -> 8.27 us
  waiting for transfers between devices: 45.1 us -> 55.8 us
  starting transfers between devices: 42.6 us -> 34.7 us
  other arithmetic: 5.44 us -> 2.39 us
  local copies, waits for them, and re-layouts: 4.27 us -> 2.54 us
    pallas_call x5 -> x4, Pallas kernels: 24.9 us -> 8.27 us  [call(): pl.pallas_call(body, out_shape=shapes, in_specs=specs(len(args), scalars)...]
    ppermute x20 -> x28, starting transfers between devices: 40.7 us -> 30.3 us  [exchange(): return lax.ppermute(value, ('blk', 'grp'), perm)]
    ppermute x20 -> x28, waiting for transfers between devices: 42.3 us -> 50.6 us  [exchange(): return lax.ppermute(value, ('blk', 'grp'), perm)]
    ppermute x8 -> x12, starting transfers between devices: 1.95 us -> 4.41 us  [swap_cores(): return lax.ppermute(value, 'grp', [(0, 1), (1, 0)])]
    ppermute x8 -> x12, waiting for transfers between devices: 2.83 us -> 5.21 us  [swap_cores(): return lax.ppermute(value, 'grp', [(0, 1), (1, 0)])]
    add x22 -> x32, other arithmetic: 2.49 us -> 1.08 us  [the longest x2 0.81 us: place_of(): return (part ^ core) * half + position(owner, part) * piece + spot % piece]
  transfers between devices with their start and end apart: 28 -> 40, of which waited for: 20 -> 25; matrix products, arithmetic and copies ran while one was open for 4% -> 1% of each run, Pallas kernels for 12% -> 2%
where the time goes in v2:
time: 105 us
  waiting for transfers between devices  55.8 us (53%)
  starting transfers between devices  34.7 us (33%)
  Pallas kernels  8.27 us (8%)
  local copies, waits for them, and re-layouts  2.54 us (2%)
  other arithmetic  2.39 us (2%)
  between operations  1.1 us (1%)
    ppermute x28, waiting for transfers between devices, exchange(): return lax.ppermute(value, ('blk', 'grp'), perm)  50.6 us
    ppermute x28, starting transfers between devices, exchange(): return lax.ppermute(value, ('blk', 'grp'), perm)  30.3 us
    pallas_call x4, Pallas kernels, call(): pl.pallas_call(body, out_shape=shapes, in_specs=specs(len(args), scalars)...  8.27 us
    ppermute x12, waiting for transfers between devices, swap_cores(): return lax.ppermute(value, 'grp', [(0, 1), (1, 0)])  5.21 us
    ppermute x12, starting transfers between devices, swap_cores(): return lax.ppermute(value, 'grp', [(0, 1), (1, 0)])  4.41 us
  transfers between devices with their start and end apart: 40, of which 25 were waited for; matrix products, arithmetic and copies ran while one was open for 1% of the time, Pallas kernels for 2%

profile of v2, /device:TPU:0, one launch (start us, length us, event | category | flops | bytes accessed | tf_op | source)
XLA Modules:
  0.0 104.8 jit_solution(14984709867421711039)
XLA Ops:
  2.1 3.1 %collective-permute-start = (f32[3,16,128]{2,1,0:T(8,128)S(1)}, f32[3,16,128]{2,1,0:T(8,128)S(1)}, u32[]{:S(2)}, u32[]{:S(2)}) collective-permute-start(f32[3,16,128]{2,1,0:T(8,128)S(1)} %pad_maximum_fusion), channel_id=1, source_target_pairs={{0,8},{1,17},{2,10},{3,19},{4,12},{5,21},{6,14},{7,23},{8,0},{9,25... | collective-permute-start | bytes 73736 | tf_op jit(solution)/shard_map/ppermute | solution.py:34
  6.2 1.9 %shard_map.130 = (f32[256,128]{1,0:T(8,128)S(1)}, f32[256,128]{1,0:T(8,128)S(1)}) custom-call(s32[256]{0:T(256)S(1)} %reshape.44.r_0_, s32[3,64,128]{2,1,0:T(8,128)S(1)} %bitcast.22), custom_call_target="tpu_custom_call" | custom-call | bytes 10000000 | tf_op jit(solution)/shard_map/pallas_call | solution.py:315
  8.1 2.7 %collective-permute-start.1 = (f32[3,32,128]{2,1,0:T(8,128)S(1)}, f32[3,32,128]{2,1,0:T(8,128)S(1)}, u32[]{:S(2)}, u32[]{:S(2)}) collective-permute-start(f32[3,32,128]{2,1,0:T(8,128)S(1)} %maximum_select_fusion.3), channel_id=1, source_target_pairs={{0,16},{1,9},{2,18},{3,11},{4,20},{5,13},{6,22},{7,15},{8,24},{9,1... | collective-permute-start | bytes 147464 | tf_op jit(solution)/shard_map/ppermute | solution.py:34
  10.7 2.9 %collective-permute-done.1 = f32[3,32,128]{2,1,0:T(8,128)S(1)} collective-permute-done((f32[3,32,128]{2,1,0:T(8,128)S(1)}, f32[3,32,128]{2,1,0:T(8,128)S(1)}, u32[]{:S(2)}, u32[]{:S(2)}) %collective-permute-start.1) | collective-permute-done | bytes 49184 | tf_op jit(solution)/shard_map/ppermute | solution.py:34
  13.7 1.6 %collective-permute-start.3 = (f32[3,64,128]{2,1,0:T(8,128)S(1)}, f32[3,64,128]{2,1,0:T(8,128)S(1)}, u32[]{:S(2)}, u32[]{:S(2)}) collective-permute-start(f32[3,64,128]{2,1,0:T(8,128)S(1)} %maximum_select_fusion.2), channel_id=1, source_target_pairs={{0,2},{1,5},{2,0},{3,7},{4,6},{5,1},{6,4},{7,3},{8,10},{9,13},{10,... | collective-permute-start | bytes 294920 | tf_op jit(solution)/shard_map/ppermute | solution.py:34
  15.8 2.6 %collective-permute-done.3 = f32[3,64,128]{2,1,0:T(8,128)S(1)} collective-permute-done((f32[3,64,128]{2,1,0:T(8,128)S(1)}, f32[3,64,128]{2,1,0:T(8,128)S(1)}, u32[]{:S(2)}, u32[]{:S(2)}) %collective-permute-start.3) | collective-permute-done | bytes 98336 | tf_op jit(solution)/shard_map/ppermute | solution.py:34
  18.4 1.8 %collective-permute-done.4 = f32[256,128]{1,0:T(8,128)S(1)} collective-permute-done((f32[256,128]{1,0:T(8,128)S(1)}, f32[256,128]{1,0:T(8,128)S(1)}, u32[]{:S(2)}, u32[]{:S(2)}) %collective-permute-start.4) | collective-permute-done | bytes 131104 | tf_op jit(solution)/shard_map/ppermute | solution.py:34
  20.3 1.7 %collective-permute-start.5 = (f32[3,128,128]{2,1,0:T(8,128)S(1)}, f32[3,128,128]{2,1,0:T(8,128)S(1)}, u32[]{:S(2)}, u32[]{:S(2)}) collective-permute-start(f32[3,128,128]{2,1,0:T(8,128)S(1)} %maximum_select_fusion.1), channel_id=1, source_target_pairs={{0,4},{1,3},{2,6},{3,1},{4,0},{5,7},{6,2},{7,5},{8,12},{9,11},{10,... | collective-permute-start | bytes 589832 | tf_op jit(solution)/shard_map/ppermute | solution.py:34
  22.3 5.0 %collective-permute-done.6 = f32[256,128]{1,0:T(8,128)S(1)} collective-permute-done((f32[256,128]{1,0:T(8,128)S(1)}, f32[256,128]{1,0:T(8,128)S(1)}, u32[]{:S(2)}, u32[]{:S(2)}) %collective-permute-start.6) | collective-permute-done | bytes 131104 | tf_op jit(solution)/shard_map/ppermute | solution.py:34
  30.2 2.1 %shard_map.131 = (f32[3,64,128]{2,1,0:T(8,128)S(1)}, f32[128,128]{1,0:T(8,128)S(1)}, f32[128,128]{1,0:T(8,128)S(1)}, f32[128,128]{1,0:T(8,128)S(1)}, f32[128,128]{1,0:T(8,128)S(1)}) custom-call(s32[256]{0:T(256)S(1)} %reshape.44.r_0_, f32[512,128]{1,0:T(8,128)S(1)} %get-tuple-element.63.r_1_.r_7_, s32[3,64,128]{2,1,0:T(8,128)S(1)} %bitcast.23, ...), custom_call_target="tpu_custom_call" | custom-call | bytes 15000000 | tf_op jit(solution)/shard_map/pallas_call | solution.py:315
  33.1 3.1 %collective-permute-start.13 = (f32[128,128]{1,0:T(8,128)S(1)}, f32[128,128]{1,0:T(8,128)S(1)}, u32[]{:S(2)}, u32[]{:S(2)}) collective-permute-start(f32[128,128]{1,0:T(8,128)S(1)} %get-tuple-element.42), channel_id=1, source_target_pairs={{0,1},{1,0},{2,3},{3,2},{4,5},{5,4},{6,7},{7,6},{8,9},{9,8},{10,11... | collective-permute-start | bytes 196616 | tf_op jit(solution)/shard_map/ppermute | solution.py:27
  37.8 3.3 %collective-permute-start.21 = (f32[256,128]{1,0:T(8,128)S(1)}, f32[256,128]{1,0:T(8,128)S(1)}, u32[]{:S(2)}, u32[]{:S(2)}) collective-permute-start(f32[256,128]{1,0:T(8,128)S(1)} %add.301), channel_id=1, source_target_pairs={{0,16},{1,9},{2,18},{3,11},{4,20},{5,13},{6,22},{7,15},{8,24},{9,1... | collective-permute-start | bytes 393224 | tf_op jit(solution)/shard_map/ppermute | solution.py:34
  41.1 1.6 %collective-permute-start.10 = (f32[128,128]{1,0:T(8,128)S(1)}, f32[128,128]{1,0:T(8,128)S(1)}, u32[]{:S(2)}, u32[]{:S(2)}) collective-permute-start(f32[128,128]{1,0:T(8,128)S(1)} %add.292), channel_id=1, source_target_pairs={{0,4},{1,3},{2,6},{3,1},{4,0},{5,7},{6,2},{7,5},{8,12},{9,11},{10,... | collective-permute-start | bytes 196616 | tf_op jit(solution)/shard_map/ppermute | solution.py:34
  43.3 2.1 %collective-permute-done.10 = f32[128,128]{1,0:T(8,128)S(1)} collective-permute-done((f32[128,128]{1,0:T(8,128)S(1)}, f32[128,128]{1,0:T(8,128)S(1)}, u32[]{:S(2)}, u32[]{:S(2)}) %collective-permute-start.10) | collective-permute-done | bytes 65568 | tf_op jit(solution)/shard_map/ppermute | solution.py:34
  45.4 1.6 %collective-permute-start.11 = (f32[128,128]{1,0:T(8,128)S(1)}, f32[128,128]{1,0:T(8,128)S(1)}, u32[]{:S(2)}, u32[]{:S(2)}) collective-permute-start(f32[128,128]{1,0:T(8,128)S(1)} %add.293), channel_id=1, source_target_pairs={{0,8},{1,17},{2,10},{3,19},{4,12},{5,21},{6,14},{7,23},{8,0},{9,25... | collective-permute-start | bytes 196616 | tf_op jit(solution)/shard_map/ppermute | solution.py:34
  47.1 2.8 %collective-permute-done.15 = f32[128,128]{1,0:T(8,128)S(1)} collective-permute-done((f32[128,128]{1,0:T(8,128)S(1)}, f32[128,128]{1,0:T(8,128)S(1)}, u32[]{:S(2)}, u32[]{:S(2)}) %collective-permute-start.15) | collective-permute-done | bytes 65568 | tf_op jit(solution)/shard_map/ppermute | solution.py:34
  51.2 3.0 %collective-permute-done.16 = f32[128,128]{1,0:T(8,128)S(1)} collective-permute-done((f32[128,128]{1,0:T(8,128)S(1)}, f32[128,128]{1,0:T(8,128)S(1)}, u32[]{:S(2)}, u32[]{:S(2)}) %collective-permute-start.16) | collective-permute-done | bytes 65568 | tf_op jit(solution)/shard_map/ppermute | solution.py:34
  55.0 1.8 %collective-permute-done.12 = f32[128,128]{1,0:T(8,128)S(1)} collective-permute-done((f32[128,128]{1,0:T(8,128)S(1)}, f32[128,128]{1,0:T(8,128)S(1)}, u32[]{:S(2)}, u32[]{:S(2)}) %collective-permute-start.12) | collective-permute-done | bytes 65568 | tf_op jit(solution)/shard_map/ppermute | solution.py:34
  56.9 1.6 %collective-permute-done.17 = f32[128,128]{1,0:T(8,128)S(1)} collective-permute-done((f32[128,128]{1,0:T(8,128)S(1)}, f32[128,128]{1,0:T(8,128)S(1)}, u32[]{:S(2)}, u32[]{:S(2)}) %collective-permute-start.17) | collective-permute-done | bytes 65568 | tf_op jit(solution)/shard_map/ppermute | solution.py:34
  59.9 2.2 %shard_map.132 = (f32[3,64,128]{2,1,0:T(8,128)S(1)}, f32[3,64,128]{2,1,0:T(8,128)S(1)}, f32[512,128]{1,0:T(8,128)S(1)}, f32[128,128]{1,0:T(8,128)S(1)}, f32[128,...) custom-call(s32[256]{0:T(256)S(1)} %reshape.44.r_0_, f32[128,128]{1,0:T(8,128)S(1)} %add.295.r_1_, ...), custom_call_target="tpu_custom_call" | custom-call | bytes 15000000 | tf_op jit(solution)/shard_map/pallas_call | solution.py:315
  64.7 3.1 %collective-permute-done.24 = f32[128,128]{1,0:T(8,128)S(1)} collective-permute-done((f32[128,128]{1,0:T(8,128)S(1)}, f32[128,128]{1,0:T(8,128)S(1)}, u32[]{:S(2)}, u32[]{:S(2)}) %collective-permute-start.24) | collective-permute-done | bytes 65568 | tf_op jit(solution)/shard_map/ppermute | solution.py:34
  69.7 2.4 %collective-permute-done.25 = f32[128,128]{1,0:T(8,128)S(1)} collective-permute-done((f32[128,128]{1,0:T(8,128)S(1)}, f32[128,128]{1,0:T(8,128)S(1)}, u32[]{:S(2)}, u32[]{:S(2)}) %collective-permute-start.25) | collective-permute-done | bytes 65568 | tf_op jit(solution)/shard_map/ppermute | solution.py:34
  72.6 3.2 %collective-permute-done.30 = f32[128,128]{1,0:T(8,128)S(1)} collective-permute-done((f32[128,128]{1,0:T(8,128)S(1)}, f32[128,128]{1,0:T(8,128)S(1)}, u32[]{:S(2)}, u32[]{:S(2)}) %collective-permute-start.30) | collective-permute-done | bytes 65568 | tf_op jit(solution)/shard_map/ppermute | solution.py:34
  75.8 1.5 %collective-permute-start.31 = (f32[128,128]{1,0:T(8,128)S(1)}, f32[128,128]{1,0:T(8,128)S(1)}, u32[]{:S(2)}, u32[]{:S(2)}) collective-permute-start(f32[128,128]{1,0:T(8,128)S(1)} %add.310), channel_id=1, source_target_pairs={{0,2},{1,5},{2,0},{3,7},{4,6},{5,1},{6,4},{7,3},{8,10},{9,13},{10,... | collective-permute-start | bytes 196616 | tf_op jit(solution)/shard_map/ppermute | solution.py:34
  77.4 2.7 %collective-permute-done.31 = f32[128,128]{1,0:T(8,128)S(1)} collective-permute-done((f32[128,128]{1,0:T(8,128)S(1)}, f32[128,128]{1,0:T(8,128)S(1)}, u32[]{:S(2)}, u32[]{:S(2)}) %collective-permute-start.31) | collective-permute-done | bytes 65568 | tf_op jit(solution)/shard_map/ppermute | solution.py:34
  82.6 1.8 %collective-permute-done.32 = f32[128,128]{1,0:T(8,128)S(1)} collective-permute-done((f32[128,128]{1,0:T(8,128)S(1)}, f32[128,128]{1,0:T(8,128)S(1)}, u32[]{:S(2)}, u32[]{:S(2)}) %collective-permute-start.32) | collective-permute-done | bytes 65568 | tf_op jit(solution)/shard_map/ppermute | solution.py:34
  85.8 2.1 %shard_map.133 = (f32[2,40]{1,0:T(2,128)S(1)}, f32[3,64,128]{2,1,0:T(8,128)}, f32[32,128]{1,0:T(8,128)}) custom-call(s32[256]{0:T(256)S(1)} %reshape.44.r_0_, s32[2]{0:T(128)S(1)} %fusion.9.r_1_, f32[128,128]{1,0:T(8,128)S(1)} %add.307.r_2_, f32[128,128]{1,0:T(8,128)S(1)} %add.312.r_3_, f32[128,128]{1,0:T(8,128)S(1)} %collective-permute-done.33.r_4_, ...), custom_call_target="tpu_custom_call" | custom-call | bytes 10000000 | tf_op jit(solution)/shard_map/pallas_call | solution.py:315
  89.1 1.4 %collective-permute-start.36 = (f32[2,40]{1,0:T(2,128)S(1)}, f32[2,40]{1,0:T(2,128)S(1)}, u32[]{:S(2)}, u32[]{:S(2)}) collective-permute-start(f32[2,40]{1,0:T(2,128)S(1)} %add.313), channel_id=1, source_target_pairs={{0,2},{1,5},{2,0},{3,7},{4,6},{5,1},{6,4},{7,3},{8,10},{9,13},{10,... | collective-permute-start | bytes 968 | tf_op jit(solution)/shard_map/ppermute | solution.py:34
  90.5 2.1 %collective-permute-done.36 = f32[2,40]{1,0:T(2,128)S(1)} collective-permute-done((f32[2,40]{1,0:T(2,128)S(1)}, f32[2,40]{1,0:T(2,128)S(1)}, u32[]{:S(2)}, u32[]{:S(2)}) %collective-permute-start.36) | collective-permute-done | bytes 352 | tf_op jit(solution)/shard_map/ppermute | solution.py:34
  94.0 2.2 %collective-permute-done.37 = f32[2,40]{1,0:T(2,128)S(1)} collective-permute-done((f32[2,40]{1,0:T(2,128)S(1)}, f32[2,40]{1,0:T(2,128)S(1)}, u32[]{:S(2)}, u32[]{:S(2)}) %collective-permute-start.37) | collective-permute-done | bytes 352 | tf_op jit(solution)/shard_map/ppermute | solution.py:34
  96.2 3.6 %collective-permute-done.38 = f32[2,40]{1,0:T(2,128)S(1)} collective-permute-done((f32[2,40]{1,0:T(2,128)S(1)}, f32[2,40]{1,0:T(2,128)S(1)}, u32[]{:S(2)}, u32[]{:S(2)}) %collective-permute-start.38) | collective-permute-done | bytes 352 | tf_op jit(solution)/shard_map/ppermute | solution.py:34
  100.4 3.9 %collective-permute-done.39 = f32[2,40]{1,0:T(2,128)S(1)} collective-permute-done((f32[2,40]{1,0:T(2,128)S(1)}, f32[2,40]{1,0:T(2,128)S(1)}, u32[]{:S(2)}, u32[]{:S(2)}) %collective-permute-start.39) | collective-permute-done | bytes 352 | tf_op jit(solution)/shard_map/ppermute | solution.py:34
  (113 shorter events, 25.3 us)
Async XLA Ops:
  2.1 6.0 %collective-permute-start = (f32[3,16,128]{2,1,0:T(8,128)S(1)}, f32[3,16,128]{2,1,0:T(8,128)S(1)}, u32[]{:S(2)}, u32[]{:S(2)}) collective-permute-start(f32[3,16,128]{2,1,0:T(8,128)S(1)} %pad_maximum_fusion), channel_id=1, source_target_pairs={{0,8},{1,17},{2,10},{3,19},{4,12},{5,21},{6,14},{7,23},{8,0},{9,25... | collective-permute-start | bytes 73736 | tf_op jit(solution)/shard_map/ppermute | solution.py:34
  8.1 5.6 %collective-permute-start.1 = (f32[3,32,128]{2,1,0:T(8,128)S(1)}, f32[3,32,128]{2,1,0:T(8,128)S(1)}, u32[]{:S(2)}, u32[]{:S(2)}) collective-permute-start(f32[3,32,128]{2,1,0:T(8,128)S(1)} %maximum_select_fusion.3), channel_id=1, source_target_pairs={{0,16},{1,9},{2,18},{3,11},{4,20},{5,13},{6,22},{7,15},{8,24},{9,1... | collective-permute-start | bytes 147464 | tf_op jit(solution)/shard_map/ppermute | solution.py:34
  10.7 2.9 %collective-permute-start.2 = (f32[256,128]{1,0:T(8,128)S(1)}, f32[256,128]{1,0:T(8,128)S(1)}, u32[]{:S(2)}, u32[]{:S(2)}) collective-permute-start(f32[256,128]{1,0:T(8,128)S(1)} %get-tuple-element.33), channel_id=1, source_target_pairs={{0,1},{1,0},{2,3},{3,2},{4,5},{5,4},{6,7},{7,6},{8,9},{9,8},{10,11... | collective-permute-start | bytes 393224 | tf_op jit(solution)/shard_map/ppermute | solution.py:27
  13.7 4.7 %collective-permute-start.3 = (f32[3,64,128]{2,1,0:T(8,128)S(1)}, f32[3,64,128]{2,1,0:T(8,128)S(1)}, u32[]{:S(2)}, u32[]{:S(2)}) collective-permute-start(f32[3,64,128]{2,1,0:T(8,128)S(1)} %maximum_select_fusion.2), channel_id=1, source_target_pairs={{0,2},{1,5},{2,0},{3,7},{4,6},{5,1},{6,4},{7,3},{8,10},{9,13},{10,... | collective-permute-start | bytes 294920 | tf_op jit(solution)/shard_map/ppermute | solution.py:34
  15.3 5.0 %collective-permute-start.4 = (f32[256,128]{1,0:T(8,128)S(1)}, f32[256,128]{1,0:T(8,128)S(1)}, u32[]{:S(2)}, u32[]{:S(2)}) collective-permute-start(f32[256,128]{1,0:T(8,128)S(1)} %add.285), channel_id=1, source_target_pairs={{0,2},{1,5},{2,0},{3,7},{4,6},{5,1},{6,4},{7,3},{8,10},{9,13},{10,... | collective-permute-start | bytes 393224 | tf_op jit(solution)/shard_map/ppermute | solution.py:34
  20.3 7.2 %collective-permute-start.5 = (f32[3,128,128]{2,1,0:T(8,128)S(1)}, f32[3,128,128]{2,1,0:T(8,128)S(1)}, u32[]{:S(2)}, u32[]{:S(2)}) collective-permute-start(f32[3,128,128]{2,1,0:T(8,128)S(1)} %maximum_select_fusion.1), channel_id=1, source_target_pairs={{0,4},{1,3},{2,6},{3,1},{4,0},{5,7},{6,2},{7,5},{8,12},{9,11},{10,... | collective-permute-start | bytes 589832 | tf_op jit(solution)/shard_map/ppermute | solution.py:34
  21.9 5.5 %collective-permute-start.6 = (f32[256,128]{1,0:T(8,128)S(1)}, f32[256,128]{1,0:T(8,128)S(1)}, u32[]{:S(2)}, u32[]{:S(2)}) collective-permute-start(f32[256,128]{1,0:T(8,128)S(1)} %add.286), channel_id=1, source_target_pairs={{0,4},{1,3},{2,6},{3,1},{4,0},{5,7},{6,2},{7,5},{8,12},{9,11},{10,... | collective-permute-start | bytes 393224 | tf_op jit(solution)/shard_map/ppermute | solution.py:34
  32.3 3.8 %collective-permute-start.8 = (f32[128,128]{1,0:T(8,128)S(1)}, f32[128,128]{1,0:T(8,128)S(1)}, u32[]{:S(2)}, u32[]{:S(2)}) collective-permute-start(f32[128,128]{1,0:T(8,128)S(1)} %get-tuple-element.40), channel_id=1, source_target_pairs={{0,1},{1,0},{2,3},{3,2},{4,5},{5,4},{6,7},{7,6},{8,9},{9,8},{10,11... | collective-permute-start | bytes 196616 | tf_op jit(solution)/shard_map/ppermute | solution.py:27
  32.5 5.2 %collective-permute-start.20 = (f32[256,128]{1,0:T(8,128)S(1)}, f32[256,128]{1,0:T(8,128)S(1)}, u32[]{:S(2)}, u32[]{:S(2)}) collective-permute-start(f32[256,128]{1,0:T(8,128)S(1)} %add.287), channel_id=1, source_target_pairs={{0,8},{1,17},{2,10},{3,19},{4,12},{5,21},{6,14},{7,23},{8,0},{9,25... | collective-permute-start | bytes 393224 | tf_op jit(solution)/shard_map/ppermute | solution.py:34
  33.1 4.2 %collective-permute-start.13 = (f32[128,128]{1,0:T(8,128)S(1)}, f32[128,128]{1,0:T(8,128)S(1)}, u32[]{:S(2)}, u32[]{:S(2)}) collective-permute-start(f32[128,128]{1,0:T(8,128)S(1)} %get-tuple-element.42), channel_id=1, source_target_pairs={{0,1},{1,0},{2,3},{3,2},{4,5},{5,4},{6,7},{7,6},{8,9},{9,8},{10,11... | collective-permute-start | bytes 196616 | tf_op jit(solution)/shard_map/ppermute | solution.py:27
  36.1 4.9 %collective-permute-start.9 = (f32[128,128]{1,0:T(8,128)S(1)}, f32[128,128]{1,0:T(8,128)S(1)}, u32[]{:S(2)}, u32[]{:S(2)}) collective-permute-start(f32[128,128]{1,0:T(8,128)S(1)} %add.291), channel_id=1, source_target_pairs={{0,2},{1,5},{2,0},{3,7},{4,6},{5,1},{6,4},{7,3},{8,10},{9,13},{10,... | collective-permute-start | bytes 196616 | tf_op jit(solution)/shard_map/ppermute | solution.py:34
  37.3 5.4 %collective-permute-start.14 = (f32[128,128]{1,0:T(8,128)S(1)}, f32[128,128]{1,0:T(8,128)S(1)}, u32[]{:S(2)}, u32[]{:S(2)}) collective-permute-start(f32[128,128]{1,0:T(8,128)S(1)} %add.296), channel_id=1, source_target_pairs={{0,8},{1,17},{2,10},{3,19},{4,12},{5,21},{6,14},{7,23},{8,0},{9,25... | collective-permute-start | bytes 196616 | tf_op jit(solution)/shard_map/ppermute | solution.py:34
  37.8 13.3 %collective-permute-start.21 = (f32[256,128]{1,0:T(8,128)S(1)}, f32[256,128]{1,0:T(8,128)S(1)}, u32[]{:S(2)}, u32[]{:S(2)}) collective-permute-start(f32[256,128]{1,0:T(8,128)S(1)} %add.301), channel_id=1, source_target_pairs={{0,16},{1,9},{2,18},{3,11},{4,20},{5,13},{6,22},{7,15},{8,24},{9,1... | collective-permute-start | bytes 393224 | tf_op jit(solution)/shard_map/ppermute | solution.py:34
  41.1 4.3 %collective-permute-start.10 = (f32[128,128]{1,0:T(8,128)S(1)}, f32[128,128]{1,0:T(8,128)S(1)}, u32[]{:S(2)}, u32[]{:S(2)}) collective-permute-start(f32[128,128]{1,0:T(8,128)S(1)} %add.292), channel_id=1, source_target_pairs={{0,4},{1,3},{2,6},{3,1},{4,0},{5,7},{6,2},{7,5},{8,12},{9,11},{10,... | collective-permute-start | bytes 196616 | tf_op jit(solution)/shard_map/ppermute | solution.py:34
  42.7 7.2 %collective-permute-start.15 = (f32[128,128]{1,0:T(8,128)S(1)}, f32[128,128]{1,0:T(8,128)S(1)}, u32[]{:S(2)}, u32[]{:S(2)}) collective-permute-start(f32[128,128]{1,0:T(8,128)S(1)} %add.297), channel_id=1, source_target_pairs={{0,16},{1,9},{2,18},{3,11},{4,20},{5,13},{6,22},{7,15},{8,24},{9,1... | collective-permute-start | bytes 196616 | tf_op jit(solution)/shard_map/ppermute | solution.py:34
  45.4 5.7 %collective-permute-start.11 = (f32[128,128]{1,0:T(8,128)S(1)}, f32[128,128]{1,0:T(8,128)S(1)}, u32[]{:S(2)}, u32[]{:S(2)}) collective-permute-start(f32[128,128]{1,0:T(8,128)S(1)} %add.293), channel_id=1, source_target_pairs={{0,8},{1,17},{2,10},{3,19},{4,12},{5,21},{6,14},{7,23},{8,0},{9,25... | collective-permute-start | bytes 196616 | tf_op jit(solution)/shard_map/ppermute | solution.py:34
  49.9 4.3 %collective-permute-start.16 = (f32[128,128]{1,0:T(8,128)S(1)}, f32[128,128]{1,0:T(8,128)S(1)}, u32[]{:S(2)}, u32[]{:S(2)}) collective-permute-start(f32[128,128]{1,0:T(8,128)S(1)} %add.298), channel_id=1, source_target_pairs={{0,2},{1,5},{2,0},{3,7},{4,6},{5,1},{6,4},{7,3},{8,10},{9,13},{10,... | collective-permute-start | bytes 196616 | tf_op jit(solution)/shard_map/ppermute | solution.py:34
  51.1 7.6 %collective-permute-start.22 = (f32[256,128]{1,0:T(8,128)S(1)}, f32[256,128]{1,0:T(8,128)S(1)}, u32[]{:S(2)}, u32[]{:S(2)}) collective-permute-start(f32[256,128]{1,0:T(8,128)S(1)} %add.302.r_5_.r_6_), channel_id=1, source_target_pairs={{0,1},{1,0},{2,3},{3,2},{4,5},{5,4},{6,7},{7,6},{8,9},{9,8},{10,11... | collective-permute-start | bytes 393224 | tf_op jit(solution)/shard_map/ppermute | solution.py:27
  51.2 5.7 %collective-permute-start.12 = (f32[128,128]{1,0:T(8,128)S(1)}, f32[128,128]{1,0:T(8,128)S(1)}, u32[]{:S(2)}, u32[]{:S(2)}) collective-permute-start(f32[128,128]{1,0:T(8,128)S(1)} %add.294), channel_id=1, source_target_pairs={{0,16},{1,9},{2,18},{3,11},{4,20},{5,13},{6,22},{7,15},{8,24},{9,1... | collective-permute-start | bytes 196616 | tf_op jit(solution)/shard_map/ppermute | solution.py:34
  54.2 4.3 %collective-permute-start.17 = (f32[128,128]{1,0:T(8,128)S(1)}, f32[128,128]{1,0:T(8,128)S(1)}, u32[]{:S(2)}, u32[]{:S(2)}) collective-permute-start(f32[128,128]{1,0:T(8,128)S(1)} %add.299), channel_id=1, source_target_pairs={{0,4},{1,3},{2,6},{3,1},{4,0},{5,7},{6,2},{7,5},{8,12},{9,11},{10,... | collective-permute-start | bytes 196616 | tf_op jit(solution)/shard_map/ppermute | solution.py:34
  63.4 4.3 %collective-permute-start.24 = (f32[128,128]{1,0:T(8,128)S(1)}, f32[128,128]{1,0:T(8,128)S(1)}, u32[]{:S(2)}, u32[]{:S(2)}) collective-permute-start(f32[128,128]{1,0:T(8,128)S(1)} %add.303), channel_id=1, source_target_pairs={{0,2},{1,5},{2,0},{3,7},{4,6},{5,1},{6,4},{7,3},{8,10},{9,13},{10,... | collective-permute-start | bytes 196616 | tf_op jit(solution)/shard_map/ppermute | solution.py:34
  64.6 4.8 %collective-permute-start.29 = (f32[128,128]{1,0:T(8,128)S(1)}, f32[128,128]{1,0:T(8,128)S(1)}, u32[]{:S(2)}, u32[]{:S(2)}) collective-permute-start(f32[128,128]{1,0:T(8,128)S(1)} %add.308), channel_id=1, source_target_pairs={{0,8},{1,17},{2,10},{3,19},{4,12},{5,21},{6,14},{7,23},{8,0},{9,25... | collective-permute-start | bytes 196616 | tf_op jit(solution)/shard_map/ppermute | solution.py:34
  67.8 4.3 %collective-permute-start.25 = (f32[128,128]{1,0:T(8,128)S(1)}, f32[128,128]{1,0:T(8,128)S(1)}, u32[]{:S(2)}, u32[]{:S(2)}) collective-permute-start(f32[128,128]{1,0:T(8,128)S(1)} %add.304), channel_id=1, source_target_pairs={{0,4},{1,3},{2,6},{3,1},{4,0},{5,7},{6,2},{7,5},{8,12},{9,11},{10,... | collective-permute-start | bytes 196616 | tf_op jit(solution)/shard_map/ppermute | solution.py:34
  69.4 6.3 %collective-permute-start.30 = (f32[128,128]{1,0:T(8,128)S(1)}, f32[128,128]{1,0:T(8,128)S(1)}, u32[]{:S(2)}, u32[]{:S(2)}) collective-permute-start(f32[128,128]{1,0:T(8,128)S(1)} %add.309), channel_id=1, source_target_pairs={{0,16},{1,9},{2,18},{3,11},{4,20},{5,13},{6,22},{7,15},{8,24},{9,1... | collective-permute-start | bytes 196616 | tf_op jit(solution)/shard_map/ppermute | solution.py:34
  72.1 5.2 %collective-permute-start.26 = (f32[128,128]{1,0:T(8,128)S(1)}, f32[128,128]{1,0:T(8,128)S(1)}, u32[]{:S(2)}, u32[]{:S(2)}) collective-permute-start(f32[128,128]{1,0:T(8,128)S(1)} %add.305), channel_id=1, source_target_pairs={{0,8},{1,17},{2,10},{3,19},{4,12},{5,21},{6,14},{7,23},{8,0},{9,25... | collective-permute-start | bytes 196616 | tf_op jit(solution)/shard_map/ppermute | solution.py:34
  75.8 4.3 %collective-permute-start.31 = (f32[128,128]{1,0:T(8,128)S(1)}, f32[128,128]{1,0:T(8,128)S(1)}, u32[]{:S(2)}, u32[]{:S(2)}) collective-permute-start(f32[128,128]{1,0:T(8,128)S(1)} %add.310), channel_id=1, source_target_pairs={{0,2},{1,5},{2,0},{3,7},{4,6},{5,1},{6,4},{7,3},{8,10},{9,13},{10,... | collective-permute-start | bytes 196616 | tf_op jit(solution)/shard_map/ppermute | solution.py:34
  77.3 5.2 %collective-permute-start.27 = (f32[128,128]{1,0:T(8,128)S(1)}, f32[128,128]{1,0:T(8,128)S(1)}, u32[]{:S(2)}, u32[]{:S(2)}) collective-permute-start(f32[128,128]{1,0:T(8,128)S(1)} %add.306), channel_id=1, source_target_pairs={{0,16},{1,9},{2,18},{3,11},{4,20},{5,13},{6,22},{7,15},{8,24},{9,1... | collective-permute-start | bytes 196616 | tf_op jit(solution)/shard_map/ppermute | solution.py:34
  80.1 4.3 %collective-permute-start.32 = (f32[128,128]{1,0:T(8,128)S(1)}, f32[128,128]{1,0:T(8,128)S(1)}, u32[]{:S(2)}, u32[]{:S(2)}) collective-permute-start(f32[128,128]{1,0:T(8,128)S(1)} %add.311), channel_id=1, source_target_pairs={{0,4},{1,3},{2,6},{3,1},{4,0},{5,7},{6,2},{7,5},{8,12},{9,11},{10,... | collective-permute-start | bytes 196616 | tf_op jit(solution)/shard_map/ppermute | solution.py:34
  89.1 3.6 %collective-permute-start.36 = (f32[2,40]{1,0:T(2,128)S(1)}, f32[2,40]{1,0:T(2,128)S(1)}, u32[]{:S(2)}, u32[]{:S(2)}) collective-permute-start(f32[2,40]{1,0:T(2,128)S(1)} %add.313), channel_id=1, source_target_pairs={{0,2},{1,5},{2,0},{3,7},{4,6},{5,1},{6,4},{7,3},{8,10},{9,13},{10,... | collective-permute-start | bytes 968 | tf_op jit(solution)/shard_map/ppermute | solution.py:34
  92.6 3.6 %collective-permute-start.37 = (f32[2,40]{1,0:T(2,128)S(1)}, f32[2,40]{1,0:T(2,128)S(1)}, u32[]{:S(2)}, u32[]{:S(2)}) collective-permute-start(f32[2,40]{1,0:T(2,128)S(1)} %add.314), channel_id=1, source_target_pairs={{0,4},{1,3},{2,6},{3,1},{4,0},{5,7},{6,2},{7,5},{8,12},{9,11},{10,... | collective-permute-start | bytes 968 | tf_op jit(solution)/shard_map/ppermute | solution.py:34
  96.2 3.6 %collective-permute-start.38 = (f32[2,40]{1,0:T(2,128)S(1)}, f32[2,40]{1,0:T(2,128)S(1)}, u32[]{:S(2)}, u32[]{:S(2)}) collective-permute-start(f32[2,40]{1,0:T(2,128)S(1)} %add.315), channel_id=1, source_target_pairs={{0,8},{1,17},{2,10},{3,19},{4,12},{5,21},{6,14},{7,23},{8,0},{9,25... | collective-permute-start | bytes 968 | tf_op jit(solution)/shard_map/ppermute | solution.py:34
  99.8 4.5 %collective-permute-start.39 = (f32[2,40]{1,0:T(2,128)S(1)}, f32[2,40]{1,0:T(2,128)S(1)}, u32[]{:S(2)}, u32[]{:S(2)}) collective-permute-start(f32[2,40]{1,0:T(2,128)S(1)} %add.316), channel_id=1, source_target_pairs={{0,16},{1,9},{2,18},{3,11},{4,20},{5,13},{6,22},{7,15},{8,24},{9,1... | collective-permute-start | bytes 968 | tf_op jit(solution)/shard_map/ppermute | solution.py:34
  (15 other events, 22.1 us)

commit v3 on v2

v3 whole, which is shorter than its diff:
```python
import jax
import jax.numpy as jnp
from jax import lax
from jax.experimental import pallas as pl
from jax.experimental.pallas import tpu as pltpu
from jax.sharding import PartitionSpec as P

TEMPL = 40
PENALTY = 1.0
LEARN_RATE = 2.0
GROUP = 8
LIMIT = 8 * 1024 * 1024
UNROLL = 8
VMEM = pltpu.VMEM
SMEM = pltpu.SMEM


def swap_cores(value):
    return lax.ppermute(value, "grp", [(0, 1), (1, 0)])


def deal(parts, axes="blk"):
    return lax.all_to_all(parts, axes, 0, 0, tiled=True)


def tell(own, count, meanwhile=()):
    mine = deal(jnp.broadcast_to(own[None], (count,) + own.shape)).reshape(-1, own.shape[1])
    if meanwhile:
        mine, meanwhile = lax.optimization_barrier((mine, meanwhile))
    gathered = jnp.concatenate([mine, swap_cores(mine)], axis=0)
    return (gathered,) + meanwhile if meanwhile else gathered


def collect(keep, send, count):
    parts = keep + swap_cores(send)
    return jnp.sum(deal(parts.reshape((count, -1) + parts.shape[1:])), axis=0)


def row_of(row, height, width):
    return jnp.broadcast_to(row, (height, width))


def load_windows(place_ref, field_ref, window_ref, tiles, list_len, shift=0):
    @pl.loop(0, tiles // GROUP, unroll=UNROLL)
    def _(group):
        base = pl.multiple_of(group * GROUP, GROUP)
        for i in range(GROUP):
            for k in range(list_len):
                spot = place_ref[(base + i) * list_len + k] + shift
                window_ref[k, pl.ds(base + i, 1), :] = field_ref[pl.ds(spot, 1), :]


def fetch_rows(window_ref, rows, slot, list_len, width):
    lane = slot & (width - 1)
    which = slot // width
    result = jnp.zeros(slot.shape, jnp.float32)
    for k in range(list_len):
        taken = jnp.take_along_axis(window_ref[k, rows, :], lane, axis=1, mode="promise_in_bounds")
        result = jnp.where(which == k, taken, result)
    return result


def split_three(value):
    first = value.astype(jnp.bfloat16).astype(jnp.float32)
    rest = value - first
    second = rest.astype(jnp.bfloat16).astype(jnp.float32)
    return first, second, rest - second


def scatter_tile(place_ref, sum_ref, beside, tile, lows, tops, values, list_len, width):
    narrow = width // 2
    height = 2 * list_len
    row = lax.broadcasted_iota(jnp.int32, (height, width), 0)
    spot = lax.broadcasted_iota(jnp.int32, (narrow, width), 0)
    hot, left = [], []
    for low, top, parts in zip(lows, tops, values):
        hot.append((row_of(low, narrow, width) == spot).astype(jnp.float32).astype(jnp.bfloat16))
        here = row_of(top, height, width) == row
        left.append(
            jnp.concatenate(
                [jnp.where(here, row_of(part, height, width), 0.0) for part in parts], axis=0
            ).astype(jnp.bfloat16)
        )
    summed = lax.dot_general(
        jnp.concatenate(left, axis=1),
        jnp.concatenate(hot, axis=1),
        (((1,), (1,)), ((), ())),
        preferred_element_type=jnp.float32,
    )
    bands = [summed[j * height : (j + 1) * height] for j in range(len(values[0]))]
    spots = [place_ref[tile * list_len + k] for k in range(list_len)]
    totals = [(0, bands[0] + bands[1] + bands[2])]
    if beside:
        totals.append((beside, bands[3]))
    for shift, total in totals:
        total = jnp.concatenate([total[:list_len], total[list_len:]], axis=1)
        olds = [sum_ref[pl.ds(at + shift, 1), :] for at in spots]
        for k, at in enumerate(spots):
            sum_ref[pl.ds(at + shift, 1), :] = olds[k] + total[k : k + 1]


def slot_parts(slot, list_len, width):
    narrow = width // 2
    low = slot & (narrow - 1)
    top = ((slot & (width - 1)) // narrow) * list_len + slot // width
    return low, jnp.where(slot < list_len * width, top, 2 * list_len)


def sweep_kernel(*refs, list_len, beside):
    first = beside > 0
    if first:
        (place_ref, field_ref, slot_ref, coef_ref, off_ref, dual_ref, temp_ref, weight_ref,
         moved_ref, keep_ref, send_ref, sum_ref, window_ref) = refs
    else:
        (place_ref, field_ref, slot_ref, coef_ref, off_ref, dual_ref, temp_ref, weight_ref,
         old_ref, moved_ref, next_ref, keep_ref, send_ref, sum_ref, window_ref) = refs
    arity, tiles, width = slot_ref.shape
    templates = weight_ref.shape[1]
    load_windows(place_ref, field_ref, window_ref, tiles, list_len)
    sum_ref[...] = jnp.zeros_like(sum_ref)
    one = jnp.ones((GROUP, width), jnp.float32)

    @pl.loop(0, tiles // GROUP, unroll=UNROLL)
    def _(group):
        base = pl.multiple_of(group * GROUP, GROUP)
        rows = pl.ds(base, GROUP)
        templ = temp_ref[rows, :]
        hot = row_of(templ, GROUP, templates) == lax.broadcasted_iota(
            jnp.int32, (GROUP, templates), 1
        )
        weight = jnp.sum(
            jnp.where(hot, row_of(weight_ref[...], GROUP, templates), 0.0), axis=1, keepdims=True
        )
        weight = jnp.broadcast_to(weight, (GROUP, width))
        squared = jnp.broadcast_to(templ % 2 == 1, (GROUP, width))
        slots = [slot_ref[s, rows, :] for s in range(arity)]
        used = [q < list_len * width for q in slots]
        acts = [jnp.where(used[s], coef_ref[s, rows, :], 0.0) for s in range(arity)]
        copies = [fetch_rows(window_ref, rows, q, list_len, width) for q in slots]
        duals = [dual_ref[s, rows, :] for s in range(arity)]
        if not first:
            duals = [
                d + jnp.where(m, old_ref[s, rows, :] - c, 0.0)
                for s, (d, m, c) in enumerate(zip(duals, used, copies))
            ]
            for s in range(arity):
                next_ref[s, rows, :] = duals[s]
        shifted = [c - d for c, d in zip(copies, duals)]
        linear = sum(a * v for a, v in zip(acts, shifted)) + off_ref[rows, :]
        norm = sum(a * a for a in acts)
        plain = jnp.clip(linear / norm, 0.0, weight / PENALTY)
        square = 2.0 * weight * jnp.maximum(linear, 0.0) / (PENALTY + 2.0 * weight * norm)
        chosen = jnp.where(squared, square, plain)
        parts = []
        for s in range(arity):
            moved = shifted[s] - chosen * acts[s]
            moved_ref[s, rows, :] = moved
            pieces = split_three(jnp.where(used[s], moved + duals[s], 0.0))
            parts.append(pieces + (one,) if first else pieces)
        halves = [slot_parts(q, list_len, width) for q in slots]
        for i in range(GROUP):
            scatter_tile(
                place_ref,
                sum_ref,
                beside,
                base + i,
                [h[0][i : i + 1] for h in halves],
                [h[1][i : i + 1] for h in halves],
                [tuple(p[i : i + 1] for p in part) for part in parts],
                list_len,
                width,
            )

    half = keep_ref.shape[0]
    keep_ref[...] = sum_ref[:half]
    send_ref[...] = sum_ref[half:]


def energy_kernel(*refs, list_len, beside):
    (place_ref, first_ref, own_ref, field_ref, start_ref, slot_ref, coef_ref, off_ref, dual_ref,
     temp_ref, weight_ref, old_ref, energy_ref, next_ref, owned_ref, window_ref, other_ref) = refs
    arity, tiles, width = slot_ref.shape
    templates = weight_ref.shape[1]
    piece = owned_ref.shape[0] // 2
    for h in range(2):
        start = pl.multiple_of(own_ref[h], GROUP)
        owned_ref[h * piece : (h + 1) * piece] = field_ref[pl.ds(start, piece), :]
    load_windows(place_ref, field_ref, window_ref, tiles, list_len)
    load_windows(first_ref, start_ref, other_ref, tiles, list_len, beside)

    def step(group, totals):
        base = pl.multiple_of(group * GROUP, GROUP)
        rows = pl.ds(base, GROUP)
        templ = temp_ref[rows, :]
        hot = row_of(templ, GROUP, templates) == lax.broadcasted_iota(
            jnp.int32, (GROUP, templates), 1
        )
        squared = jnp.broadcast_to(templ % 2 == 1, (GROUP, width))
        lines = [off_ref[rows, :]] * 2
        for s in range(arity):
            slot = slot_ref[s, rows, :]
            used = slot < list_len * width
            act = jnp.where(used, coef_ref[s, rows, :], 0.0)
            copies = [
                fetch_rows(ref, rows, slot, list_len, width) for ref in (window_ref, other_ref)
            ]
            lines = [line + act * copy for line, copy in zip(lines, copies)]
            next_ref[s, rows, :] = dual_ref[s, rows, :] + jnp.where(
                used, old_ref[s, rows, :] - copies[0], 0.0
            )
        results = []
        for total, line in zip(totals, lines):
            positive = jnp.maximum(line, 0.0)
            rule = jnp.where(squared, positive * positive, positive)
            tile = jnp.sum(rule, axis=1, keepdims=True)
            results.append(
                total + jnp.where(hot, jnp.broadcast_to(tile, (GROUP, templates)), 0.0)
            )
        return tuple(results)

    zero = jnp.zeros((GROUP, templates), jnp.float32)
    totals = lax.fori_loop(0, tiles // GROUP, step, (zero, zero), unroll=UNROLL)
    energy_ref[...] = jnp.concatenate(
        [jnp.sum(total, axis=0, keepdims=True) for total in totals], axis=1
    )


def specs(count, scalars):
    return [pl.BlockSpec(memory_space=SMEM)] * scalars + [
        pl.BlockSpec(memory_space=VMEM)
    ] * (count - scalars)


def call(body, args, scalars, outs, scratch, work):
    shapes = tuple(jax.ShapeDtypeStruct(s, jnp.float32) for s in outs)
    return pl.pallas_call(
        body,
        out_shape=shapes,
        in_specs=specs(len(args), scalars),
        out_specs=tuple(specs(len(outs), 0)),
        scratch_shapes=[VMEM(s, jnp.float32) for s in scratch],
        compiler_params=pltpu.CompilerParams(vmem_limit_bytes=LIMIT),
        cost_estimate=pl.CostEstimate(flops=0, bytes_accessed=work, transcendentals=0),
    )(*args)


def local(
    atom_value,
    target_value,
    observed,
    block_owner,
    block_local,
    slot_index,
    coefficient,
    offset,
    dual_value,
    template,
    weight,
):
    device = lax.axis_index("blk")
    count = lax.axis_size("blk")
    core = lax.axis_index("grp")
    groups = lax.axis_size("grp")
    atom_blk, width = atom_value.shape
    tiles = template.shape[1]
    list_len = block_owner.shape[1]
    arity = slot_index.shape[0]
    devices = count * groups
    piece = atom_blk // groups
    half = count * piece
    start = device * tiles
    owner = lax.dynamic_slice_in_dim(block_owner, start, tiles, 0)
    spot = lax.dynamic_slice_in_dim(block_local, start, tiles, 0)

    def place_of(owner, spot, stride):
        part = spot // piece
        return (part ^ core) * (count * stride) + owner * stride + spot % piece

    place_first = place_of(owner, spot, 2 * piece).reshape(-1)
    place = place_of(owner, spot, piece).reshape(-1)
    own = place_of(device, jnp.arange(2, dtype=jnp.int32) * piece, piece)
    slots = slot_index.reshape(arity, tiles, width)
    coeffs = coefficient.reshape(arity, tiles, width)
    offsets = offset.reshape(tiles, width)
    duals = dual_value.reshape(arity, tiles, width)
    templates = (core * (TEMPL // groups) + template[0])[:, None]
    weights = weight[None, :]
    rule = (arity, tiles, width)
    window = (list_len, tiles, width)

    def share(field):
        return lax.dynamic_slice_in_dim(field, core * piece, piece, 0)

    mine, fixed = share(atom_value), share(observed)
    start_fields, *early = tell(
        jnp.concatenate([mine, share(target_value)], axis=0),
        count,
        (place_first, place, own, fixed, templates, slots, coeffs, offsets, duals),
    )
    place_first, place, own, fixed, templates, slots, coeffs, offsets, duals = early
    moved, keep, send = call(
        lambda *r: sweep_kernel(*r, list_len=list_len, beside=piece),
        (place_first, start_fields, slots, coeffs, offsets, duals, templates, weights),
        1,
        (rule, (2 * half, width), (2 * half, width)),
        ((4 * half, width), window),
        15_000_000,
    )
    sums = collect(keep, send, count)
    counted = sums[piece:] + 1.0

    def refresh(sums, before):
        stepped = jnp.clip((sums + before) / counted, 0.0, 1.0)
        return jnp.where(fixed == 1, before, stepped)

    mine = refresh(sums[:piece], mine)
    values = tell(mine, count)
    moved, duals, keep, send = call(
        lambda *r: sweep_kernel(*r, list_len=list_len, beside=0),
        (place, values, slots, coeffs, offsets, duals, templates, weights, moved),
        1,
        (rule, rule, (half, width), (half, width)),
        ((2 * half, width), window),
        15_000_000,
    )
    values = tell(refresh(collect(keep, send, count), mine), count)
    energies, dual_next, consensus = call(
        lambda *r: energy_kernel(*r, list_len=list_len, beside=piece),
        (place, place_first, own, values, start_fields, slots, coeffs, offsets, duals, templates,
         weights, moved),
        3,
        ((1, 2 * TEMPL), rule, (atom_blk, width)),
        (window, window),
        10_000_000,
    )
    energies = deal(jnp.broadcast_to(energies[None], (devices, 1, 2 * TEMPL)), ("blk", "grp"))
    energies = jnp.sum(energies, axis=(0, 1))
    e_value, e_target = energies[:TEMPL], energies[TEMPL:]
    weight_next = weight * jnp.exp(-LEARN_RATE * (e_value - e_target) / (e_value + e_target + 1.0))
    return consensus, dual_next.reshape(dual_value.shape), weight_next


def solution(mesh):
    in_specs = (
        P("blk", None),
        P("blk", None),
        P("blk", None),
        P(),
        P(),
        P(None, "grp", "blk"),
        P(None, "grp", "blk"),
        P("grp", "blk"),
        P(None, "grp", "blk"),
        P("grp", "blk"),
        P(),
    )
    out_specs = (P("blk", None), P(None, "grp", "blk"), P())
    return jax.shard_map(local, mesh=mesh, in_specs=in_specs, out_specs=out_specs, check_vma=False)
```

time: 105 us -> 90.9 us (0.87)
  blocking collectives: 0 us -> 54.8 us
  waiting for transfers between devices: 55.8 us -> 14.6 us
  starting transfers between devices: 34.7 us -> 8.76 us
  Pallas kernels: 8.27 us -> 6.39 us
    all_to_all x0 -> x5, blocking collectives: none -> 54.8 us  [deal(): return lax.all_to_all(parts, axes, 0, 0, tiled=True)]
    ppermute x28 -> x0, waiting for transfers between devices: 50.6 us -> none  [exchange(): return lax.ppermute(value, ('blk', 'grp'), perm)]
    ppermute x28 -> x0, starting transfers between devices: 30.3 us -> none  [exchange(): return lax.ppermute(value, ('blk', 'grp'), perm)]
    all_to_all x0 -> x1, starting transfers between devices: none -> 8.34 us  [deal(): return lax.all_to_all(parts, axes, 0, 0, tiled=True)]
    all_to_all x0 -> x1, waiting for transfers between devices: none -> 7.97 us  [deal(): return lax.all_to_all(parts, axes, 0, 0, tiled=True)]
    ppermute x12 -> x5, starting transfers between devices: 4.41 us -> 0.42 us  [swap_cores(): return lax.ppermute(value, 'grp', [(0, 1), (1, 0)])]
    pallas_call x4 -> x3, Pallas kernels: 8.27 us -> 6.39 us  [call(): pl.pallas_call(body, out_shape=shapes, in_specs=specs(len(args), scalars)...]
    ppermute x12 -> x5, waiting for transfers between devices: 5.21 us -> 6.66 us  [swap_cores(): return lax.ppermute(value, 'grp', [(0, 1), (1, 0)])]
  transfers between devices with their start and end apart: 40 -> 6, of which waited for: 25 -> 6; matrix products, arithmetic and copies ran while one was open for 1% -> 1% of each run, Pallas kernels for 2% -> 0%
where the time goes in v3:
time: 90.9 us; the launch traced here: 90.4 us
  blocking collectives  54.8 us (60%)
  waiting for transfers between devices  14.6 us (16%)
  starting transfers between devices  8.76 us (10%)
  Pallas kernels  6.39 us (7%)
  local copies, waits for them, and re-layouts  3.31 us (4%)
  other arithmetic  1.58 us (2%)
    all_to_all x5, blocking collectives, deal(): return lax.all_to_all(parts, axes, 0, 0, tiled=True)  54.8 us
    all_to_all x1, starting transfers between devices, deal(): return lax.all_to_all(parts, axes, 0, 0, tiled=True)  8.34 us
    all_to_all x1, waiting for transfers between devices, deal(): return lax.all_to_all(parts, axes, 0, 0, tiled=True)  7.97 us
    ppermute x5, waiting for transfers between devices, swap_cores(): return lax.ppermute(value, 'grp', [(0, 1), (1, 0)])  6.66 us
    pallas_call x3, Pallas kernels, call(): pl.pallas_call(body, out_shape=shapes, in_specs=specs(len(args), scalars)...  6.39 us
  transfers between devices with their start and end apart: 6, of which 6 were waited for; matrix products, arithmetic and copies ran while one was open for 1% of the time, Pallas kernels for 0%

profile of v3, /device:TPU:0, one launch (start us, length us, event | category | flops | bytes accessed | tf_op | source)
XLA Modules:
  0.0 90.4 jit_solution(3504551893608602320)
XLA Ops:
  0.6 0.0 copy-start
  0.7 0.7 constant_dynamic-slice_fusion.1
  1.4 0.7 broadcast_in_dim.12
  2.1 8.3 %all-to-all-start = ((f32[16,32,128]{2,1,0:T(8,128)}), f32[16,32,128]{2,1,0:T(8,128)S(1)}, u32[]{:S(2)}, u32[]{:S(2)}) async-start(f32[16,32,128]{2,1,0:T(8,128)} %broadcast_in_dim.12), calls=%async_computation | async-start | bytes 524288 | tf_op jit(solution)/shard_map/all_to_all | solution.py:23
  10.5 0.8 add_add_fusion
  11.3 0.1 copy.31
  11.4 0.1 reshape.62.r_0_
  11.5 0.1 copy.30
  11.6 0.1 reshape.61.r_0_.r_1_
  11.7 0.0 copy-start.6
  11.7 0.6 copy-done.6
  12.4 8.0 %all-to-all-done = f32[16,32,128]{2,1,0:T(8,128)S(1)} async-done(((f32[16,32,128]{2,1,0:T(8,128)}), f32[16,32,128]{2,1,0:T(8,128)S(1)}, u32[]{:S(2)}, u32[]{:S(2)}) %all-to-all-start) | async-done | bytes 262176 | tf_op jit(solution)/shard_map/all_to_all | solution.py:23
  20.3 0.1 copy.32.r_6_.r_9_
  20.5 0.0 copy-start.1
  20.5 0.0 copy-start.2
  20.5 1.4 %collective-permute-done = f32[512,128]{1,0:T(8,128)S(1)} collective-permute-done((f32[512,128]{1,0:T(8,128)S(1)}, f32[512,128]{1,0:T(8,128)S(1)}, u32[]{:S(2)}, u32[]{:S(2)}) %collective-permute-start) | collective-permute-done | bytes 262176 | tf_op jit(solution)/shard_map/ppermute | solution.py:19
  21.9 0.6 copy-done.5
  22.5 2.1 %shard_map.130 = (f32[3,64,128]{2,1,0:T(8,128)S(1)}, f32[512,128]{1,0:T(8,128)S(1)}, f32[512,128]{1,0:T(8,128)S(1)}) custom-call(s32[256]{0:T(256)S(1)} %reshape.61.r_0_.r_1_, f32[1024,128]{1,0:T(8,128)S(1)} %constant_dynamic-update-slice_fusion.r_1_.r_4_, s32[3,64,128]{2,1,0:T(8,128)S(1)} %bitcast.15, f32[3,64,128]{2,1,0:T(8,128)S(1)} %bitcast.18, ...), custom_call_target="tpu_custom_call" | custom-call | bytes 15000000 | tf_op jit(solution)/shard_map/pallas_call | solution.py:236
  24.7 0.2 collective-permute-start.1
  24.9 1.4 %collective-permute-done.1 = f32[512,128]{1,0:T(8,128)S(1)} collective-permute-done((f32[512,128]{1,0:T(8,128)S(1)}, f32[512,128]{1,0:T(8,128)S(1)}, u32[]{:S(2)}, u32[]{:S(2)}) %collective-permute-start.1) | collective-permute-done | bytes 262176 | tf_op jit(solution)/shard_map/ppermute | solution.py:19
  26.3 13.5 %all_to_all.30 = f32[16,32,128]{2,1,0:T(8,128)S(1)} all-to-all(f32[16,32,128]{2,1,0:T(8,128)S(1)} %bitcast.30), channel_id=1, replica_groups=mesh['blk'=16,'grp'=2] {'blk'}, dimensions={0} | all-to-all | bytes 524288 | tf_op jit(solution)/shard_map/all_to_all | solution.py:23
  39.9 11.1 %all_to_all.31 = f32[16,16,128]{2,1,0:T(8,128)S(1)} all-to-all(f32[16,16,128]{2,1,0:T(8,128)S(1)} %broadcast_in_dim.14), channel_id=1, replica_groups=mesh['blk'=16,'grp'=2] {'blk'}, dimensions={0} | all-to-all | bytes 262144 | tf_op jit(solution)/shard_map/all_to_all | solution.py:23
  51.0 1.3 %collective-permute-done.2 = f32[256,128]{1,0:T(8,128)S(1)} collective-permute-done((f32[256,128]{1,0:T(8,128)S(1)}, f32[256,128]{1,0:T(8,128)S(1)}, u32[]{:S(2)}, u32[]{:S(2)}) %collective-permute-start.2) | collective-permute-done | bytes 131104 | tf_op jit(solution)/shard_map/ppermute | solution.py:19
  52.4 2.1 %shard_map.131 = (f32[3,64,128]{2,1,0:T(8,128)S(1)}, f32[3,64,128]{2,1,0:T(8,128)S(1)}, f32[256,128]{1,0:T(8,128)S(1)}, f32[256,128]{1,0:T(8,128)S(1)}) custom-call(s32[256]{0:T(256)S(1)} %reshape.62.r_0_, f32[512,128]{1,0:T(8,128)S(1)} %pad_maximum_fusion.r_1_, s32[3,64,128]{2,1,0:T(8,128)S(1)} %bitcast.16, f32[3,64,128]{2,1,0:T(8,128)S(1)} %bitcast.19, ...), custom_call_target="tpu_custom_call" | custom-call | bytes 15000000 | tf_op jit(solution)/shard_map/pallas_call | solution.py:236
  54.5 0.2 collective-permute-start.3
  54.7 1.2 %collective-permute-done.3 = f32[256,128]{1,0:T(8,128)S(1)} collective-permute-done((f32[256,128]{1,0:T(8,128)S(1)}, f32[256,128]{1,0:T(8,128)S(1)}, u32[]{:S(2)}, u32[]{:S(2)}) %collective-permute-start.3) | collective-permute-done | bytes 131104 | tf_op jit(solution)/shard_map/ppermute | solution.py:19
  56.0 10.6 %all_to_all.32 = f32[16,16,128]{2,1,0:T(8,128)S(1)} all-to-all(f32[16,16,128]{2,1,0:T(8,128)S(1)} %bitcast.33), channel_id=1, replica_groups=mesh['blk'=16,'grp'=2] {'blk'}, dimensions={0} | all-to-all | bytes 262144 | tf_op jit(solution)/shard_map/all_to_all | solution.py:23
  66.6 10.7 %all_to_all.33 = f32[16,16,128]{2,1,0:T(8,128)S(1)} all-to-all(f32[16,16,128]{2,1,0:T(8,128)S(1)} %broadcast_in_dim.15), channel_id=1, replica_groups=mesh['blk'=16,'grp'=2] {'blk'}, dimensions={0} | all-to-all | bytes 262144 | tf_op jit(solution)/shard_map/all_to_all | solution.py:23
  77.3 1.3 %collective-permute-done.4 = f32[256,128]{1,0:T(8,128)S(1)} collective-permute-done((f32[256,128]{1,0:T(8,128)S(1)}, f32[256,128]{1,0:T(8,128)S(1)}, u32[]{:S(2)}, u32[]{:S(2)}) %collective-permute-start.4) | collective-permute-done | bytes 131104 | tf_op jit(solution)/shard_map/ppermute | solution.py:19
  78.7 2.1 %shard_map.132 = (f32[1,80]{1,0:T(1,128)S(1)}, f32[3,64,128]{2,1,0:T(8,128)}, f32[32,128]{1,0:T(8,128)}) custom-call(s32[256]{0:T(256)S(1)} %reshape.62.r_0_, s32[256]{0:T(256)S(1)} %reshape.61.r_0_.r_1_, s32[2]{0:T(128)S(1)} %fusion.5.r_2_, f32[512,128]{1,0:T(8,128)S(1)} %pad_maximum_fusion.1.r_3_, ...), custom_call_target="tpu_custom_call" | custom-call | bytes 10000000 | tf_op jit(solution)/shard_map/pallas_call | solution.py:236
  80.9 8.9 %all_to_all.34 = f32[32,1,80]{2,1,0:T(1,128)S(1)} all-to-all(f32[32,1,80]{2,1,0:T(1,128)S(1)} %broadcast_in_dim.17), channel_id=1, replica_groups=mesh['blk'=16,'grp'=2] {'blk','grp'}, dimensions={0} | all-to-all | bytes 20480 | tf_op jit(solution)/shard_map/all_to_all | solution.py:23
  89.8 0.6 exponential_multiply_fusion
  (29 shorter events, 0.3 us)
Async XLA Ops:
  0.6 11.1 %copy-start = (s32[32,128]{1,0:T(8,128)S(1)}, s32[32,128]{1,0:T(8,128)}, u32[]{:S(2)}) copy-start(s32[32,128]{1,0:T(8,128)} %param.13) | copy-start | bytes 49156
  2.1 18.2 %all-to-all-start = ((f32[16,32,128]{2,1,0:T(8,128)}), f32[16,32,128]{2,1,0:T(8,128)S(1)}, u32[]{:S(2)}, u32[]{:S(2)}) async-start(f32[16,32,128]{2,1,0:T(8,128)} %broadcast_in_dim.12), calls=%async_computation | async-start | bytes 524288 | tf_op jit(solution)/shard_map/all_to_all | solution.py:23
  11.7 0.7 copy-start.6
  20.3 1.5 %collective-permute-start = (f32[512,128]{1,0:T(8,128)S(1)}, f32[512,128]{1,0:T(8,128)S(1)}, u32[]{:S(2)}, u32[]{:S(2)}) collective-permute-start(f32[512,128]{1,0:T(8,128)S(1)} %bitcast.31), channel_id=1, source_target_pairs={{0,1},{1,0},{2,3},{3,2},{4,5},{5,4},{6,7},{7,6},{8,9},{9,8},{10,11... | collective-permute-start | bytes 786440 | tf_op jit(solution)/shard_map/ppermute | solution.py:19
  20.5 1.5 %copy-start.1 = (s32[3,1,8192]{2,1,0:T(1,128)S(1)}, s32[3,1,8192]{2,1,0:T(1,128)}, u32[]{:S(2)}) copy-start(s32[3,1,8192]{2,1,0:T(1,128)} %param.16) | copy-start | bytes 294916
  20.5 1.4 %copy-start.2 = (f32[3,1,8192]{2,1,0:T(1,128)S(1)}, f32[3,1,8192]{2,1,0:T(1,128)}, u32[]{:S(2)}) copy-start(f32[3,1,8192]{2,1,0:T(1,128)} %param.17) | copy-start | bytes 294916
  20.5 1.4 %copy-start.3 = (f32[3,1,8192]{2,1,0:T(1,128)S(1)}, f32[3,1,8192]{2,1,0:T(1,128)}, u32[]{:S(2)}) copy-start(f32[3,1,8192]{2,1,0:T(1,128)} %param.19) | copy-start | bytes 294916
  20.5 1.4 %copy-start.4 = (f32[1,8192]{1,0:T(1,128)S(1)}, f32[1,8192]{1,0:T(1,128)}, u32[]{:S(2)}) copy-start(f32[1,8192]{1,0:T(1,128)} %param.18) | copy-start | bytes 98308
  21.9 0.7 copy-start.5
  24.7 1.6 %collective-permute-start.1 = (f32[512,128]{1,0:T(8,128)S(1)}, f32[512,128]{1,0:T(8,128)S(1)}, u32[]{:S(2)}, u32[]{:S(2)}) collective-permute-start(f32[512,128]{1,0:T(8,128)S(1)} %get-tuple-element.34), channel_id=1, source_target_pairs={{0,1},{1,0},{2,3},{3,2},{4,5},{5,4},{6,7},{7,6},{8,9},{9,8},{10,11... | collective-permute-start | bytes 786440 | tf_op jit(solution)/shard_map/ppermute | solution.py:19
  51.0 1.3 %collective-permute-start.2 = (f32[256,128]{1,0:T(8,128)S(1)}, f32[256,128]{1,0:T(8,128)S(1)}, u32[]{:S(2)}, u32[]{:S(2)}) collective-permute-start(f32[256,128]{1,0:T(8,128)S(1)} %bitcast.34), channel_id=1, source_target_pairs={{0,1},{1,0},{2,3},{3,2},{4,5},{5,4},{6,7},{7,6},{8,9},{9,8},{10,11... | collective-permute-start | bytes 393224 | tf_op jit(solution)/shard_map/ppermute | solution.py:19
  54.5 1.4 %collective-permute-start.3 = (f32[256,128]{1,0:T(8,128)S(1)}, f32[256,128]{1,0:T(8,128)S(1)}, u32[]{:S(2)}, u32[]{:S(2)}) collective-permute-start(f32[256,128]{1,0:T(8,128)S(1)} %get-tuple-element.37), channel_id=1, source_target_pairs={{0,1},{1,0},{2,3},{3,2},{4,5},{5,4},{6,7},{7,6},{8,9},{9,8},{10,11... | collective-permute-start | bytes 393224 | tf_op jit(solution)/shard_map/ppermute | solution.py:19
  77.3 1.3 %collective-permute-start.4 = (f32[256,128]{1,0:T(8,128)S(1)}, f32[256,128]{1,0:T(8,128)S(1)}, u32[]{:S(2)}, u32[]{:S(2)}) collective-permute-start(f32[256,128]{1,0:T(8,128)S(1)} %bitcast.36), channel_id=1, source_target_pairs={{0,1},{1,0},{2,3},{3,2},{4,5},{5,4},{6,7},{7,6},{8,9},{9,8},{10,11... | collective-permute-start | bytes 393224 | tf_op jit(solution)/shard_map/ppermute | solution.py:19

commit v4 on v3

--- a/solution.py
+++ b/solution.py
@@ -19,12 +19,12 @@
     return lax.ppermute(value, "grp", [(0, 1), (1, 0)])
 
 
-def deal(parts, axes="blk"):
-    return lax.all_to_all(parts, axes, 0, 0, tiled=True)
-
-
-def tell(own, count, meanwhile=()):
-    mine = deal(jnp.broadcast_to(own[None], (count,) + own.shape)).reshape(-1, own.shape[1])
+def deal(parts):
+    return lax.all_to_all(parts, ("blk", "grp"), 0, 0, tiled=True)
+
+
+def tell(own, meanwhile=()):
+    mine = deal(own).reshape(-1, own.shape[-1])
     if meanwhile:
         mine, meanwhile = lax.optimization_barrier((mine, meanwhile))
     gathered = jnp.concatenate([mine, swap_cores(mine)], axis=0)
@@ -33,21 +33,23 @@
 
 def collect(keep, send, count):
     parts = keep + swap_cores(send)
-    return jnp.sum(deal(parts.reshape((count, -1) + parts.shape[1:])), axis=0)
+    width = parts.shape[1]
+    return jnp.sum(deal(parts.reshape(2 * count, -1, width)).reshape(count, -1, width), axis=0)
 
 
 def row_of(row, height, width):
     return jnp.broadcast_to(row, (height, width))
 
 
-def load_windows(place_ref, field_ref, window_ref, tiles, list_len, shift=0):
+def load_windows(place_ref, field_ref, windows, tiles, list_len):
     @pl.loop(0, tiles // GROUP, unroll=UNROLL)
     def _(group):
         base = pl.multiple_of(group * GROUP, GROUP)
         for i in range(GROUP):
             for k in range(list_len):
-                spot = place_ref[(base + i) * list_len + k] + shift
-                window_ref[k, pl.ds(base + i, 1), :] = field_ref[pl.ds(spot, 1), :]
+                spot = place_ref[(base + i) * list_len + k]
+                for shift, window_ref in windows:
+                    window_ref[k, pl.ds(base + i, 1), :] = field_ref[pl.ds(spot + shift, 1), :]
 
 
 def fetch_rows(window_ref, rows, slot, list_len, width):
@@ -106,22 +108,30 @@
     return low, jnp.where(slot < list_len * width, top, 2 * list_len)
 
 
+def rule_energy(line, squared, hot):
+    positive = jnp.maximum(line, 0.0)
+    rule = jnp.where(squared, positive * positive, positive)
+    tile = jnp.sum(rule, axis=1, keepdims=True)
+    return jnp.where(hot, jnp.broadcast_to(tile, hot.shape), 0.0)
+
+
 def sweep_kernel(*refs, list_len, beside):
     first = beside > 0
     if first:
         (place_ref, field_ref, slot_ref, coef_ref, off_ref, dual_ref, temp_ref, weight_ref,
-         moved_ref, keep_ref, send_ref, sum_ref, window_ref) = refs
+         moved_ref, energy_ref, keep_ref, send_ref, sum_ref, window_ref, other_ref) = refs
+        windows = [(0, window_ref), (beside, other_ref)]
     else:
         (place_ref, field_ref, slot_ref, coef_ref, off_ref, dual_ref, temp_ref, weight_ref,
          old_ref, moved_ref, next_ref, keep_ref, send_ref, sum_ref, window_ref) = refs
+        windows = [(0, window_ref)]
     arity, tiles, width = slot_ref.shape
     templates = weight_ref.shape[1]
-    load_windows(place_ref, field_ref, window_ref, tiles, list_len)
+    load_windows(place_ref, field_ref, windows, tiles, list_len)
     sum_ref[...] = jnp.zeros_like(sum_ref)
     one = jnp.ones((GROUP, width), jnp.float32)
 
-    @pl.loop(0, tiles // GROUP, unroll=UNROLL)
-    def _(group):
+    def step(group, energy):
         base = pl.multiple_of(group * GROUP, GROUP)
         rows = pl.ds(base, GROUP)
         templ = temp_ref[rows, :]
@@ -136,6 +146,10 @@
         slots = [slot_ref[s, rows, :] for s in range(arity)]
         used = [q < list_len * width for q in slots]
         acts = [jnp.where(used[s], coef_ref[s, rows, :], 0.0) for s in range(arity)]
+        if first:
+            goals = [fetch_rows(other_ref, rows, q, list_len, width) for q in slots]
+            line = sum(a * c for a, c in zip(acts, goals)) + off_ref[rows, :]
+            energy = energy + rule_energy(line, squared, hot)
         copies = [fetch_rows(window_ref, rows, q, list_len, width) for q in slots]
         duals = [dual_ref[s, rows, :] for s in range(arity)]
         if not first:
@@ -170,25 +184,29 @@
                 list_len,
                 width,
             )
-
+        return energy
+
+    energy = jnp.zeros((GROUP, templates), jnp.float32)
+    energy = lax.fori_loop(0, tiles // GROUP, step, energy, unroll=UNROLL)
+    if first:
+        energy_ref[...] = jnp.sum(energy, axis=0, keepdims=True)
     half = keep_ref.shape[0]
     keep_ref[...] = sum_ref[:half]
     send_ref[...] = sum_ref[half:]
 
 
-def energy_kernel(*refs, list_len, beside):
-    (place_ref, first_ref, own_ref, field_ref, start_ref, slot_ref, coef_ref, off_ref, dual_ref,
-     temp_ref, weight_ref, old_ref, energy_ref, next_ref, owned_ref, window_ref, other_ref) = refs
+def energy_kernel(*refs, list_len):
+    (place_ref, own_ref, field_ref, slot_ref, coef_ref, off_ref, dual_ref, temp_ref, goal_ref,
+     old_ref, energy_ref, next_ref, owned_ref, window_ref) = refs
     arity, tiles, width = slot_ref.shape
-    templates = weight_ref.shape[1]
-    piece = owned_ref.shape[0] // 2
-    for h in range(2):
+    templates = goal_ref.shape[1]
+    piece = owned_ref.shape[0] // own_ref.shape[0]
+    for h in range(own_ref.shape[0]):
         start = pl.multiple_of(own_ref[h], GROUP)
         owned_ref[h * piece : (h + 1) * piece] = field_ref[pl.ds(start, piece), :]
-    load_windows(place_ref, field_ref, window_ref, tiles, list_len)
-    load_windows(first_ref, start_ref, other_ref, tiles, list_len, beside)
-
-    def step(group, totals):
+    load_windows(place_ref, field_ref, [(0, window_ref)], tiles, list_len)
+
+    def step(group, energy):
         base = pl.multiple_of(group * GROUP, GROUP)
         rows = pl.ds(base, GROUP)
         templ = temp_ref[rows, :]
@@ -196,32 +214,21 @@
             jnp.int32, (GROUP, templates), 1
         )
         squared = jnp.broadcast_to(templ % 2 == 1, (GROUP, width))
-        lines = [off_ref[rows, :]] * 2
+        line = off_ref[rows, :]
         for s in range(arity):
             slot = slot_ref[s, rows, :]
             used = slot < list_len * width
-            act = jnp.where(used, coef_ref[s, rows, :], 0.0)
-            copies = [
-                fetch_rows(ref, rows, slot, list_len, width) for ref in (window_ref, other_ref)
-            ]
-            lines = [line + act * copy for line, copy in zip(lines, copies)]
+            copy = fetch_rows(window_ref, rows, slot, list_len, width)
+            line = line + jnp.where(used, coef_ref[s, rows, :], 0.0) * copy
             next_ref[s, rows, :] = dual_ref[s, rows, :] + jnp.where(
-                used, old_ref[s, rows, :] - copies[0], 0.0
+                used, old_ref[s, rows, :] - copy, 0.0
             )
-        results = []
-        for total, line in zip(totals, lines):
-            positive = jnp.maximum(line, 0.0)
-            rule = jnp.where(squared, positive * positive, positive)
-            tile = jnp.sum(rule, axis=1, keepdims=True)
-            results.append(
-                total + jnp.where(hot, jnp.broadcast_to(tile, (GROUP, templates)), 0.0)
-            )
-        return tuple(results)
-
-    zero = jnp.zeros((GROUP, templates), jnp.float32)
-    totals = lax.fori_loop(0, tiles // GROUP, step, (zero, zero), unroll=UNROLL)
+        return energy + rule_energy(line, squared, hot)
+
+    energy = jnp.zeros((GROUP, templates), jnp.float32)
+    energy = lax.fori_loop(0, tiles // GROUP, step, energy, unroll=UNROLL)
     energy_ref[...] = jnp.concatenate(
-        [jnp.sum(total, axis=0, keepdims=True) for total in totals], axis=1
+        [jnp.sum(energy, axis=0, keepdims=True), goal_ref[...]], axis=1
     )
 
 
@@ -267,18 +274,20 @@
     arity = slot_index.shape[0]
     devices = count * groups
     piece = atom_blk // groups
-    half = count * piece
+    part = piece // 2
+    half = devices * part
     start = device * tiles
     owner = lax.dynamic_slice_in_dim(block_owner, start, tiles, 0)
     spot = lax.dynamic_slice_in_dim(block_local, start, tiles, 0)
 
     def place_of(owner, spot, stride):
-        part = spot // piece
-        return (part ^ core) * (count * stride) + owner * stride + spot % piece
-
-    place_first = place_of(owner, spot, 2 * piece).reshape(-1)
-    place = place_of(owner, spot, piece).reshape(-1)
-    own = place_of(device, jnp.arange(2, dtype=jnp.int32) * piece, piece)
+        holder = owner * groups + spot // piece
+        handler = (spot // part) % 2
+        return (handler ^ core) * (devices * stride) + holder * stride + spot % part
+
+    place_first = place_of(owner, spot, piece).reshape(-1)
+    place = place_of(owner, spot, part).reshape(-1)
+    own = place_of(device, jnp.arange(2 * groups, dtype=jnp.int32) * part, part)
     slots = slot_index.reshape(arity, tiles, width)
     coeffs = coefficient.reshape(arity, tiles, width)
     offsets = offset.reshape(tiles, width)
@@ -291,30 +300,36 @@
     def share(field):
         return lax.dynamic_slice_in_dim(field, core * piece, piece, 0)
 
-    mine, fixed = share(atom_value), share(observed)
+    def spread(field):
+        return jnp.broadcast_to(
+            field.reshape(1, 2, part, width), (count, 2, part, width)
+        ).reshape(devices, part, width)
+
     start_fields, *early = tell(
-        jnp.concatenate([mine, share(target_value)], axis=0),
-        count,
-        (place_first, place, own, fixed, templates, slots, coeffs, offsets, duals),
-    )
-    place_first, place, own, fixed, templates, slots, coeffs, offsets, duals = early
-    moved, keep, send = call(
-        lambda *r: sweep_kernel(*r, list_len=list_len, beside=piece),
+        jnp.concatenate([spread(share(atom_value)), spread(share(target_value))], axis=1),
+        (place_first, place, own, share(atom_value), share(observed), templates, slots, coeffs,
+         offsets, duals, weights),
+    )
+    (place_first, place, own, mine, fixed, templates, slots, coeffs, offsets, duals,
+     weights) = early
+    moved, e_target, keep, send = call(
+        lambda *r: sweep_kernel(*r, list_len=list_len, beside=part),
         (place_first, start_fields, slots, coeffs, offsets, duals, templates, weights),
         1,
-        (rule, (2 * half, width), (2 * half, width)),
-        ((4 * half, width), window),
+        (rule, (1, TEMPL), (2 * half, width), (2 * half, width)),
+        ((4 * half, width), window, window),
         15_000_000,
     )
     sums = collect(keep, send, count)
-    counted = sums[piece:] + 1.0
+    sums = sums.reshape(2, 2, part, width)
+    counted = sums[:, 1].reshape(piece, width) + 1.0
 
     def refresh(sums, before):
         stepped = jnp.clip((sums + before) / counted, 0.0, 1.0)
         return jnp.where(fixed == 1, before, stepped)
 
-    mine = refresh(sums[:piece], mine)
-    values = tell(mine, count)
+    mine = refresh(sums[:, 0].reshape(piece, width), mine)
+    values = tell(spread(mine))
     moved, duals, keep, send = call(
         lambda *r: sweep_kernel(*r, list_len=list_len, beside=0),
         (place, values, slots, coeffs, offsets, duals, templates, weights, moved),
@@ -323,17 +338,16 @@
         ((2 * half, width), window),
         15_000_000,
     )
-    values = tell(refresh(collect(keep, send, count), mine), count)
+    values = tell(spread(refresh(collect(keep, send, count), mine)))
     energies, dual_next, consensus = call(
-        lambda *r: energy_kernel(*r, list_len=list_len, beside=piece),
-        (place, place_first, own, values, start_fields, slots, coeffs, offsets, duals, templates,
-         weights, moved),
-        3,
+        lambda *r: energy_kernel(*r, list_len=list_len),
+        (place, own, values, slots, coeffs, offsets, duals, templates, e_target, moved),
+        2,
         ((1, 2 * TEMPL), rule, (atom_blk, width)),
-        (window, window),
+        (window,),
         10_000_000,
     )
-    energies = deal(jnp.broadcast_to(energies[None], (devices, 1, 2 * TEMPL)), ("blk", "grp"))
+    energies = deal(jnp.broadcast_to(energies[None], (devices, 1, 2 * TEMPL)))
     energies = jnp.sum(energies, axis=(0, 1))
     e_value, e_target = energies[:TEMPL], energies[TEMPL:]
     weight_next = weight * jnp.exp(-LEARN_RATE * (e_value - e_target) / (e_value + e_target + 1.0))

time: 90.9 us -> 87.2 us (0.959)
  blocking collectives: 54.8 us -> 52.1 us
    all_to_all x5, blocking collectives: 54.8 us -> 52.1 us  [deal(): return lax.all_to_all(parts, ('blk', 'grp'), 0, 0, tiled=True)]
    all_to_all x1, starting transfers between devices: 8.34 us -> 7.33 us  [deal(): return lax.all_to_all(parts, ('blk', 'grp'), 0, 0, tiled=True)]
  transfers between devices with their start and end apart: 6 -> 6, of which waited for: 6 -> 6; matrix products, arithmetic and copies ran while one was open for 1% -> 2% of each run, Pallas kernels for 0% -> 0%
where the time goes in v4:
time: 87.2 us; the launch traced here: 86.6 us
  blocking collectives  52.1 us (60%)
  waiting for transfers between devices  14.2 us (16%)
  starting transfers between devices  8.25 us (9%)
  Pallas kernels  6.26 us (7%)
  local copies, waits for them, and re-layouts  2.63 us (3%)
  other arithmetic  2.36 us (3%)
    all_to_all x5, blocking collectives, deal(): return lax.all_to_all(parts, ('blk', 'grp'), 0, 0, tiled=True)  52.1 us
    all_to_all x1, waiting for transfers between devices, deal(): return lax.all_to_all(parts, ('blk', 'grp'), 0, 0, tiled=True)  7.98 us
    all_to_all x1, starting transfers between devices, deal(): return lax.all_to_all(parts, ('blk', 'grp'), 0, 0, tiled=True)  7.33 us
    pallas_call x3, Pallas kernels, call(): pl.pallas_call(body, out_shape=shapes, in_specs=specs(len(args), scalars)...  6.26 us
    ppermute x5, waiting for transfers between devices, swap_cores(): return lax.ppermute(value, 'grp', [(0, 1), (1, 0)])  6.18 us
  transfers between devices with their start and end apart: 6, of which 6 were waited for; matrix products, arithmetic and copies ran while one was open for 2% of the time, Pallas kernels for 0%

profile of v4, /device:TPU:0, one launch (start us, length us, event | category | flops | bytes accessed | tf_op | source)
XLA Modules:
  0.0 86.6 jit_solution(722226879020311839)
XLA Ops:
  0.6 0.0 copy-start
  0.7 0.7 dynamic-slice_bitcast_fusion
  1.4 0.7 pad_maximum_fusion.1
  2.1 7.3 %all-to-all-start = ((f32[32,16,128]{2,1,0:T(8,128)}), f32[32,16,128]{2,1,0:T(8,128)S(1)}, u32[]{:S(2)}, u32[]{:S(2)}) async-start(f32[32,16,128]{2,1,0:T(8,128)} %pad_maximum_fusion.1), calls=%async_computation | async-start | bytes 524288 | tf_op jit(solution)/shard_map/all_to_all | solution.py:23
  9.5 0.8 add_add_fusion
  10.2 0.1 copy.31
  10.3 0.1 reshape.92.r_0_
  10.5 0.1 copy.30
  10.6 0.1 reshape.91.r_0_
  10.7 0.7 copy-done.6
  11.4 0.7 copy-done.7
  12.0 8.0 %all-to-all-done = f32[32,16,128]{2,1,0:T(8,128)S(1)} async-done(((f32[32,16,128]{2,1,0:T(8,128)}), f32[32,16,128]{2,1,0:T(8,128)S(1)}, u32[]{:S(2)}, u32[]{:S(2)}) %all-to-all-start) | async-done | bytes 262176 | tf_op jit(solution)/shard_map/all_to_all | solution.py:23
  20.0 0.1 copy.32.r_6_.r_7_
  20.2 0.0 copy-start.5
  20.2 1.4 %collective-permute-done = f32[512,128]{1,0:T(8,128)S(1)} collective-permute-done((f32[512,128]{1,0:T(8,128)S(1)}, f32[512,128]{1,0:T(8,128)S(1)}, u32[]{:S(2)}, u32[]{:S(2)}) %collective-permute-start) | collective-permute-done | bytes 262176 | tf_op jit(solution)/shard_map/ppermute | solution.py:19
  21.6 2.4 %shard_map.130 = (f32[3,64,128]{2,1,0:T(8,128)S(1)}, f32[1,40]{1,0:T(1,128)S(1)}, f32[512,128]{1,0:T(8,128)S(1)}, f32[512,128]{1,0:T(8,128)S(1)}) custom-call(s32[256]{0:T(256)S(1)} %reshape.91.r_0_, f32[1024,128]{1,0:T(8,128)S(1)} %pad_maximum_fusion.r_1_, s32[3,64,128]{2,1,0:T(8,128)S(1)} %bitcast.59, f32[3,64,128]{2,1,0:T(8,128)S(1)} %bitcast.62, ...), custom_call_target="tpu_custom_call" | custom-call | bytes 15000000 | tf_op jit(solution)/shard_map/pallas_call | solution.py:243
  24.0 0.2 collective-permute-start.1
  24.2 1.4 %collective-permute-done.1 = f32[512,128]{1,0:T(8,128)S(1)} collective-permute-done((f32[512,128]{1,0:T(8,128)S(1)}, f32[512,128]{1,0:T(8,128)S(1)}, u32[]{:S(2)}, u32[]{:S(2)}) %collective-permute-start.1) | collective-permute-done | bytes 262176 | tf_op jit(solution)/shard_map/ppermute | solution.py:19
  25.7 12.8 %all_to_all.30 = f32[32,16,128]{2,1,0:T(8,128)S(1)} all-to-all(f32[32,16,128]{2,1,0:T(8,128)S(1)} %bitcast.73), channel_id=1, replica_groups=mesh['blk'=16,'grp'=2] {'blk','grp'}, dimensions={0} | all-to-all | bytes 524288 | tf_op jit(solution)/shard_map/all_to_all | solution.py:23
  38.5 10.4 %all_to_all.31 = f32[32,8,128]{2,1,0:T(8,128)S(1)} all-to-all(f32[32,8,128]{2,1,0:T(8,128)S(1)} %bitcast.77), channel_id=1, replica_groups=mesh['blk'=16,'grp'=2] {'blk','grp'}, dimensions={0} | all-to-all | bytes 262144 | tf_op jit(solution)/shard_map/all_to_all | solution.py:23
  48.9 0.2 collective-permute-start.2
  49.1 1.1 %collective-permute-done.2 = f32[256,128]{1,0:T(8,128)S(1)} collective-permute-done((f32[256,128]{1,0:T(8,128)S(1)}, f32[256,128]{1,0:T(8,128)S(1)}, u32[]{:S(2)}, u32[]{:S(2)}) %collective-permute-start.2) | collective-permute-done | bytes 131104 | tf_op jit(solution)/shard_map/ppermute | solution.py:19
  50.3 2.1 %shard_map.131 = (f32[3,64,128]{2,1,0:T(8,128)S(1)}, f32[3,64,128]{2,1,0:T(8,128)S(1)}, f32[256,128]{1,0:T(8,128)S(1)}, f32[256,128]{1,0:T(8,128)S(1)}) custom-call(s32[256]{0:T(256)S(1)} %reshape.92.r_0_, f32[512,128]{1,0:T(8,128)S(1)} %pad_maximum_fusion.2.r_1_, s32[3,64,128]{2,1,0:T(8,128)S(1)} %bitcast.60, f32[3,64,128]{2,1,0:T(8,128)S(1)} %bitcast.63, ...), custom_call_target="tpu_custom_call" | custom-call | bytes 15000000 | tf_op jit(solution)/shard_map/pallas_call | solution.py:243
  52.4 0.3 collective-permute-start.3
  52.7 1.1 %collective-permute-done.3 = f32[256,128]{1,0:T(8,128)S(1)} collective-permute-done((f32[256,128]{1,0:T(8,128)S(1)}, f32[256,128]{1,0:T(8,128)S(1)}, u32[]{:S(2)}, u32[]{:S(2)}) %collective-permute-start.3) | collective-permute-done | bytes 131104 | tf_op jit(solution)/shard_map/ppermute | solution.py:19
  53.8 10.0 %all_to_all.32 = f32[32,8,128]{2,1,0:T(8,128)S(1)} all-to-all(f32[32,8,128]{2,1,0:T(8,128)S(1)} %add_bitcast_fusion), channel_id=1, replica_groups=mesh['blk'=16,'grp'=2] {'blk','grp'}, dimensions={0} | all-to-all | bytes 262144 | tf_op jit(solution)/shard_map/all_to_all | solution.py:23
  63.9 10.0 %all_to_all.33 = f32[32,8,128]{2,1,0:T(8,128)S(1)} all-to-all(f32[32,8,128]{2,1,0:T(8,128)S(1)} %bitcast.79), channel_id=1, replica_groups=mesh['blk'=16,'grp'=2] {'blk','grp'}, dimensions={0} | all-to-all | bytes 262144 | tf_op jit(solution)/shard_map/all_to_all | solution.py:23
  73.8 0.2 collective-permute-start.4
  74.0 1.1 %collective-permute-done.4 = f32[256,128]{1,0:T(8,128)S(1)} collective-permute-done((f32[256,128]{1,0:T(8,128)S(1)}, f32[256,128]{1,0:T(8,128)S(1)}, u32[]{:S(2)}, u32[]{:S(2)}) %collective-permute-start.4) | collective-permute-done | bytes 131104 | tf_op jit(solution)/shard_map/ppermute | solution.py:19
  75.2 1.8 %shard_map.132 = (f32[1,80]{1,0:T(1,128)S(1)}, f32[3,64,128]{2,1,0:T(8,128)}, f32[32,128]{1,0:T(8,128)}) custom-call(s32[256]{0:T(256)S(1)} %reshape.92.r_0_, s32[4]{0:T(128)S(1)} %fusion.9.r_1_, f32[512,128]{1,0:T(8,128)S(1)} %pad_maximum_fusion.3.r_2_, s32[3,64,128]{2,1,0:T(8,128)S(1)} %bitcast.61, f32[3,64,128]{2,1,0:T(8,128)S(1)} %bitcast.64, ...), custom_call_target="tpu_custom_call" | custom-call | bytes 10000000 | tf_op jit(solution)/shard_map/pallas_call | solution.py:243
  77.0 8.9 %all_to_all.34 = f32[32,1,80]{2,1,0:T(1,128)S(1)} all-to-all(f32[32,1,80]{2,1,0:T(1,128)S(1)} %broadcast_in_dim.50), channel_id=1, replica_groups=mesh['blk'=16,'grp'=2] {'blk','grp'}, dimensions={0} | all-to-all | bytes 20480 | tf_op jit(solution)/shard_map/all_to_all | solution.py:23
  86.0 0.6 exponential_multiply_fusion
  (33 shorter events, 0.3 us)
Async XLA Ops:
  0.6 0.7 copy-start
  2.1 17.9 %all-to-all-start = ((f32[32,16,128]{2,1,0:T(8,128)}), f32[32,16,128]{2,1,0:T(8,128)S(1)}, u32[]{:S(2)}, u32[]{:S(2)}) async-start(f32[32,16,128]{2,1,0:T(8,128)} %pad_maximum_fusion.1), calls=%async_computation | async-start | bytes 524288 | tf_op jit(solution)/shard_map/all_to_all | solution.py:23
  10.7 0.7 copy-start.6
  11.4 0.7 copy-start.7
  20.0 1.5 %collective-permute-start = (f32[512,128]{1,0:T(8,128)S(1)}, f32[512,128]{1,0:T(8,128)S(1)}, u32[]{:S(2)}, u32[]{:S(2)}) collective-permute-start(f32[512,128]{1,0:T(8,128)S(1)} %bitcast.75), channel_id=1, source_target_pairs={{0,1},{1,0},{2,3},{3,2},{4,5},{5,4},{6,7},{7,6},{8,9},{9,8},{10,11... | collective-permute-start | bytes 786440 | tf_op jit(solution)/shard_map/ppermute | solution.py:19
  20.1 1.5 %copy-start.1 = (s32[3,1,8192]{2,1,0:T(1,128)S(1)}, s32[3,1,8192]{2,1,0:T(1,128)}, u32[]{:S(2)}) copy-start(s32[3,1,8192]{2,1,0:T(1,128)} %param.16) | copy-start | bytes 294916
  20.1 1.5 %copy-start.2 = (f32[3,1,8192]{2,1,0:T(1,128)S(1)}, f32[3,1,8192]{2,1,0:T(1,128)}, u32[]{:S(2)}) copy-start(f32[3,1,8192]{2,1,0:T(1,128)} %param.17) | copy-start | bytes 294916
  20.1 1.5 %copy-start.3 = (f32[3,1,8192]{2,1,0:T(1,128)S(1)}, f32[3,1,8192]{2,1,0:T(1,128)}, u32[]{:S(2)}) copy-start(f32[3,1,8192]{2,1,0:T(1,128)} %param.19) | copy-start | bytes 294916
  20.1 1.5 %copy-start.4 = (f32[1,8192]{1,0:T(1,128)S(1)}, f32[1,8192]{1,0:T(1,128)}, u32[]{:S(2)}) copy-start(f32[1,8192]{1,0:T(1,128)} %param.18) | copy-start | bytes 98308
  20.2 1.5 %copy-start.5 = (f32[40]{0:T(128)S(1)}, f32[40]{0:T(128)}, u32[]{:S(2)}) copy-start(f32[40]{0:T(128)} %param.21) | copy-start | bytes 484
  24.0 1.6 %collective-permute-start.1 = (f32[512,128]{1,0:T(8,128)S(1)}, f32[512,128]{1,0:T(8,128)S(1)}, u32[]{:S(2)}, u32[]{:S(2)}) collective-permute-start(f32[512,128]{1,0:T(8,128)S(1)} %get-tuple-element.39), channel_id=1, source_target_pairs={{0,1},{1,0},{2,3},{3,2},{4,5},{5,4},{6,7},{7,6},{8,9},{9,8},{10,11... | collective-permute-start | bytes 786440 | tf_op jit(solution)/shard_map/ppermute | solution.py:19
  48.9 1.3 %collective-permute-start.2 = (f32[256,128]{1,0:T(8,128)S(1)}, f32[256,128]{1,0:T(8,128)S(1)}, u32[]{:S(2)}, u32[]{:S(2)}) collective-permute-start(f32[256,128]{1,0:T(8,128)S(1)} %bitcast.80), channel_id=1, source_target_pairs={{0,1},{1,0},{2,3},{3,2},{4,5},{5,4},{6,7},{7,6},{8,9},{9,8},{10,11... | collective-permute-start | bytes 393224 | tf_op jit(solution)/shard_map/ppermute | solution.py:19
  52.4 1.4 %collective-permute-start.3 = (f32[256,128]{1,0:T(8,128)S(1)}, f32[256,128]{1,0:T(8,128)S(1)}, u32[]{:S(2)}, u32[]{:S(2)}) collective-permute-start(f32[256,128]{1,0:T(8,128)S(1)} %get-tuple-element.42), channel_id=1, source_target_pairs={{0,1},{1,0},{2,3},{3,2},{4,5},{5,4},{6,7},{7,6},{8,9},{9,8},{10,11... | collective-permute-start | bytes 393224 | tf_op jit(solution)/shard_map/ppermute | solution.py:19
  73.8 1.3 %collective-permute-start.4 = (f32[256,128]{1,0:T(8,128)S(1)}, f32[256,128]{1,0:T(8,128)S(1)}, u32[]{:S(2)}, u32[]{:S(2)}) collective-permute-start(f32[256,128]{1,0:T(8,128)S(1)} %bitcast.82), channel_id=1, source_target_pairs={{0,1},{1,0},{2,3},{3,2},{4,5},{5,4},{6,7},{7,6},{8,9},{9,8},{10,11... | collective-permute-start | bytes 393224 | tf_op jit(solution)/shard_map/ppermute | solution.py:19

commit v5 on v4

--- a/solution.py
+++ b/solution.py
@@ -31,10 +31,8 @@
     return (gathered,) + meanwhile if meanwhile else gathered
 
 
-def collect(keep, send, count):
-    parts = keep + swap_cores(send)
-    width = parts.shape[1]
-    return jnp.sum(deal(parts.reshape(2 * count, -1, width)).reshape(count, -1, width), axis=0)
+def collect(parts, count):
+    return jnp.sum(deal(parts).reshape(count, -1, parts.shape[-1]), axis=0)
 
 
 def row_of(row, height, width):
@@ -69,36 +67,60 @@
     return first, second, rest - second
 
 
-def scatter_tile(place_ref, sum_ref, beside, tile, lows, tops, values, list_len, width):
+def one_hot(low, narrow, width):
+    packed = jnp.broadcast_to(low.astype(jnp.float32), (16, width)).astype(jnp.bfloat16)
+    spot = lax.broadcasted_iota(jnp.int32, (narrow, width), 0)
+    spot = spot.astype(jnp.float32).astype(jnp.bfloat16)
+    same = jnp.concatenate([packed] * (narrow // 16), axis=0) == spot
+    return jnp.where(same, jnp.bfloat16(1), jnp.bfloat16(0))
+
+
+def product(left, hot):
+    return lax.dot_general(
+        left, hot, (((1,), (1,)), ((), ())), preferred_element_type=jnp.float32
+    )
+
+
+def scatter_pair(place_ref, sum_ref, tile, lows, tops, values, list_len, width):
     narrow = width // 2
     height = 2 * list_len
+    pieces = len(values[0][0])
+    bands = pieces + pieces % 2
     row = lax.broadcasted_iota(jnp.int32, (height, width), 0)
-    spot = lax.broadcasted_iota(jnp.int32, (narrow, width), 0)
-    hot, left = [], []
-    for low, top, parts in zip(lows, tops, values):
-        hot.append((row_of(low, narrow, width) == spot).astype(jnp.float32).astype(jnp.bfloat16))
-        here = row_of(top, height, width) == row
-        left.append(
-            jnp.concatenate(
-                [jnp.where(here, row_of(part, height, width), 0.0) for part in parts], axis=0
-            ).astype(jnp.bfloat16)
+    blank = jnp.zeros((height, width), jnp.float32)
+    empty = jnp.zeros((bands * height, width), jnp.bfloat16)
+    hots, lefts = [], []
+    for own_lows, own_tops, own_values in zip(lows, tops, values):
+        hots.append([one_hot(low, narrow, width) for low in own_lows])
+        left = []
+        for top, parts in zip(own_tops, own_values):
+            here = row_of(top, height, width) == row
+            rows = [jnp.where(here, row_of(part, height, width), 0.0) for part in parts]
+            rows = rows + [blank] * (bands - len(rows))
+            left.append(jnp.concatenate(rows, axis=0).astype(jnp.bfloat16))
+        lefts.append(left)
+    shared = product(
+        jnp.concatenate(
+            [
+                jnp.concatenate([lefts[0][-1], empty], axis=1),
+                jnp.concatenate([empty, lefts[1][-1]], axis=1),
+            ],
+            axis=0,
+        ),
+        jnp.concatenate([hots[0][-1], hots[1][-1]], axis=1),
+    )
+    for j in range(2):
+        summed = shared[j * bands * height : (j + 1) * bands * height]
+        summed = summed + product(
+            jnp.concatenate(lefts[j][:-1], axis=1), jnp.concatenate(hots[j][:-1], axis=1)
         )
-    summed = lax.dot_general(
-        jnp.concatenate(left, axis=1),
-        jnp.concatenate(hot, axis=1),
-        (((1,), (1,)), ((), ())),
-        preferred_element_type=jnp.float32,
-    )
-    bands = [summed[j * height : (j + 1) * height] for j in range(len(values[0]))]
-    spots = [place_ref[tile * list_len + k] for k in range(list_len)]
-    totals = [(0, bands[0] + bands[1] + bands[2])]
-    if beside:
-        totals.append((beside, bands[3]))
-    for shift, total in totals:
+        parts = [summed[i * height : (i + 1) * height] for i in range(bands)]
+        spots = [place_ref[(tile + j) * list_len + k] for k in range(list_len)]
+        total = sum(parts[1:pieces], parts[0])
         total = jnp.concatenate([total[:list_len], total[list_len:]], axis=1)
-        olds = [sum_ref[pl.ds(at + shift, 1), :] for at in spots]
+        olds = [sum_ref[pl.ds(at, 1), :] for at in spots]
         for k, at in enumerate(spots):
-            sum_ref[pl.ds(at + shift, 1), :] = olds[k] + total[k : k + 1]
+            sum_ref[pl.ds(at, 1), :] = olds[k] + total[k : k + 1]
 
 
 def slot_parts(slot, list_len, width):
@@ -108,6 +130,34 @@
     return low, jnp.where(slot < list_len * width, top, 2 * list_len)
 
 
+def count_kernel(place_ref, slot_ref, keep_ref, send_ref, sum_ref, *, list_len):
+    arity, tiles, width = slot_ref.shape
+    sum_ref[...] = jnp.zeros_like(sum_ref)
+    one = (jnp.ones((1, width), jnp.float32),)
+
+    @pl.loop(0, tiles // GROUP, unroll=UNROLL)
+    def _(group):
+        base = pl.multiple_of(group * GROUP, GROUP)
+        rows = pl.ds(base, GROUP)
+        halves = [slot_parts(slot_ref[s, rows, :], list_len, width) for s in range(arity)]
+        for i in range(0, GROUP, 2):
+            pair = (slice(i, i + 1), slice(i + 1, i + 2))
+            scatter_pair(
+                place_ref,
+                sum_ref,
+                base + i,
+                [[h[0][at] for h in halves] for at in pair],
+                [[h[1][at] for h in halves] for at in pair],
+                [[one] * arity for at in pair],
+                list_len,
+                width,
+            )
+
+    half = keep_ref.shape[0]
+    keep_ref[...] = sum_ref[:half]
+    send_ref[...] = sum_ref[half:]
+
+
 def rule_energy(line, squared, hot):
     positive = jnp.maximum(line, 0.0)
     rule = jnp.where(squared, positive * positive, positive)
@@ -118,18 +168,17 @@
 def sweep_kernel(*refs, list_len, beside):
     first = beside > 0
     if first:
-        (place_ref, field_ref, slot_ref, coef_ref, off_ref, dual_ref, temp_ref, weight_ref,
-         moved_ref, energy_ref, keep_ref, send_ref, sum_ref, window_ref, other_ref) = refs
+        (place_ref, first_ref, field_ref, slot_ref, coef_ref, off_ref, dual_ref, temp_ref,
+         weight_ref, moved_ref, energy_ref, keep_ref, send_ref, sum_ref, window_ref, other_ref) = refs
         windows = [(0, window_ref), (beside, other_ref)]
     else:
         (place_ref, field_ref, slot_ref, coef_ref, off_ref, dual_ref, temp_ref, weight_ref,
          old_ref, moved_ref, next_ref, keep_ref, send_ref, sum_ref, window_ref) = refs
-        windows = [(0, window_ref)]
+        first_ref, windows = place_ref, [(0, window_ref)]
     arity, tiles, width = slot_ref.shape
     templates = weight_ref.shape[1]
-    load_windows(place_ref, field_ref, windows, tiles, list_len)
+    load_windows(first_ref, field_ref, windows, tiles, list_len)
     sum_ref[...] = jnp.zeros_like(sum_ref)
-    one = jnp.ones((GROUP, width), jnp.float32)
 
     def step(group, energy):
         base = pl.multiple_of(group * GROUP, GROUP)
@@ -169,18 +218,17 @@
         for s in range(arity):
             moved = shifted[s] - chosen * acts[s]
             moved_ref[s, rows, :] = moved
-            pieces = split_three(jnp.where(used[s], moved + duals[s], 0.0))
-            parts.append(pieces + (one,) if first else pieces)
+            parts.append(split_three(jnp.where(used[s], moved + duals[s], 0.0)))
         halves = [slot_parts(q, list_len, width) for q in slots]
-        for i in range(GROUP):
-            scatter_tile(
+        for i in range(0, GROUP, 2):
+            pair = (slice(i, i + 1), slice(i + 1, i + 2))
+            scatter_pair(
                 place_ref,
                 sum_ref,
-                beside,
                 base + i,
-                [h[0][i : i + 1] for h in halves],
-                [h[1][i : i + 1] for h in halves],
-                [tuple(p[i : i + 1] for p in part) for part in parts],
+                [[h[0][at] for h in halves] for at in pair],
+                [[h[1][at] for h in halves] for at in pair],
+                [[tuple(p[at] for p in part) for part in parts] for at in pair],
                 list_len,
                 width,
             )
@@ -305,22 +353,35 @@
             field.reshape(1, 2, part, width), (count, 2, part, width)
         ).reshape(devices, part, width)
 
+    def by_device(keep, send):
+        return (keep + swap_cores(send)).reshape(devices, part, width)
+
+    counts = by_device(
+        *call(
+            lambda *r: count_kernel(*r, list_len=list_len),
+            (place, slots),
+            1,
+            ((half, width), (half, width)),
+            ((2 * half, width),),
+            8_000_000,
+        )
+    )
     start_fields, *early = tell(
         jnp.concatenate([spread(share(atom_value)), spread(share(target_value))], axis=1),
         (place_first, place, own, share(atom_value), share(observed), templates, slots, coeffs,
-         offsets, duals, weights),
+         offsets, duals, weights, counts),
     )
     (place_first, place, own, mine, fixed, templates, slots, coeffs, offsets, duals,
-     weights) = early
+     weights, counts) = early
     moved, e_target, keep, send = call(
         lambda *r: sweep_kernel(*r, list_len=list_len, beside=part),
-        (place_first, start_fields, slots, coeffs, offsets, duals, templates, weights),
-        1,
-        (rule, (1, TEMPL), (2 * half, width), (2 * half, width)),
-        ((4 * half, width), window, window),
+        (place, place_first, start_fields, slots, coeffs, offsets, duals, templates, weights),
+        2,
+        (rule, (1, TEMPL), (half, width), (half, width)),
+        ((2 * half, width), window, window),
         15_000_000,
     )
-    sums = collect(keep, send, count)
+    sums = collect(jnp.concatenate([by_device(keep, send), counts], axis=1), count)
     sums = sums.reshape(2, 2, part, width)
     counted = sums[:, 1].reshape(piece, width) + 1.0
 
@@ -338,7 +399,7 @@
         ((2 * half, width), window),
         15_000_000,
     )
-    values = tell(spread(refresh(collect(keep, send, count), mine)))
+    values = tell(spread(refresh(collect(by_device(keep, send), count), mine)))
     energies, dual_next, consensus = call(
         lambda *r: energy_kernel(*r, list_len=list_len),
         (place, own, values, slots, coeffs, offsets, duals, templates, e_target, moved),

time: 87.2 us -> 86.6 us (level)
  waiting for transfers between devices: 14.2 us -> 12.4 us
  Pallas kernels: 6.26 us -> 7.48 us
    all_to_all x1, waiting for transfers between devices: 7.98 us -> 6.43 us  [deal(): return lax.all_to_all(parts, ('blk', 'grp'), 0, 0, tiled=True)]
    pallas_call x3 -> x4, Pallas kernels: 6.26 us -> 7.48 us  [call(): pl.pallas_call(body, out_shape=shapes, in_specs=specs(len(args), scalars)...]
    ppermute x5 -> x6, waiting for transfers between devices: 6.18 us -> 6.01 us  [swap_cores(): return lax.ppermute(value, 'grp', [(0, 1), (1, 0)])]
  transfers between devices with their start and end apart: 6 -> 7, of which waited for: 6 -> 6; matrix products, arithmetic and copies ran while one was open for 2% -> 2% of each run, Pallas kernels for 0% -> 2%
where the time goes in v5:
time: 86.6 us; the launch traced here: 86 us
  blocking collectives  52.1 us (60%)
  waiting for transfers between devices  12.4 us (14%)
  starting transfers between devices  8.53 us (10%)
  Pallas kernels  7.48 us (9%)
  other arithmetic  2.36 us (3%)
  local copies, waits for them, and re-layouts  2.24 us (3%)
    all_to_all x5, blocking collectives, deal(): return lax.all_to_all(parts, ('blk', 'grp'), 0, 0, tiled=True)  52.1 us
    pallas_call x4, Pallas kernels, call(): pl.pallas_call(body, out_shape=shapes, in_specs=specs(len(args), scalars)...  7.48 us
    all_to_all x1, starting transfers between devices, deal(): return lax.all_to_all(parts, ('blk', 'grp'), 0, 0, tiled=True)  7.33 us
    all_to_all x1, waiting for transfers between devices, deal(): return lax.all_to_all(parts, ('blk', 'grp'), 0, 0, tiled=True)  6.43 us
    ppermute x6, waiting for transfers between devices, swap_cores(): return lax.ppermute(value, 'grp', [(0, 1), (1, 0)])  6.01 us
  transfers between devices with their start and end apart: 7, of which 6 were waited for; matrix products, arithmetic and copies ran while one was open for 2% of the time, Pallas kernels for 2%

profile of v5, /device:TPU:0, one launch (start us, length us, event | category | flops | bytes accessed | tf_op | source)
XLA Modules:
  0.0 86.0 jit_solution(9155426810454036863)
XLA Ops:
  0.7 0.7 copy-done
  1.4 0.7 pad_maximum_fusion.1
  2.1 7.3 %all-to-all-start = ((f32[32,16,128]{2,1,0:T(8,128)}), f32[32,16,128]{2,1,0:T(8,128)S(1)}, u32[]{:S(2)}, u32[]{:S(2)}) async-start(f32[32,16,128]{2,1,0:T(8,128)} %pad_maximum_fusion.1), calls=%async_computation | async-start | bytes 524288 | tf_op jit(solution)/shard_map/all_to_all | solution.py:23
  9.5 0.8 add_add_fusion
  10.3 0.1 copy.31
  10.4 0.1 reshape.95.r_0_
  10.5 1.6 %shard_map.130 = (f32[256,128]{1,0:T(8,128)S(1)}, f32[256,128]{1,0:T(8,128)S(1)}) custom-call(s32[256]{0:T(256)S(1)} %reshape.95.r_0_, s32[3,64,128]{2,1,0:T(8,128)S(1)} %bitcast.62), custom_call_target="tpu_custom_call" | custom-call | bytes 8000000 | tf_op jit(solution)/shard_map/pallas_call | solution.py:291
  12.1 0.3 collective-permute-start
  12.4 0.3 copy-done.8
  12.8 0.1 copy.30
  12.9 0.1 reshape.94.r_1_
  13.0 0.6 copy-done.7
  13.6 6.4 %all-to-all-done = f32[32,16,128]{2,1,0:T(8,128)S(1)} async-done(((f32[32,16,128]{2,1,0:T(8,128)}), f32[32,16,128]{2,1,0:T(8,128)S(1)}, u32[]{:S(2)}, u32[]{:S(2)}) %all-to-all-start) | async-done | bytes 262176 | tf_op jit(solution)/shard_map/all_to_all | solution.py:23
  20.0 0.1 copy.32.r_7_.r_6_
  20.2 1.4 %collective-permute-done.1 = f32[512,128]{1,0:T(8,128)S(1)} collective-permute-done((f32[512,128]{1,0:T(8,128)S(1)}, f32[512,128]{1,0:T(8,128)S(1)}, u32[]{:S(2)}, u32[]{:S(2)}) %collective-permute-start.1) | collective-permute-done | bytes 262176 | tf_op jit(solution)/shard_map/ppermute | solution.py:19
  21.7 2.2 %shard_map.131 = (f32[3,64,128]{2,1,0:T(8,128)S(1)}, f32[1,40]{1,0:T(1,128)S(1)}, f32[256,128]{1,0:T(8,128)S(1)}, f32[256,128]{1,0:T(8,128)S(1)}) custom-call(s32[256]{0:T(256)S(1)} %reshape.95.r_0_, s32[256]{0:T(256)S(1)} %reshape.94.r_1_, f32[1024,128]{1,0:T(8,128)S(1)} %pad_maximum_fusion.r_2_, s32[3,64,128]{2,1,0:T(8,128)S(1)} %bitcast.63, ...), custom_call_target="tpu_custom_call" | custom-call | bytes 15000000 | tf_op jit(solution)/shard_map/pallas_call | solution.py:291
  23.8 0.2 collective-permute-start.2
  24.0 1.2 %collective-permute-done.2 = f32[256,128]{1,0:T(8,128)S(1)} collective-permute-done((f32[256,128]{1,0:T(8,128)S(1)}, f32[256,128]{1,0:T(8,128)S(1)}, u32[]{:S(2)}, u32[]{:S(2)}) %collective-permute-start.2) | collective-permute-done | bytes 131104 | tf_op jit(solution)/shard_map/ppermute | solution.py:19
  25.2 12.8 %all_to_all.30 = f32[32,16,128]{2,1,0:T(8,128)S(1)} all-to-all(f32[32,16,128]{2,1,0:T(8,128)S(1)} %pad_maximum_fusion.2), channel_id=1, replica_groups=mesh['blk'=16,'grp'=2] {'blk','grp'}, dimensions={0} | all-to-all | bytes 524288 | tf_op jit(solution)/shard_map/all_to_all | solution.py:23
  38.1 10.4 %all_to_all.31 = f32[32,8,128]{2,1,0:T(8,128)S(1)} all-to-all(f32[32,8,128]{2,1,0:T(8,128)S(1)} %bitcast.80), channel_id=1, replica_groups=mesh['blk'=16,'grp'=2] {'blk','grp'}, dimensions={0} | all-to-all | bytes 262144 | tf_op jit(solution)/shard_map/all_to_all | solution.py:23
  48.5 0.2 collective-permute-start.3
  48.7 1.1 %collective-permute-done.3 = f32[256,128]{1,0:T(8,128)S(1)} collective-permute-done((f32[256,128]{1,0:T(8,128)S(1)}, f32[256,128]{1,0:T(8,128)S(1)}, u32[]{:S(2)}, u32[]{:S(2)}) %collective-permute-start.3) | collective-permute-done | bytes 131104 | tf_op jit(solution)/shard_map/ppermute | solution.py:19
  49.8 1.9 %shard_map.132 = (f32[3,64,128]{2,1,0:T(8,128)S(1)}, f32[3,64,128]{2,1,0:T(8,128)S(1)}, f32[256,128]{1,0:T(8,128)S(1)}, f32[256,128]{1,0:T(8,128)S(1)}) custom-call(s32[256]{0:T(256)S(1)} %reshape.95.r_0_, f32[512,128]{1,0:T(8,128)S(1)} %pad_maximum_fusion.3.r_1_, s32[3,64,128]{2,1,0:T(8,128)S(1)} %bitcast.64, f32[3,64,128]{2,1,0:T(8,128)S(1)} %bitcast.67, ...), custom_call_target="tpu_custom_call" | custom-call | bytes 15000000 | tf_op jit(solution)/shard_map/pallas_call | solution.py:291
  51.8 0.3 collective-permute-start.4
  52.1 1.1 %collective-permute-done.4 = f32[256,128]{1,0:T(8,128)S(1)} collective-permute-done((f32[256,128]{1,0:T(8,128)S(1)}, f32[256,128]{1,0:T(8,128)S(1)}, u32[]{:S(2)}, u32[]{:S(2)}) %collective-permute-start.4) | collective-permute-done | bytes 131104 | tf_op jit(solution)/shard_map/ppermute | solution.py:19
  53.2 10.0 %all_to_all.32 = f32[32,8,128]{2,1,0:T(8,128)S(1)} all-to-all(f32[32,8,128]{2,1,0:T(8,128)S(1)} %add_bitcast_fusion), channel_id=1, replica_groups=mesh['blk'=16,'grp'=2] {'blk','grp'}, dimensions={0} | all-to-all | bytes 262144 | tf_op jit(solution)/shard_map/all_to_all | solution.py:23
  63.2 10.0 %all_to_all.33 = f32[32,8,128]{2,1,0:T(8,128)S(1)} all-to-all(f32[32,8,128]{2,1,0:T(8,128)S(1)} %bitcast.82), channel_id=1, replica_groups=mesh['blk'=16,'grp'=2] {'blk','grp'}, dimensions={0} | all-to-all | bytes 262144 | tf_op jit(solution)/shard_map/all_to_all | solution.py:23
  73.2 0.2 collective-permute-start.5
  73.4 1.1 %collective-permute-done.5 = f32[256,128]{1,0:T(8,128)S(1)} collective-permute-done((f32[256,128]{1,0:T(8,128)S(1)}, f32[256,128]{1,0:T(8,128)S(1)}, u32[]{:S(2)}, u32[]{:S(2)}) %collective-permute-start.5) | collective-permute-done | bytes 131104 | tf_op jit(solution)/shard_map/ppermute | solution.py:19
  74.6 1.8 %shard_map.133 = (f32[1,80]{1,0:T(1,128)S(1)}, f32[3,64,128]{2,1,0:T(8,128)}, f32[32,128]{1,0:T(8,128)}) custom-call(s32[256]{0:T(256)S(1)} %reshape.95.r_0_, s32[4]{0:T(128)S(1)} %fusion.9.r_1_, f32[512,128]{1,0:T(8,128)S(1)} %pad_maximum_fusion.4.r_2_, s32[3,64,128]{2,1,0:T(8,128)S(1)} %bitcast.65, f32[3,64,128]{2,1,0:T(8,128)S(1)} %bitcast.68, ...), custom_call_target="tpu_custom_call" | custom-call | bytes 10000000 | tf_op jit(solution)/shard_map/pallas_call | solution.py:291
  76.4 8.9 %all_to_all.34 = f32[32,1,80]{2,1,0:T(1,128)S(1)} all-to-all(f32[32,1,80]{2,1,0:T(1,128)S(1)} %broadcast_in_dim.50), channel_id=1, replica_groups=mesh['blk'=16,'grp'=2] {'blk','grp'}, dimensions={0} | all-to-all | bytes 20480 | tf_op jit(solution)/shard_map/all_to_all | solution.py:23
  85.4 0.6 exponential_multiply_fusion
  (40 shorter events, 0.4 us)
Async XLA Ops:
  0.6 0.7 copy-start
  0.6 0.7 copy-start.6
  2.1 8.3 %copy-start.1 = (s32[3,1,8192]{2,1,0:T(1,128)S(1)}, s32[3,1,8192]{2,1,0:T(1,128)}, u32[]{:S(2)}) copy-start(s32[3,1,8192]{2,1,0:T(1,128)} %param.16) | copy-start | bytes 294916
  2.1 17.9 %all-to-all-start = ((f32[32,16,128]{2,1,0:T(8,128)}), f32[32,16,128]{2,1,0:T(8,128)S(1)}, u32[]{:S(2)}, u32[]{:S(2)}) async-start(f32[32,16,128]{2,1,0:T(8,128)} %pad_maximum_fusion.1), calls=%async_computation | async-start | bytes 524288 | tf_op jit(solution)/shard_map/all_to_all | solution.py:23
  12.1 0.7 copy-start.8
  12.1 1.5 %collective-permute-start = (f32[256,128]{1,0:T(8,128)S(1)}, f32[256,128]{1,0:T(8,128)S(1)}, u32[]{:S(2)}, u32[]{:S(2)}) collective-permute-start(f32[256,128]{1,0:T(8,128)S(1)} %get-tuple-element.30), channel_id=1, source_target_pairs={{0,1},{1,0},{2,3},{3,2},{4,5},{5,4},{6,7},{7,6},{8,9},{9,8},{10,11... | collective-permute-start | bytes 393224 | tf_op jit(solution)/shard_map/ppermute | solution.py:19
  12.9 0.7 copy-start.7
  20.0 1.5 %collective-permute-start.1 = (f32[512,128]{1,0:T(8,128)S(1)}, f32[512,128]{1,0:T(8,128)S(1)}, u32[]{:S(2)}, u32[]{:S(2)}) collective-permute-start(f32[512,128]{1,0:T(8,128)S(1)} %bitcast.78), channel_id=1, source_target_pairs={{0,1},{1,0},{2,3},{3,2},{4,5},{5,4},{6,7},{7,6},{8,9},{9,8},{10,11... | collective-permute-start | bytes 786440 | tf_op jit(solution)/shard_map/ppermute | solution.py:19
  20.1 1.5 %copy-start.2 = (f32[3,1,8192]{2,1,0:T(1,128)S(1)}, f32[3,1,8192]{2,1,0:T(1,128)}, u32[]{:S(2)}) copy-start(f32[3,1,8192]{2,1,0:T(1,128)} %param.17) | copy-start | bytes 294916
  20.1 1.5 %copy-start.3 = (f32[3,1,8192]{2,1,0:T(1,128)S(1)}, f32[3,1,8192]{2,1,0:T(1,128)}, u32[]{:S(2)}) copy-start(f32[3,1,8192]{2,1,0:T(1,128)} %param.19) | copy-start | bytes 294916
  20.1 1.5 %copy-start.4 = (f32[1,8192]{1,0:T(1,128)S(1)}, f32[1,8192]{1,0:T(1,128)}, u32[]{:S(2)}) copy-start(f32[1,8192]{1,0:T(1,128)} %param.18) | copy-start | bytes 98308
  20.2 1.5 %copy-start.5 = (f32[40]{0:T(128)S(1)}, f32[40]{0:T(128)}, u32[]{:S(2)}) copy-start(f32[40]{0:T(128)} %param.21) | copy-start | bytes 484
  23.8 1.4 %collective-permute-start.2 = (f32[256,128]{1,0:T(8,128)S(1)}, f32[256,128]{1,0:T(8,128)S(1)}, u32[]{:S(2)}, u32[]{:S(2)}) collective-permute-start(f32[256,128]{1,0:T(8,128)S(1)} %get-tuple-element.44), channel_id=1, source_target_pairs={{0,1},{1,0},{2,3},{3,2},{4,5},{5,4},{6,7},{7,6},{8,9},{9,8},{10,11... | collective-permute-start | bytes 393224 | tf_op jit(solution)/shard_map/ppermute | solution.py:19
  48.5 1.3 %collective-permute-start.3 = (f32[256,128]{1,0:T(8,128)S(1)}, f32[256,128]{1,0:T(8,128)S(1)}, u32[]{:S(2)}, u32[]{:S(2)}) collective-permute-start(f32[256,128]{1,0:T(8,128)S(1)} %bitcast.83), channel_id=1, source_target_pairs={{0,1},{1,0},{2,3},{3,2},{4,5},{5,4},{6,7},{7,6},{8,9},{9,8},{10,11... | collective-permute-start | bytes 393224 | tf_op jit(solution)/shard_map/ppermute | solution.py:19
  51.8 1.4 %collective-permute-start.4 = (f32[256,128]{1,0:T(8,128)S(1)}, f32[256,128]{1,0:T(8,128)S(1)}, u32[]{:S(2)}, u32[]{:S(2)}) collective-permute-start(f32[256,128]{1,0:T(8,128)S(1)} %get-tuple-element.48), channel_id=1, source_target_pairs={{0,1},{1,0},{2,3},{3,2},{4,5},{5,4},{6,7},{7,6},{8,9},{9,8},{10,11... | collective-permute-start | bytes 393224 | tf_op jit(solution)/shard_map/ppermute | solution.py:19
  73.2 1.3 %collective-permute-start.5 = (f32[256,128]{1,0:T(8,128)S(1)}, f32[256,128]{1,0:T(8,128)S(1)}, u32[]{:S(2)}, u32[]{:S(2)}) collective-permute-start(f32[256,128]{1,0:T(8,128)S(1)} %bitcast.85), channel_id=1, source_target_pairs={{0,1},{1,0},{2,3},{3,2},{4,5},{5,4},{6,7},{7,6},{8,9},{9,8},{10,11... | collective-permute-start | bytes 393224 | tf_op jit(solution)/shard_map/ppermute | solution.py:19
